TPU v7x, 32 devices: a whole 2x2x4 slice. The times are simulated.
32 devices in a mesh: dp: 8 (over z, core), tp: 4 (over y, x).
Axes of the slice: x: 2, y: 2, z: 4, core: 2. Of those that a mesh axis runs over, the one named last changes fastest.
Arguments:
- x_in: bfloat16 [8192, 2048], P(('dp', 'tp')), may hold values from -6 to 6
- norm_gain: float32 [2048], replicated, may hold values from 0.5 to 1.5
- w_z: bfloat16 [2048, 4096], P(None, 'tp'), may hold values from -0.125 to 0.125
- w_x: bfloat16 [2048, 4096], P(None, 'tp'), may hold values from -0.125 to 0.125
- w_b: bfloat16 [2048, 128], P(None, 'tp'), may hold values from -0.125 to 0.125
- w_c: bfloat16 [2048, 128], P(None, 'tp'), may hold values from -0.125 to 0.125
- w_dt: bfloat16 [2048, 64], P(None, 'tp'), may hold values from -0.125 to 0.125
- conv_w: float32 [4352, 4], replicated, may hold values from -3 to 3
- conv_b: float32 [4352], replicated, may hold values from -3 to 3
- dt_bias: float32 [64], replicated, may hold values from -6 to -2
- a_log: float32 [64], replicated, may hold values from -2.5 to 0.5
- d_skip: float32 [64], replicated, may hold values from 0.5 to 1.5
- gate_gain: float32 [4096], replicated, may hold values from 0.5 to 1.5
- w_out: bfloat16 [4096, 2048], P('tp'), may hold values from -0.09375 to 0.09375
- doc_lens: int32 [8, 8], P('dp'), may hold values from 1 to 512, 1024 in all within a row
- d_out: bfloat16 [8192, 2048], P(('dp', 'tp')), may hold values from -6 to 6
Outputs:
- block_out: bfloat16 [8192, 2048], P(('dp', 'tp'))
- grad_x: float32 [8192, 2048], P(('dp', 'tp'))
- grad_norm_gain: float32 [2048], replicated
- grad_w_z: float32 [2048, 4096], P('dp', 'tp')
- grad_w_x: float32 [2048, 4096], P('dp', 'tp')
- grad_w_b: float32 [2048, 128], P('dp', 'tp')
- grad_w_c: float32 [2048, 128], P('dp', 'tp')
- grad_w_dt: float32 [2048, 64], P('dp', 'tp')
- grad_conv_w: float32 [4352, 4], replicated
- grad_conv_b: float32 [4352], replicated
- grad_dt_bias: float32 [64], replicated
- grad_a_log: float32 [64], replicated
- grad_d_skip: float32 [64], replicated
- grad_gate_gain: float32 [4096], replicated
- grad_w_out: float32 [4096, 2048], P('tp', 'dp')
Inputs may be any that keep to these rules, and one draw needn't show every extreme that they name: `doc_lens`: each row gives, in order, the lengths of the 8 documents packed into one sequence of 1024 tokens; a row sums to 1024 and its longest document has exactly 512 tokens.
All inputs are finite; a program needn't handle non-finite values.
Results may differ from a plain program's by a relative error of at most 0.012.
Values may be sent and summed in bfloat16 or wider, within the bound.
A program may use at most 256 MiB of HBM per device.

v0:
```python
import functools

import jax
import jax.numpy as jnp
from jax import lax
from jax.experimental import pallas as pl
from jax.experimental.pallas import tpu as pltpu
from jax.sharding import PartitionSpec as P

EPSILON = 1e-05
HIGHEST = lax.Precision.HIGHEST
F32 = jnp.float32
BF16 = jnp.bfloat16
CHUNK = 128
LANES = 128
CONTRACT_FIRST = (((0,), (0,)), ((), ()))
CONTRACT_LAST = (((1,), (1,)), ((), ()))


def dot(a, b, dims=(((1,), (0,)), ((), ()))):
    return lax.dot_general(a, b, dims, preferred_element_type=F32)


def two_parts(v):
    high = v.astype(BF16)
    return jnp.concatenate([high, (v - high.astype(F32)).astype(BF16)], axis=1)


def prepare_chunk(width, x, bc, raw_dt, pos, prm_ref, head_ref, expand_ref, ext):
    rows = CHUNK
    ext[8:, :width] = x.astype(F32)
    ext[8:, width:] = bc.astype(F32)
    pre = prm_ref[3:4, :] * ext[8:, :] + prm_ref[4:5, :]
    for back in (1, 2, 3):
        here = (pos >= back).astype(F32)
        pre = pre + prm_ref[3 - back : 4 - back, :] * (ext[8 - back : 8 - back + rows, :] * here)
    sig = jax.nn.sigmoid(pre)
    act = pre * sig
    xc = act[:, :width]
    state_size = (act.shape[1] - width) // 2
    b_rows = act[:, width : width + state_size].astype(BF16)
    c_rows = act[:, width + state_size :].astype(BF16)
    raw = raw_dt.astype(F32) + head_ref[0:1, :]
    dt = jnp.maximum(raw, 0.0) + jnp.log1p(jnp.exp(-jnp.abs(raw)))
    log_decay = -dt * head_ref[1:2, :]
    t_idx = lax.broadcasted_iota(jnp.int32, (rows, rows), 0)
    s_idx = lax.broadcasted_iota(jnp.int32, (rows, rows), 1)
    lower = (s_idx <= t_idx).astype(F32)
    cum = lax.dot_general(
        lower, log_decay, (((1,), (0,)), ((), ())), precision=HIGHEST, preferred_element_type=F32
    )
    same = (s_idx <= t_idx) & (s_idx >= t_idx - pos)
    scores = jnp.where(same, dot(c_rows, b_rows, CONTRACT_LAST), 0.0)
    t_col = lax.broadcasted_iota(jnp.int32, (rows, 1), 0)
    pos_last = pos[rows - 1 : rows, :]
    cum_last = cum[rows - 1 : rows, :]
    inward = jnp.exp(cum) * (pos > t_col).astype(F32)
    tail = jnp.exp(cum_last - cum) * (t_col >= rows - 1 - pos_last).astype(F32)
    carried = jnp.exp(cum_last) * (pos_last >= rows).astype(F32)
    wide = dot(
        two_parts(jnp.concatenate([dt, inward, tail, jnp.broadcast_to(carried, (8, LANES))], axis=0)),
        expand_ref[...],
    )
    return dict(
        pre=pre,
        sig=sig,
        xc=xc,
        b=b_rows,
        c=c_rows,
        raw=raw,
        log_decay=log_decay,
        cum=cum,
        cum_t=cum.T,
        same=same,
        scores=scores,
        t_idx=t_idx,
        s_idx=s_idx,
        dt_w=wide[:rows],
        in_w=wide[rows : 2 * rows],
        tail_w=wide[2 * rows : 3 * rows],
        carried_w=wide[3 * rows : 3 * rows + 1],
    )


def decay_of(k, head):
    return jnp.exp(jnp.minimum(k["cum"][:, head : head + 1] - k["cum_t"][head : head + 1, :], 0.0))


def halves(pair):
    lane = lax.broadcasted_iota(jnp.int32, pair.shape, 1)
    zero = jnp.zeros_like(pair)
    return jnp.concatenate(
        [jnp.where(lane < LANES // 2, pair, zero), jnp.where(lane < LANES // 2, zero, pair)], axis=0
    )


def forward_chunk(
    width, at, zx_ref, bcdt_ref, pos_ref, prm_ref, head_ref, expand_ref, mixed_ref, g_ref, sum_ref, state_ref, ext,
    state,
):
    if isinstance(at, int):
        rows = slice(at * CHUNK, (at + 1) * CHUNK)
    else:
        rows = pl.ds(pl.multiple_of(at * CHUNK, CHUNK), CHUNK)
    ext[:8, :] = ext[CHUNK:, :]
    k = prepare_chunk(
        width,
        zx_ref[rows, width:],
        bcdt_ref[rows, : 2 * LANES],
        bcdt_ref[rows, 2 * LANES :],
        pos_ref[rows, :],
        prm_ref,
        head_ref,
        expand_ref,
        ext,
    )
    stepped = (k["xc"] * k["dt_w"]).astype(BF16)
    held = state[...]
    held_low = held.astype(BF16)
    state_ref[at] = held_low
    reached = dot(k["c"], held_low) * k["in_w"] + prm_ref[6:7, :width] * k["xc"]
    weighted = (stepped.astype(F32) * k["tail_w"]).astype(BF16)
    state[...] = k["carried_w"] * held + dot(k["b"], weighted, CONTRACT_FIRST)
    for pair in range(width // LANES):
        lanes = slice(pair * LANES, (pair + 1) * LANES)
        mixing = jnp.concatenate(
            [
                (decay_of(k, 2 * pair) * k["scores"]).astype(BF16),
                (decay_of(k, 2 * pair + 1) * k["scores"]).astype(BF16),
            ],
            axis=1,
        )
        mixed_ref[rows, lanes] = dot(mixing, halves(stepped[:, lanes])) + reached[:, lanes]
    z = zx_ref[rows, :width].astype(F32)
    g = mixed_ref[rows, :] * (z * jax.nn.sigmoid(z))
    g_ref[rows, :] = g
    total = jnp.sum(g * g, axis=1, keepdims=True)
    sum_ref[:, rows] = jnp.broadcast_to(total, (CHUNK, LANES)).T[:8, :]


def forward_kernel(
    width, zx_ref, bcdt_ref, pos_ref, prm_ref, head_ref, expand_ref, mixed_ref, g_ref, sum_ref, state_ref, ext, state
):
    @pl.when(pl.program_id(0) == 0)
    def _():
        state[...] = jnp.zeros_like(state)
        ext[...] = jnp.zeros_like(ext)

    forward_chunk(
        width, 0, zx_ref, bcdt_ref, pos_ref, prm_ref, head_ref, expand_ref, mixed_ref, g_ref, sum_ref, state_ref, ext,
        state,
    )


def backward_chunk(
    width, tokens, halo_x, halo_bc, held, zx_ref, bcdt_ref, pos_ref, prm_ref, head_ref, expand_ref, mixed_ref, g_ref,
    dyo_ref, coef_ref, grad_x_ref, grad_bcdt_ref, grad_t_ref, small_ref, ext, d_state, later, later_pos,
):
    rows = CHUNK
    ext[:8, :width] = halo_x.astype(F32)[8:, :]
    ext[:8, width:] = halo_bc.astype(F32)[8:, :]
    pos = pos_ref[tokens, :]
    k = prepare_chunk(
        width,
        zx_ref[tokens, width:],
        bcdt_ref[tokens, : 2 * LANES],
        bcdt_ref[tokens, 2 * LANES :],
        pos,
        prm_ref,
        head_ref,
        expand_ref,
        ext,
    )
    xc = k["xc"]
    z = zx_ref[tokens, :width].astype(F32)
    r_col = coef_ref[tokens, 0:1]
    back_col = coef_ref[tokens, 8:9]
    g = g_ref[tokens, :]
    dyo = dyo_ref[tokens, :].astype(F32)
    skip = prm_ref[6:7, :width]
    y = mixed_ref[tokens, :] - skip * xc
    dg = r_col * (dyo * prm_ref[5:6, :width]) - g * back_col
    dy = dg * (z * jax.nn.sigmoid(z))
    small_ref[5:6, :width] += jnp.sum(dyo * g * r_col, axis=0, keepdims=True)
    small_ref[6:7, :width] += jnp.sum(dy * xc, axis=0, keepdims=True)

    stepped = (xc * k["dt_w"]).astype(BF16)
    dy_low = dy.astype(BF16)
    d_held = d_state[...]
    d_held_low = d_held.astype(BF16)
    held_low = held
    weighted = (stepped.astype(F32) * k["tail_w"]).astype(BF16)
    dy_in = (dy * k["in_w"]).astype(BF16)
    from_state = dot(k["b"], d_held_low) * k["tail_w"]
    dc = dot(dy_in, held_low, CONTRACT_LAST)
    db = dot(weighted, d_held_low, CONTRACT_LAST)
    d_state[...] = k["carried_w"] * d_held + dot(k["c"], dy_in, CONTRACT_FIRST)
    d_scores = jnp.zeros((rows, rows), F32)
    d_stepped = []
    for pair in range(width // LANES):
        lanes = slice(pair * LANES, (pair + 1) * LANES)
        decay_a = decay_of(k, 2 * pair)
        decay_b = decay_of(k, 2 * pair + 1)
        mixing = jnp.concatenate(
            [(decay_a * k["scores"]).astype(BF16), (decay_b * k["scores"]).astype(BF16)], axis=0
        )
        d_mixing = dot(dy_low[:, lanes], halves(stepped[:, lanes]), CONTRACT_LAST)
        d_scores = d_scores + decay_a * d_mixing[:, :rows] + decay_b * d_mixing[:, rows:]
        d_stepped.append(dot(mixing, halves(dy_low[:, lanes]), CONTRACT_FIRST))
    d_stepped = jnp.concatenate(d_stepped, axis=1) + from_state
    d_scores = jnp.where(k["same"], d_scores, 0.0).astype(BF16)
    dc = dc + dot(d_scores, k["b"])
    db = db + dot(d_scores, k["c"], CONTRACT_FIRST)
    dxc = skip * dy + d_stepped * k["dt_w"]

    stepped_f = stepped.astype(F32)
    tail_term = jnp.sum(stepped_f * from_state, axis=0, keepdims=True) + k["carried_w"] * jnp.sum(
        held_low.astype(F32) * d_held, axis=0, keepdims=True
    )
    gathered = two_parts(
        jnp.concatenate(
            [
                d_stepped * xc,
                dy_low.astype(F32) * y - stepped_f * d_stepped,
                jnp.broadcast_to(tail_term, (8, width)),
            ],
            axis=0,
        )
    )
    expand = expand_ref[:LANES, :]
    narrow = dot(gathered[:, :width], expand, CONTRACT_LAST) + dot(gathered[:, width:], expand, CONTRACT_LAST)
    d_dt = narrow[:rows]
    d_cum = narrow[rows : 2 * rows]
    upper = (k["s_idx"] >= k["t_idx"]).astype(F32)
    d_decay = (
        lax.dot_general(
            upper, d_cum, (((1,), (0,)), ((), ())), precision=HIGHEST, preferred_element_type=F32
        )
        + narrow[2 * rows : 2 * rows + 1]
    )
    d_raw = (d_dt - d_decay * head_ref[1:2, :]) * jax.nn.sigmoid(k["raw"])
    small_ref[7:8, :LANES] += jnp.sum(d_raw, axis=0, keepdims=True)
    small_ref[7:8, LANES : 2 * LANES] += jnp.sum(d_decay * k["log_decay"], axis=0, keepdims=True)
    grad_bcdt_ref[tokens, 2 * LANES :] = d_raw.astype(BF16)

    pre, sig = k["pre"], k["sig"]
    d_pre = jnp.concatenate([dxc, db, dc], axis=1) * (sig * (1.0 + pre * (1.0 - sig)))
    small_ref[4:5, :] += jnp.sum(d_pre, axis=0, keepdims=True)
    later[:rows, :] = d_pre
    later_pos[:rows, :] = jnp.broadcast_to(pos, (rows, LANES))
    d_in = prm_ref[3:4, :] * d_pre
    small_ref[3:4, :] += jnp.sum(d_pre * ext[8:, :], axis=0, keepdims=True)
    for back in (1, 2, 3):
        here = (pos >= back).astype(F32)
        small_ref[3 - back : 4 - back, :] += jnp.sum(
            d_pre * (ext[8 - back : 8 - back + rows, :] * here), axis=0, keepdims=True
        )
        there = (later_pos[back : back + rows, 0:1] >= back).astype(F32)
        d_in = d_in + prm_ref[3 - back : 4 - back, :] * (later[back : back + rows, :] * there)
    grad_x_ref[tokens, :] = d_in[:, :width].astype(BF16)
    grad_bcdt_ref[tokens, : 2 * LANES] = d_in[:, width:].astype(BF16)
    later[rows:, :] = later[:8, :]
    later_pos[rows:, :] = later_pos[:8, :]
    if grad_t_ref is not None:
        grad_t_ref[:width, tokens] = d_in[:, :width].T.astype(BF16)


def backward_start(small_ref, d_state, later, later_pos):
    d_state[...] = jnp.zeros_like(d_state)
    later[...] = jnp.zeros_like(later)
    later_pos[...] = jnp.zeros_like(later_pos)
    small_ref[...] = jnp.zeros_like(small_ref)


def backward_kernel(
    width, zx_ref, bcdt_ref, halo_x_ref, halo_bc_ref, pos_ref, prm_ref, head_ref,
    expand_ref, mixed_ref, g_ref, state_ref, dyo_ref, coef_ref, grad_x_ref, grad_bcdt_ref, small_ref, ext, d_state,
    later, later_pos,
):
    @pl.when(pl.program_id(0) == 0)
    def _():
        backward_start(small_ref, d_state, later, later_pos)

    backward_chunk(
        width, slice(0, CHUNK), halo_x_ref[...], halo_bc_ref[:, : 2 * LANES], state_ref[0], zx_ref, bcdt_ref, pos_ref,
        prm_ref, head_ref, expand_ref, mixed_ref, g_ref, dyo_ref, coef_ref, grad_x_ref, grad_bcdt_ref, None, small_ref,
        ext, d_state, later, later_pos,
    )


def mixer_forward(width, zx, bcdt, pos, prm, head_prm, expand):
    rows = zx.shape[0]
    chunks = rows // CHUNK

    def tokens(columns):
        return pl.BlockSpec((CHUNK, columns), lambda i: (i, 0))

    def whole(array):
        return pl.BlockSpec(array.shape, lambda i: (0, 0))

    return pl.pallas_call(
        functools.partial(forward_kernel, width),
        out_shape=(
            jax.ShapeDtypeStruct((rows, width), F32),
            jax.ShapeDtypeStruct((rows, width), F32),
            jax.ShapeDtypeStruct((8, rows), F32),
            jax.ShapeDtypeStruct((chunks, LANES, width), BF16),
        ),
        grid=(chunks,),
        in_specs=[tokens(2 * width), tokens(3 * LANES), tokens(1), whole(prm), whole(head_prm), whole(expand)],
        out_specs=(
            tokens(width),
            tokens(width),
            pl.BlockSpec((8, CHUNK), lambda i: (0, i)),
            pl.BlockSpec((1, LANES, width), lambda i: (i, 0, 0)),
        ),
        scratch_shapes=[
            pltpu.VMEM((CHUNK + 8, width + 2 * LANES), F32),
            pltpu.VMEM((LANES, width), F32),
        ],
        compiler_params=pltpu.CompilerParams(
            dimension_semantics=("arbitrary",), vmem_limit_bytes=40 * 1024 * 1024
        ),
    )(zx, bcdt, pos, prm, head_prm, expand)


def mixer_backward(width, zx, bcdt, pos, prm, head_prm, expand, mixed, g, states, dyo, coef):
    rows = zx.shape[0]
    chunks = rows // CHUNK

    def tokens(columns):
        return pl.BlockSpec((CHUNK, columns), lambda i: (chunks - 1 - i, 0))

    def before(columns, place):
        return pl.BlockSpec(
            (16, columns), lambda i: (jnp.maximum((chunks - 1 - i) * (CHUNK // 16) - 1, 0), place)
        )

    def whole(array):
        return pl.BlockSpec(array.shape, lambda i: (0, 0))

    return pl.pallas_call(
        functools.partial(backward_kernel, width),
        out_shape=(
            jax.ShapeDtypeStruct((rows, width), BF16),
            jax.ShapeDtypeStruct((rows, 3 * LANES), BF16),
            jax.ShapeDtypeStruct((8, width + 2 * LANES), F32),
        ),
        grid=(chunks,),
        in_specs=[
            tokens(2 * width),
            tokens(3 * LANES),
            before(width, 1),
            before(3 * LANES, 0),
            tokens(1),
            whole(prm),
            whole(head_prm),
            whole(expand),
            tokens(width),
            tokens(width),
            pl.BlockSpec((1, LANES, width), lambda i: (chunks - 1 - i, 0, 0)),
            tokens(width),
            tokens(LANES),
        ],
        out_specs=(
            tokens(width),
            tokens(3 * LANES),
            pl.BlockSpec((8, width + 2 * LANES), lambda i: (0, 0)),
        ),
        scratch_shapes=[
            pltpu.VMEM((CHUNK + 8, width + 2 * LANES), F32),
            pltpu.VMEM((LANES, width), F32),
            pltpu.VMEM((CHUNK + 8, width + 2 * LANES), F32),
            pltpu.VMEM((CHUNK + 8, LANES), jnp.int32),
        ],
        compiler_params=pltpu.CompilerParams(
            dimension_semantics=("arbitrary",), vmem_limit_bytes=48 * 1024 * 1024
        ),
        cost_estimate=pl.CostEstimate(flops=rows * width * 2048, bytes_accessed=rows * width * 20, transcendentals=0),
    )(zx, bcdt, zx, bcdt, pos, prm, head_prm, expand, mixed, g, states, dyo, coef)


MESH = pl.DeviceIdType.MESH


def tp_places():
    me = lax.axis_index("tp")
    return me, me + 1 - 2 * lax.rem(me, 2), lax.rem(me + 2, 4), 3 - me


def greet(peers):
    barrier = pltpu.get_barrier_semaphore()
    for peer in peers:
        pl.semaphore_signal(barrier, inc=1, device_id=peer, device_id_type=MESH)
    pl.semaphore_wait(barrier, len(peers))


def send(src, dst, send_sem, recv_sem, peer):
    return pltpu.make_async_remote_copy(
        src_ref=src, dst_ref=dst, send_sem=send_sem, recv_sem=recv_sem, device_id=peer, device_id_type=MESH
    )


class Gather:
    def __init__(self, whole, rows, send_sems, recv_sems, own=None):
        me, side, up, _ = tp_places()
        half = rows // 2

        def part(place, start, count):
            return whole.at[pl.ds(pl.multiple_of(place * rows + start, half), count)]

        own = part(me, 0, rows) if own is None else own
        self.to_side = send(own, part(me, 0, rows), send_sems.at[0], recv_sems.at[0], {"tp": side})
        self.to_up = send(own, part(me, 0, rows), send_sems.at[1], recv_sems.at[1], {"tp": up})
        self.pass_up = send(
            part(side, 0, half), part(side, 0, half), send_sems.at[2], recv_sems.at[2], {"tp": up}
        )
        self.pass_side = send(
            part(up, half, half), part(up, half, half), send_sems.at[3], recv_sems.at[3], {"tp": side}
        )

    def start(self):
        self.to_side.start()
        self.to_up.start()

    def forward(self):
        self.to_side.wait_recv()
        self.pass_up.start()
        self.to_up.wait_recv()
        self.pass_side.start()

    def finish(self):
        self.pass_up.wait_recv()
        self.pass_side.wait_recv()

    def end(self):
        for copy in (self.to_side, self.to_up, self.pass_up, self.pass_side):
            copy.wait_send()


def set_up(width, heads, inner, taps_ref, flat_ref, lens_ref, prm, head, expand, pos):
    rank = lax.axis_index("tp")
    channels = taps_ref.shape[1]
    own = pl.ds(pl.multiple_of(rank * width, LANES), width)
    own_gain = pl.ds(pl.multiple_of(channels + rank * width, LANES), width)
    prm[...] = jnp.zeros_like(prm)
    prm[0:4, :width] = taps_ref[:, own]
    prm[0:4, width:] = taps_ref[:, inner:]
    prm[4:5, :width] = flat_ref[:, own]
    prm[4:5, width:] = flat_ref[:, inner:channels]
    prm[5:6, :width] = flat_ref[:, own_gain]
    lane = lax.broadcasted_iota(jnp.int32, (LANES, LANES), 1)
    pick = ((lax.broadcasted_iota(jnp.int32, (LANES, LANES), 0) == lane + rank * heads) & (lane < heads)).astype(F32)
    start = channels + inner
    tiles = [jnp.broadcast_to(flat_ref[:, start + n * LANES : start + (n + 1) * LANES], (8, LANES)) for n in range(3)]
    tiles[1] = jnp.exp(tiles[1])
    picked = lax.dot_general(
        jnp.concatenate(tiles, axis=0), pick, (((1,), (0,)), ((), ())), precision=HIGHEST, preferred_element_type=F32
    )
    head[...] = jnp.concatenate([picked[0:1], picked[8:9], jnp.zeros((6, LANES), F32)], axis=0)
    row = lax.broadcasted_iota(jnp.int32, (2 * LANES, width), 0)
    column = lax.broadcasted_iota(jnp.int32, (2 * LANES, width), 1)
    expand[...] = (lax.rem(row, LANES) == column // (width // heads)).astype(F32).astype(BF16)
    prm[6:7, :width] = dot(two_parts(picked[16:24]), expand[...])[0:1]
    starts = [jnp.int32(0)]
    for n in range(lens_ref.shape[1] - 1):
        starts.append(starts[-1] + lens_ref[0, n])

    def place(i, carry):
        token = lax.broadcasted_iota(jnp.int32, (CHUNK, 1), 0) + i * CHUNK
        begun = jnp.zeros((CHUNK, 1), jnp.int32)
        for first in starts[1:]:
            begun = jnp.where(token >= first, first, begun)
        pos[pl.ds(pl.multiple_of(i * CHUNK, CHUNK), CHUNK), :] = token - begun
        return carry

    lax.fori_loop(0, pos.shape[0] // CHUNK, place, 0)


def first_kernel(
    inner, heads, own_cols, x_ref, gain_ref, small_ref, taps_ref, flat_ref, lens_ref, wz_ref, wx_ref, w_out_ref, d_own_ref,
    u_out, zx_out, bcdt_out, wbc_out, mixed_out, g_out, yo_out, yo_t_out, state_out, d_out, dyo_out, coef_out, pos_out,
    prm_out, head_out, expand_out,
    weights, w_out, u, zx, bcdt, wbc, mixed, g, yo, yo_t, states, d, dyo, coef, pos, prm, head, expand, ext, state, sums,
    acc, sems, sum_sems, load_sems, store_sems,
):
    rows, model = x_ref.shape
    total, width = mixed.shape
    chunks = total // CHUNK
    me, side, up, far = tp_places()
    dp = lax.axis_index("dp")
    parity = lax.rem(dp, 2)
    partner = {"dp": dp + 1 - 2 * parity}

    def block(place):
        return pl.ds(pl.multiple_of(place * rows, rows), rows)

    loads = [
        pltpu.make_async_copy(wz_ref, weights.at[:, :width], load_sems.at[0]),
        pltpu.make_async_copy(wx_ref, weights.at[:, width:], load_sems.at[1]),
        pltpu.make_async_copy(w_out_ref, w_out, load_sems.at[2]),
        pltpu.make_async_copy(d_own_ref, d.at[block(me)], load_sems.at[3]),
    ]
    for copy in loads:
        copy.start()
    stores = []

    def keep(source, target):
        copy = pltpu.make_async_copy(source, target, store_sems.at[len(stores)])
        copy.start()
        stores.append(copy)

    bc_own = pl.ds(pl.multiple_of(parity * LANES, LANES), LANES)
    wbc[pl.ds(pl.multiple_of(parity * LANES + me * own_cols, own_cols), own_cols), :] = small_ref[
        pl.ds(pl.multiple_of(parity * own_cols, own_cols), own_cols), :
    ]
    greet([{"tp": side}, {"tp": up}, {"tp": far}, partner])
    small_gather = Gather(wbc.at[bc_own], own_cols, sems.at[0], sems.at[1])
    small_gather.start()

    def norm(i, carry):
        piece = pl.ds(pl.multiple_of(i * 32, 32), 32)
        x = x_ref[piece, :].astype(F32)
        scale = lax.rsqrt(jnp.mean(x * x, axis=-1, keepdims=True) + EPSILON)
        u[pl.ds(pl.multiple_of(me * rows + i * 32, 32), 32), :] = (x * scale * gain_ref[...]).astype(BF16)
        return carry

    lax.fori_loop(0, rows // 32, norm, 0)
    gather = Gather(u, rows, sems.at[2], sems.at[3])
    gather.start()
    wbc[2 * LANES :, :] = jnp.zeros((LANES, model), BF16)
    wbc[2 * LANES : 2 * LANES + heads, :] = small_ref[2 * own_cols :, :]
    set_up(width, heads, inner, taps_ref, flat_ref, lens_ref, prm, head, expand, pos)
    keep(pos, pos_out)
    keep(prm, prm_out)
    keep(head, head_out)
    keep(expand, expand_out)
    loads[0].wait()
    loads[1].wait()

    def project(place):
        piece = block(place)

        def tile(n, carry):
            columns = pl.ds(pl.multiple_of(n * 256, 256), 256)
            zx[piece, columns] = dot(u[piece, :], weights[:, columns]).astype(BF16)
            return carry

        lax.fori_loop(0, 2 * width // 256, tile, 0)

    def project_small(place):
        bcdt[block(place), :] = dot(u[block(place), :], wbc[...], CONTRACT_LAST).astype(BF16)

    small_gather.forward()
    project(me)
    small_gather.finish()
    trade = send(wbc.at[bc_own], wbc.at[bc_own], sems.at[6, 0], sems.at[6, 1], partner)
    trade.start()
    gather.forward()
    project(side)
    project(up)
    trade.wait()
    keep(wbc, wbc_out)
    project_small(me)
    project_small(side)
    project_small(up)
    gather.finish()
    loads[3].wait()
    d_gather = Gather(d, rows, sems.at[4], sems.at[5])
    d_gather.start()
    keep(u, u_out)
    project(far)
    project_small(far)
    keep(zx, zx_out)
    keep(bcdt, bcdt_out)

    state[...] = jnp.zeros_like(state)
    ext[...] = jnp.zeros_like(ext)

    def chunk(i, carry):
        forward_chunk(
            width, i, zx, bcdt, pos, prm, head, expand, mixed, g, sums.at[0, 0], states, ext, state
        )
        return carry

    lax.fori_loop(0, chunks, chunk, 0)

    def exchange(which):
        copies = [
            send(
                sums.at[which, 0], sums.at[which, 1 + n], sum_sems.at[which, 0, n], sum_sems.at[which, 1, n], {"tp": peer}
            )
            for n, peer in enumerate((side, up, far))
        ]
        for copy in copies:
            copy.start()
        return copies

    copies = exchange(0)
    keep(mixed, mixed_out)
    keep(g, g_out)
    keep(states, state_out)
    loads[2].wait()

    def back_to_heads(place):
        piece = block(place)
        acc[...] = jnp.zeros_like(acc)

        def tile(n, carry):
            columns = pl.ds(pl.multiple_of(n * 256, 256), 256)
            low = dot(d[piece, :], w_out[columns, :], CONTRACT_LAST).astype(BF16)
            dyo[piece, columns] = low
            both = low.astype(F32) * prm[5:6, columns] * g[piece, columns]
            acc[...] += both[:, :LANES] + both[:, LANES:]
            return carry

        lax.fori_loop(0, width // 256, tile, 0)
        column = jnp.sum(acc[...], axis=1, keepdims=True)
        sums[1, 0, :, piece] = jnp.broadcast_to(column, (rows, LANES)).T[:8, :]
        keep(dyo.at[piece], dyo_out.at[piece])

    d_gather.forward()
    back_to_heads(me)
    for copy in copies:
        copy.wait()

    def gate(i, carry):
        piece = pl.ds(pl.multiple_of(i * CHUNK, CHUNK), CHUNK)
        squares = sums[0, 0, :, piece] + sums[0, 1, :, piece] + sums[0, 2, :, piece] + sums[0, 3, :, piece]
        scale = lax.rsqrt(squares / inner + EPSILON)
        columns = jnp.concatenate([scale, jnp.zeros((LANES - 8, LANES), F32)], axis=0).T
        gated = g[piece, :] * columns[:, 0:1] * prm[5:6, :width]
        yo[piece, :] = gated.astype(BF16)
        yo_t[:, piece] = gated.T.astype(BF16)
        return carry

    lax.fori_loop(0, chunks, gate, 0)
    keep(yo, yo_out)
    keep(yo_t, yo_t_out)
    back_to_heads(side)
    back_to_heads(up)
    d_gather.finish()
    keep(d, d_out)
    back_to_heads(far)
    copies = exchange(1)
    for copy in copies:
        copy.wait()

    def weigh(i, carry):
        piece = pl.ds(pl.multiple_of(i * CHUNK, CHUNK), CHUNK)
        squares = sums[0, 0, :, piece] + sums[0, 1, :, piece] + sums[0, 2, :, piece] + sums[0, 3, :, piece]
        cross = sums[1, 0, :, piece] + sums[1, 1, :, piece] + sums[1, 2, :, piece] + sums[1, 3, :, piece]
        scale = lax.rsqrt(squares / inner + EPSILON)
        back = scale * scale * scale * (cross / inner)
        coef[piece, :] = jnp.concatenate([scale, back, jnp.zeros((LANES - 16, LANES), F32)], axis=0).T
        return carry

    lax.fori_loop(0, chunks, weigh, 0)
    keep(coef, coef_out)
    small_gather.end()
    gather.end()
    d_gather.end()
    for copy in stores:
        copy.wait()


def first_part(inner, heads, own_cols, x_in, gain, small, taps, flat, lens, w_z, w_x, w_out, d_out):
    rows, model = x_in.shape
    total = 4 * rows
    width = w_z.shape[1]
    chunks = total // CHUNK
    vmem = pl.BlockSpec(memory_space=pltpu.VMEM)
    anywhere = pl.BlockSpec(memory_space=pl.ANY)
    results = [
        ((total, model), BF16),
        ((total, 2 * width), BF16),
        ((total, 3 * LANES), BF16),
        ((3 * LANES, model), BF16),
        ((total, width), F32),
        ((total, width), F32),
        ((total, width), BF16),
        ((width, total), BF16),
        ((chunks, LANES, width), BF16),
        ((total, model), BF16),
        ((total, width), BF16),
        ((total, LANES), F32),
        ((total, 1), jnp.int32),
        ((8, width + 2 * LANES), F32),
        ((8, LANES), F32),
        ((2 * LANES, width), BF16),
    ]
    return pl.pallas_call(
        functools.partial(first_kernel, inner, heads, own_cols),
        out_shape=[jax.ShapeDtypeStruct(*result) for result in results],
        in_specs=[vmem] * 5 + [pl.BlockSpec(memory_space=pltpu.SMEM)] + [anywhere] * 4,
        out_specs=[anywhere] * len(results),
        scratch_shapes=[pltpu.VMEM((model, 2 * width), BF16), pltpu.VMEM((width, model), BF16)]
        + [pltpu.VMEM(*result) for result in results]
        + [
            pltpu.VMEM((CHUNK + 8, width + 2 * LANES), F32),
            pltpu.VMEM((LANES, width), F32),
            pltpu.VMEM((2, 4, 8, total), F32),
            pltpu.VMEM((rows, LANES), F32),
            pltpu.SemaphoreType.DMA((7, 4)),
            pltpu.SemaphoreType.DMA((2, 2, 3)),
            pltpu.SemaphoreType.DMA((4,)),
            pltpu.SemaphoreType.DMA((24,)),
        ],
        compiler_params=pltpu.CompilerParams(
            collective_id=0, has_side_effects=True, vmem_limit_bytes=60 * 1024 * 1024
        ),
    )(x_in, gain, small, taps, flat, lens, w_z, w_x, w_out, d_out)


def add_into(target, other):
    tile = 128

    def one(i, carry):
        piece = pl.ds(pl.multiple_of(i * tile, tile), tile)
        target[piece, :] = (target[piece, :].astype(F32) + other[piece, :].astype(F32)).astype(BF16)
        return carry

    lax.fori_loop(0, target.shape[0] // tile, one, 0)


class LineSum:
    def __init__(self, parts, pair, right, left, pair_sems, right_sems, left_sems):
        dp = lax.axis_index("dp")
        self.dp = dp
        self.count = parts.shape[0] // 2
        self.z = dp // 2
        self.parity = lax.rem(dp, 2)
        self.partner = {"dp": dp + 1 - 2 * self.parity}
        self.parts, self.pair = parts, pair
        self.lines = {1: (right, right_sems), -1: (left, left_sems)}
        self.swaps = {}
        self.pair_sems = pair_sems

    def peers(self):
        n = 2 * self.count
        return [self.partner, {"dp": lax.rem(self.dp + 2, n)}, {"dp": lax.rem(self.dp + n - 2, n)}]

    def order(self):
        low, high, out = 0, self.count - 1, []
        while low <= high:
            out += [high, low] if low < high else [low]
            low, high = low + 1, high - 1
        return out

    def swap(self, z):
        copy = send(
            self.parts.at[2 * z + 1 - self.parity], self.pair.at[z], self.pair_sems.at[0, z], self.pair_sems.at[1, z],
            self.partner,
        )
        copy.start()
        self.swaps[z] = copy

    def merge(self, z):
        self.swaps[z].wait()
        add_into(self.parts.at[2 * z + self.parity], self.pair.at[z])

    def away(self, way):
        return self.z if way == 1 else self.count - 1 - self.z

    def copy(self, way, step):
        line, line_sems = self.lines[way]
        far = self.count - step + self.away(way)
        z = far if way == 1 else self.count - 1 - far
        chunk = self.parts.at[2 * z + self.parity]
        return chunk, send(
            chunk, line.at[step - 1], line_sems.at[0, step - 1], line_sems.at[1, step - 1],
            {"dp": self.dp + 2 * way},
        )

    def arrived(self, way, step):
        line, line_sems = self.lines[way]
        return send(
            self.parts.at[self.dp], line.at[step - 1], line_sems.at[0, step - 1], line_sems.at[1, step - 1],
            self.partner,
        )

    def move(self, step):
        for way in (1, -1):
            away = self.away(way)

            @pl.when(away == 0)
            def _():
                if step > 1:
                    self.copy(way, step - 1)[1].wait_send()
                self.copy(way, step)[1].start()

            if step > 1:

                @pl.when((away >= 1) & (away <= min(step - 1, self.count - 2)))
                def _():
                    chunk, copy = self.copy(way, step)
                    self.arrived(way, step - 1).wait_recv()
                    add_into(chunk, self.lines[way][0].at[step - 2])
                    copy.start()

    def finish(self):
        last = self.count - 1
        for way in (1, -1):

            @pl.when(self.away(way) >= 1)
            def _():
                self.arrived(way, last).wait_recv()

        total = self.parts.at[self.dp]
        for way in (1, -1):

            @pl.when(self.away(way) >= 1)
            def _():
                add_into(total, self.lines[way][0].at[last - 1])

        return total

    def end(self):
        for way in (1, -1):
            away = self.away(way)
            for step in range(1, self.count):

                @pl.when((away <= step - 1) & (away <= self.count - 2) & ((away >= 1) | (step == self.count - 1)))
                def _():
                    self.copy(way, step)[1].wait_send()


class PlaneSum:
    def __init__(self, away, to_side, to_up, in_half, in_side, in_up, sems):
        _, side, up, _ = tp_places()
        side, up = {"tp": side}, {"tp": up}
        rows = to_side.shape[0]
        half = rows // 2
        self.to_side, self.to_up, self.in_half, self.half = to_side, to_up, in_half, half
        self.in_side, self.in_up = in_side, in_up
        low, high = pl.ds(0, half), pl.ds(half, half)

        def one(n, source, target, peer):
            return send(source, target, sems.at[0, n], sems.at[1, n], peer)

        self.away_side = one(0, away.at[low], in_half.at[0], side)
        self.away_up = one(1, away.at[high], in_half.at[1], up)
        self.side_low = one(2, to_side.at[low], in_side.at[low], side)
        self.side_high = one(3, to_side.at[high], in_side.at[high], side)
        self.up_low = one(4, to_up.at[low], in_up.at[low], up)
        self.up_high = one(5, to_up.at[high], in_up.at[high], up)
        self.low, self.high = low, high

    def start_far(self):
        self.away_side.start()
        self.away_up.start()

    def start_side(self):
        self.side_low.start()

    def start_up(self):
        self.up_high.start()

    def pass_on(self):
        self.away_side.wait_recv()
        add_into(self.to_up.at[self.low], self.in_half.at[0])
        self.up_low.start()
        self.away_up.wait_recv()
        add_into(self.to_side.at[self.high], self.in_half.at[1])
        self.side_high.start()

    def finish(self):
        for copy in (self.side_low, self.up_high, self.side_high, self.up_low):
            copy.wait_recv()

    def end(self):
        for copy in (self.away_side, self.away_up, self.side_low, self.side_high, self.up_low, self.up_high):
            copy.wait_send()


def plane_scratch(rows, model):
    half = rows // 2
    return [
        pltpu.VMEM((rows, model), BF16),
        pltpu.VMEM((rows, model), BF16),
        pltpu.VMEM((rows, model), BF16),
        pltpu.VMEM((2, half, model), BF16),
        pltpu.VMEM((rows, model), BF16),
        pltpu.VMEM((rows, model), BF16),
        pltpu.SemaphoreType.DMA((2, 6)),
    ]


def line_scratch(dp_count, shape):
    z = dp_count // 2
    return [
        pltpu.VMEM((dp_count,) + shape, BF16),
        pltpu.VMEM((z,) + shape, BF16),
        pltpu.VMEM((z - 1,) + shape, BF16),
        pltpu.VMEM((z - 1,) + shape, BF16),
        pltpu.SemaphoreType.DMA((2, z)),
        pltpu.SemaphoreType.DMA((2, z - 1)),
        pltpu.SemaphoreType.DMA((2, z - 1)),
    ]


class Copies:
    def __init__(self, sems):
        self.sems, self.started = sems, []

    def start(self, source, target):
        copy = pltpu.make_async_copy(source, target, self.sems.at[len(self.started)])
        copy.start()
        self.started.append(copy)
        return copy


def product_chunk(left_t, right, chunk, target, tile):
    columns = pl.ds(pl.multiple_of(chunk * target.shape[1], target.shape[1]), target.shape[1])

    def one(i, carry):
        piece = pl.ds(pl.multiple_of(i * tile, tile), tile)
        target[piece, :] = dot(left_t[piece, :], right[:, columns]).astype(BF16)
        return carry

    lax.fori_loop(0, target.shape[0] // tile, one, 0)


def second_kernel(
    x_ref, yo_ref, yo_t_ref, d_ref, w_out_ref, dyo_ref, g_ref, mixed_ref, zx_ref, coef_ref, prm_ref, u_ref,
    block_out, gw_out, dz_out, gz_out,
    yo, yo_t, d, w_out, dyo, g, mixed, z, coef, own, gz,
    parts, pair, right, left, pair_sems, right_sems, left_sems,
    away, to_side, to_up, in_half, in_side, in_up, plane_sems, load_sems, store_sems,
):
    rows, model = x_ref.shape
    total, width = yo.shape
    me, side, up, far = tp_places()
    loads, stores = Copies(load_sems), Copies(store_sems)
    load_yo = loads.start(yo_ref, yo)
    load_w = loads.start(w_out_ref, w_out)
    load_yo_t = loads.start(yo_t_ref, yo_t)
    load_d = loads.start(d_ref, d)
    rest = [
        loads.start(dyo_ref, dyo),
        loads.start(g_ref, g),
        loads.start(mixed_ref, mixed),
        loads.start(zx_ref.at[:, :width], z),
        loads.start(coef_ref, coef),
    ]
    line = LineSum(parts, pair, right, left, pair_sems, right_sems, left_sems)
    plane = PlaneSum(away, to_side, to_up, in_half, in_side, in_up, plane_sems)
    greet([{"tp": side}, {"tp": up}] + line.peers())

    def out_block(place, target):
        piece = pl.ds(pl.multiple_of(place * rows, rows), rows)

        def tile(n, carry):
            columns = pl.ds(pl.multiple_of(n * 256, 256), 256)
            target[:, columns] = dot(yo[piece, :], w_out[:, columns]).astype(target.dtype)
            return carry

        lax.fori_loop(0, model // 256, tile, 0)

    load_yo.wait()
    load_w.wait()
    out_block(far, away)
    plane.start_far()
    load_yo_t.wait()
    load_d.wait()
    for z_chunk in line.order():
        for chunk in (2 * z_chunk + 1 - line.parity, 2 * z_chunk + line.parity):
            product_chunk(yo_t, d, chunk, parts.at[chunk], width // 2)
            if z_chunk not in line.swaps:
                line.swap(z_chunk)
    load_u = loads.start(u_ref, d)
    order = line.order()
    for z_chunk in order[:2]:
        line.merge(z_chunk)
    line.move(1)
    for z_chunk in order[2:]:
        line.merge(z_chunk)
    out_block(side, to_side)
    plane.start_side()
    out_block(up, to_up)
    plane.start_up()
    out_block(me, own)
    for copy in rest:
        copy.wait()

    def gate_back(i, carry):
        piece = pl.ds(pl.multiple_of(i * CHUNK, CHUNK), CHUNK)
        z_piece = z[piece, :].astype(F32)
        sig = jax.nn.sigmoid(z_piece)
        dg = coef[piece, 0:1] * (dyo[piece, :].astype(F32) * prm_ref[5:6, :width]) - g[piece, :] * coef[piece, 8:9]
        dz = dg * mixed[piece, :] * (sig * (1.0 + z_piece * (1.0 - sig)))
        yo[piece, :] = dz.astype(BF16)
        yo_t[:, piece] = dz.T.astype(BF16)
        return carry

    chunks = total // CHUNK
    lax.fori_loop(0, chunks, gate_back, 0)
    stores.start(yo, dz_out)
    line.move(2)
    plane.pass_on()
    load_u.wait()
    dp_count = parts.shape[0]

    def gate_products(first, last):
        def one(chunk, carry):
            product_chunk(yo_t, d, chunk, gz.at[chunk], width // 2)
            return carry

        lax.fori_loop(first, last, one, 0)

    gate_products(0, dp_count)
    stores.start(gz, gz_out)
    for step in range(3, line.count):
        line.move(step)
    plane.finish()

    def add_own(i, carry):
        piece = pl.ds(pl.multiple_of(i * 32, 32), 32)
        total_out = own[piece, :] + in_side[piece, :].astype(F32) + in_up[piece, :].astype(F32)
        block_out[piece, :] = (x_ref[piece, :].astype(F32) + total_out).astype(BF16)
        return carry

    lax.fori_loop(0, rows // 32, add_own, 0)
    sum_ref = line.finish()
    gw_out[...] = sum_ref[...].astype(F32)
    line.end()
    plane.end()
    for copy in stores.started:
        copy.wait()


def second_part(x_in, yo, yo_t, d, w_out, dyo, g, mixed, zx, coef, prm, u):
    rows, model = x_in.shape
    total, width = yo.shape
    dp_count = lax.axis_size("dp")
    cut = model // dp_count
    vmem = pl.BlockSpec(memory_space=pltpu.VMEM)
    anywhere = pl.BlockSpec(memory_space=pl.ANY)
    return pl.pallas_call(
        second_kernel,
        out_shape=(
            jax.ShapeDtypeStruct((rows, model), BF16),
            jax.ShapeDtypeStruct((width, cut), F32),
            jax.ShapeDtypeStruct((total, width), BF16),
            jax.ShapeDtypeStruct((dp_count, width, cut), BF16),
        ),
        in_specs=[vmem] + [anywhere] * 9 + [vmem, anywhere],
        out_specs=(vmem, vmem, anywhere, anywhere),
        scratch_shapes=[
            pltpu.VMEM((total, width), BF16),
            pltpu.VMEM((width, total), BF16),
            pltpu.VMEM((total, model), BF16),
            pltpu.VMEM((width, model), BF16),
            pltpu.VMEM((total, width), BF16),
            pltpu.VMEM((total, width), F32),
            pltpu.VMEM((total, width), F32),
            pltpu.VMEM((total, width), BF16),
            pltpu.VMEM((total, LANES), F32),
            pltpu.VMEM((rows, model), F32),
            pltpu.VMEM((dp_count, width, cut), BF16),
        ]
        + line_scratch(dp_count, (width, cut))
        + plane_scratch(rows, model)
        + [pltpu.SemaphoreType.DMA((10,)), pltpu.SemaphoreType.DMA((2,))],
        compiler_params=pltpu.CompilerParams(
            collective_id=1, has_side_effects=True, vmem_limit_bytes=60 * 1024 * 1024
        ),
    )(x_in, yo, yo_t, d, w_out, dyo, g, mixed, zx, coef, prm, u)


def third_kernel(
    own_cols, heads, zx_ref, bcdt_ref, pos_ref, prm_ref, head_ref, expand_ref, mixed_ref, g_ref, state_ref, dyo_ref,
    coef_ref, u_ref, gz_ref,
    gw_z, dx_out, dbcdt_out, gl_out, small_out,
    zx, bcdt, mixed, g, states, dyo, u, dx, dbcdt, dx_t, gl, bc_in, ext, d_state, later, later_pos,
    parts, pair, right, left, pair_sems, right_sems, left_sems, bc_sems, load_sems, store_sems,
):
    total, width = mixed.shape
    chunks = total // CHUNK
    me, side, up, far = tp_places()
    dp_count = parts.shape[0]
    loads, stores = Copies(load_sems), Copies(store_sems)
    load_parts = loads.start(gz_ref, parts)
    first_loads = [
        loads.start(zx_ref, zx),
        loads.start(bcdt_ref, bcdt),
        loads.start(mixed_ref, mixed),
        loads.start(g_ref, g),
        loads.start(state_ref, states),
        loads.start(dyo_ref, dyo),
    ]
    load_u = loads.start(u_ref, u)
    line = LineSum(parts, pair, right, left, pair_sems, right_sems, left_sems)
    greet([{"tp": side}, {"tp": up}, {"tp": far}] + line.peers())
    load_parts.wait()
    order = line.order()
    for z_chunk in order:
        line.swap(z_chunk)
    backward_start(small_out, d_state, later, later_pos)
    for z_chunk in order[:2]:
        line.merge(z_chunk)
    line.move(1)
    for z_chunk in order[2:]:
        line.merge(z_chunk)
    for copy in first_loads:
        copy.wait()
    hooks = {3: 2, 6: 3}

    def chunk(i, carry):
        at = chunks - 1 - i
        tokens = pl.ds(pl.multiple_of(at * CHUNK, CHUNK), CHUNK)
        halo = pl.ds(pl.multiple_of(lax.rem(at * CHUNK + total - 16, total), 16), 16)
        backward_chunk(
            width, tokens, zx[halo, width:], bcdt[halo, : 2 * LANES], states[at], zx, bcdt, pos_ref, prm_ref, head_ref,
            expand_ref, mixed, g, dyo, coef_ref, dx, dbcdt, dx_t, small_out, ext, d_state, later, later_pos,
        )
        for when, step in hooks.items():

            @pl.when(i == when - 1)
            def _():
                line.move(step)

        return carry

    lax.fori_loop(0, chunks, chunk, 0)
    stores.start(dx, dx_out)
    stores.start(dbcdt, dbcdt_out)

    pick_row = lax.broadcasted_iota(jnp.int32, (2 * own_cols, 2 * LANES), 0)
    pick_col = lax.broadcasted_iota(jnp.int32, (2 * own_cols, 2 * LANES), 1)

    def columns_of(place):
        wanted = jnp.where(pick_row < own_cols, pick_row, pick_row - own_cols + LANES) + place * own_cols
        pick = (pick_col == wanted).astype(F32).astype(BF16)
        return dot(pick, dbcdt[:, : 2 * LANES], CONTRACT_LAST)

    copies = []
    for n, peer in enumerate((side, up, far)):
        bc_in[n] = columns_of(peer).astype(BF16)
        copies.append(send(bc_in.at[n], bc_in.at[3 + n], bc_sems.at[0, n], bc_sems.at[1, n], {"tp": peer}))
        copies[-1].start()
    own_bc = columns_of(me)
    dx_t[width:, :] = jnp.zeros((LANES, total), BF16)
    dx_t[width + 2 * own_cols : width + 2 * own_cols + heads, :] = dbcdt[:, 2 * LANES :].astype(F32).T[:heads, :].astype(
        BF16
    )
    load_u.wait()
    for copy in copies:
        copy.wait()
    for n in range(3):
        own_bc = own_bc + bc_in[3 + n].astype(F32)
    dx_t[width : width + 2 * own_cols, :] = own_bc.astype(BF16)

    def last_product(c, carry):
        product_chunk(dx_t, u, c, gl.at[c], (width + LANES) // 3)
        return carry

    lax.fori_loop(0, dp_count, last_product, 0)
    stores.start(gl, gl_out)
    sum_ref = line.finish()

    def turn(i, carry):
        piece = pl.ds(pl.multiple_of(i * CHUNK, CHUNK), CHUNK)
        gw_z[:, piece] = sum_ref[piece, :].astype(F32).T
        return carry

    lax.fori_loop(0, width // CHUNK, turn, 0)
    line.end()
    for copy in stores.started:
        copy.wait()


def third_part(own_cols, heads, zx, bcdt, pos, prm, head_prm, expand, mixed, g, states, dyo, coef, u, gz):
    total, width = mixed.shape
    model = u.shape[1]
    dp_count = lax.axis_size("dp")
    cut = model // dp_count
    vmem = pl.BlockSpec(memory_space=pltpu.VMEM)
    anywhere = pl.BlockSpec(memory_space=pl.ANY)
    return pl.pallas_call(
        functools.partial(third_kernel, own_cols, heads),
        out_shape=(
            jax.ShapeDtypeStruct((cut, width), F32),
            jax.ShapeDtypeStruct((total, width), BF16),
            jax.ShapeDtypeStruct((total, 3 * LANES), BF16),
            jax.ShapeDtypeStruct((dp_count, width + LANES, cut), BF16),
            jax.ShapeDtypeStruct((8, width + 2 * LANES), F32),
        ),
        in_specs=[anywhere] * 2 + [vmem] * 4 + [anywhere] * 4 + [vmem] + [anywhere] * 2,
        out_specs=(vmem, anywhere, anywhere, anywhere, vmem),
        scratch_shapes=[
            pltpu.VMEM(zx.shape, BF16),
            pltpu.VMEM(bcdt.shape, BF16),
            pltpu.VMEM((total, width), F32),
            pltpu.VMEM((total, width), F32),
            pltpu.VMEM(states.shape, BF16),
            pltpu.VMEM((total, width), BF16),
            pltpu.VMEM((total, model), BF16),
            pltpu.VMEM((total, width), BF16),
            pltpu.VMEM((total, 3 * LANES), BF16),
            pltpu.VMEM((width + LANES, total), BF16),
            pltpu.VMEM((dp_count, width + LANES, cut), BF16),
            pltpu.VMEM((6, 2 * own_cols, total), BF16),
            pltpu.VMEM((CHUNK + 8, width + 2 * LANES), F32),
            pltpu.VMEM((LANES, width), F32),
            pltpu.VMEM((CHUNK + 8, width + 2 * LANES), F32),
            pltpu.VMEM((CHUNK + 8, LANES), jnp.int32),
        ]
        + line_scratch(dp_count, (width, cut))
        + [pltpu.SemaphoreType.DMA((2, 3)), pltpu.SemaphoreType.DMA((8,)), pltpu.SemaphoreType.DMA((3,))],
        compiler_params=pltpu.CompilerParams(
            collective_id=2, has_side_effects=True, vmem_limit_bytes=60 * 1024 * 1024
        ),
    )(zx, bcdt, pos, prm, head_prm, expand, mixed, g, states, dyo, coef, u, gz)


def fourth_kernel(
    x_ref, d_own_ref, gain_ref, small_ref, dz_ref, dx_ref, dbcdt_ref, wz_ref, wx_ref, wbc_ref, u_ref, gl_ref,
    gw_x, gw_rest, grad_x, sums,
    dz, dx, dbcdt, wz, wx, wbc, u, own, gain_part, packed, over_z,
    parts, pair, right, left, pair_sems, right_sems, left_sems,
    away, to_side, to_up, in_half, in_side, in_up, plane_sems, z_sems, tp_sems, load_sems,
):
    rows, model = x_ref.shape
    width = dz.shape[1]
    me, side, up, far = tp_places()
    dp_count = parts.shape[0]
    loads = Copies(load_sems)
    load_parts = loads.start(gl_ref, parts)
    first_loads = [
        loads.start(dz_ref, dz),
        loads.start(dx_ref, dx),
        loads.start(dbcdt_ref, dbcdt),
        loads.start(wz_ref, wz),
        loads.start(wx_ref, wx),
        loads.start(wbc_ref, wbc),
        loads.start(u_ref, u),
    ]
    line = LineSum(parts, pair, right, left, pair_sems, right_sems, left_sems)
    plane = PlaneSum(away, to_side, to_up, in_half, in_side, in_up, plane_sems)
    others = [{"dp": lax.rem(line.dp + 2 * n, dp_count)} for n in range(1, dp_count // 2)]
    greet([{"tp": side}, {"tp": up}, {"tp": far}, line.partner] + others)
    load_parts.wait()
    order = line.order()
    for z_chunk in order:
        line.swap(z_chunk)
    gain_part[...] = jnp.zeros_like(gain_part)

    def du_block(place, target):
        piece = pl.ds(pl.multiple_of(place * rows, rows), rows)

        def tile(n, carry):
            columns = pl.ds(pl.multiple_of(n * 256, 256), 256)
            du = (
                dot(dz[piece, :], wz[columns, :], CONTRACT_LAST)
                + dot(dx[piece, :], wx[columns, :], CONTRACT_LAST)
                + dot(dbcdt[piece, :], wbc[:, columns])
            )
            target[:, columns] = du.astype(target.dtype)
            gain_part[0:1, columns] += jnp.sum(du * u[piece, columns].astype(F32), axis=0, keepdims=True)
            return carry

        lax.fori_loop(0, model // 256, tile, 0)

    for copy in first_loads:
        copy.wait()
    du_block(far, away)
    plane.start_far()
    for z_chunk in order[:2]:
        line.merge(z_chunk)
    line.move(1)
    for z_chunk in order[2:]:
        line.merge(z_chunk)
    du_block(side, to_side)
    plane.start_side()
    du_block(up, to_up)
    plane.start_up()
    du_block(me, own)

    wide = width + 2 * LANES
    packed[0, :, :wide] = small_ref[...]
    packed[0, :, wide:] = jnp.concatenate([gain_part[0:1, :] / gain_ref[...], jnp.zeros((7, model), F32)], axis=0)
    trade = send(packed.at[0], packed.at[1], z_sems.at[0, 0], z_sems.at[1, 0], line.partner)
    trade.start()
    plane.pass_on()
    line.move(2)
    trade.wait()
    over_z[0] = packed[0] + packed[1]
    copies = [
        send(over_z.at[0], over_z.at[n], z_sems.at[0, n], z_sems.at[1, n], others[n - 1])
        for n in range(1, dp_count // 2)
    ]
    for copy in copies:
        copy.start()
    for copy in copies:
        copy.wait()
    everything = over_z[0]
    for n in range(1, dp_count // 2):
        everything = everything + over_z[n]
    sums[me] = everything
    copies = [
        send(sums.at[me], sums.at[me], tp_sems.at[0, n], tp_sems.at[1, n], {"tp": peer})
        for n, peer in enumerate((side, up, far))
    ]
    for copy in copies:
        copy.start()
    for step in range(3, line.count):
        line.move(step)
    plane.finish()

    def norm_back(i, carry):
        piece = pl.ds(pl.multiple_of(i * 32, 32), 32)
        x = x_ref[piece, :].astype(F32)
        r_in = lax.rsqrt(jnp.mean(x * x, axis=-1, keepdims=True) + EPSILON)
        du = own[piece, :] + in_side[piece, :].astype(F32) + in_up[piece, :].astype(F32)
        e_in = du * gain_ref[...]
        back = r_in * r_in * r_in * jnp.mean(e_in * x, axis=-1, keepdims=True)
        grad_x[piece, :] = d_own_ref[piece, :].astype(F32) + r_in * e_in - x * back
        return carry

    lax.fori_loop(0, rows // 32, norm_back, 0)
    for copy in copies:
        copy.wait()
    sum_ref = line.finish()

    def turn(i, carry):
        piece = pl.ds(pl.multiple_of(i * CHUNK, CHUNK), CHUNK)
        gw_x[:, piece] = sum_ref[piece, :].astype(F32).T
        return carry

    lax.fori_loop(0, width // CHUNK, turn, 0)
    gw_rest[...] = sum_ref[width:, :].astype(F32).T
    line.end()
    plane.end()


def fourth_part(x_in, d_out, gain, small, dz, dx, dbcdt, w_z, w_x, wbc, u, gl):
    rows, model = x_in.shape
    total, width = dz.shape
    dp_count = lax.axis_size("dp")
    cut = model // dp_count
    wide = width + 2 * LANES + model
    vmem = pl.BlockSpec(memory_space=pltpu.VMEM)
    anywhere = pl.BlockSpec(memory_space=pl.ANY)
    return pl.pallas_call(
        fourth_kernel,
        out_shape=(
            jax.ShapeDtypeStruct((cut, width), F32),
            jax.ShapeDtypeStruct((cut, LANES), F32),
            jax.ShapeDtypeStruct((rows, model), F32),
            jax.ShapeDtypeStruct((4, 8, wide), F32),
        ),
        in_specs=[vmem] * 4 + [anywhere] * 8,
        out_specs=(vmem,) * 4,
        scratch_shapes=[
            pltpu.VMEM((total, width), BF16),
            pltpu.VMEM((total, width), BF16),
            pltpu.VMEM((total, 3 * LANES), BF16),
            pltpu.VMEM((model, width), BF16),
            pltpu.VMEM((model, width), BF16),
            pltpu.VMEM((3 * LANES, model), BF16),
            pltpu.VMEM((total, model), BF16),
            pltpu.VMEM((rows, model), F32),
            pltpu.VMEM((8, model), F32),
            pltpu.VMEM((2, 8, wide), F32),
            pltpu.VMEM((dp_count // 2, 8, wide), F32),
        ]
        + line_scratch(dp_count, (width + LANES, cut))
        + plane_scratch(rows, model)
        + [
            pltpu.SemaphoreType.DMA((2, dp_count // 2)),
            pltpu.SemaphoreType.DMA((2, 3)),
            pltpu.SemaphoreType.DMA((8,)),
        ],
        compiler_params=pltpu.CompilerParams(
            collective_id=3, has_side_effects=True, vmem_limit_bytes=60 * 1024 * 1024
        ),
    )(x_in, d_out, gain, small, dz, dx, dbcdt, w_z, w_x, wbc, u, gl)


def in_norm_scale(values):
    return lax.rsqrt(jnp.mean(values * values, axis=-1, keepdims=True) + EPSILON)


def body(
    x_in, norm_gain, w_z, w_x, w_b, w_c, w_dt, conv_w, conv_b, dt_bias, a_log, d_skip, gate_gain, w_out,
    doc_lens, d_out,
):
    tp_count = lax.axis_size("tp")
    rank = lax.axis_index("tp")
    dev_rows, model = x_in.shape
    rows = dev_rows * tp_count
    inner = gate_gain.shape[0]
    width = w_z.shape[1]
    heads = w_dt.shape[1]
    state_size = (conv_w.shape[0] - inner) // 2
    head_size = width // heads
    own_cols = w_b.shape[1]

    x_float = x_in.astype(F32)
    r_in = in_norm_scale(x_float)
    small_weights = jnp.concatenate([w_b, w_c, w_dt], axis=1).T
    if tp_count == 4:
        lanes = jnp.zeros((LANES - d_skip.shape[0],), F32)
        flat = jnp.concatenate([conv_b, gate_gain, dt_bias, lanes, a_log, lanes, d_skip, lanes])[None, :]
        (
            gathered, zx, bcdt, w_bcdt, mixed, g, yo, yo_t, states, grad_gathered, dyo, coef, pos, prm, head_prm, expand
        ) = first_part(
            inner, heads, own_cols, x_in, norm_gain[None, :], small_weights, conv_w.T, flat, doc_lens, w_z, w_x, w_out,
            d_out,
        )
        gain_own = prm[5, :width]
    else:
        normed = (x_float * r_in * norm_gain[None, :]).astype(BF16)
        gathered = lax.all_gather(normed, "tp", axis=0, tiled=True)
        w_bc = lax.all_gather(small_weights[: 2 * own_cols], "tp", axis=0).reshape(tp_count, 2, own_cols, model)
        w_bcdt = jnp.concatenate(
            [
                jnp.swapaxes(w_bc, 0, 1).reshape(2 * state_size, model),
                small_weights[2 * own_cols :],
                jnp.zeros((LANES - heads, model), BF16),
            ],
            axis=0,
        )
        zx = dot(gathered, jnp.concatenate([w_z, w_x], axis=1)).astype(BF16)
        bcdt = dot(gathered, w_bcdt, CONTRACT_LAST).astype(BF16)
        lengths = doc_lens[0]
        doc_starts = jnp.cumsum(lengths) - lengths
        positions = jnp.arange(rows, dtype=jnp.int32)
        started = jnp.where(positions[:, None] >= doc_starts[None, :], doc_starts[None, :], 0)
        pos = (positions - jnp.max(started, axis=1))[:, None]

        def own(array, count):
            return lax.dynamic_slice_in_dim(array, rank * count, count, axis=0)

        taps = jnp.concatenate([own(conv_w[:inner], width), conv_w[inner:]], axis=0).T
        bias = jnp.concatenate([own(conv_b[:inner], width), conv_b[inner:]])
        pad_bc = jnp.zeros((2 * state_size,), F32)
        gain_own = own(gate_gain, width)
        skip_own = jnp.repeat(own(d_skip, heads), head_size)
        prm = jnp.concatenate(
            [
                taps,
                bias[None],
                jnp.concatenate([gain_own, pad_bc])[None],
                jnp.concatenate([skip_own, pad_bc])[None],
                jnp.zeros((1, width + 2 * state_size), F32),
            ],
            axis=0,
        )
        pad_heads = jnp.zeros((LANES - heads,), F32)
        head_prm = jnp.concatenate(
            [
                jnp.concatenate([own(dt_bias, heads), pad_heads])[None],
                jnp.concatenate([jnp.exp(own(a_log, heads)), pad_heads])[None],
                jnp.zeros((6, LANES), F32),
            ],
            axis=0,
        )
        expand = (
            (jnp.arange(2 * LANES) % LANES)[:, None] == (jnp.arange(width) // head_size)[None, :]
        ).astype(BF16)
        mixed, g, g_sum, states = mixer_forward(width, zx, bcdt, pos, prm, head_prm, expand)
        grad_gathered = lax.all_gather(d_out, "tp", axis=0, tiled=True)
        dyo = dot(grad_gathered, w_out, CONTRACT_LAST).astype(BF16)
        eg_sum = jnp.sum(dyo.astype(F32) * gain_own[None, :] * g, axis=1)
        g_total, eg_total = lax.psum((g_sum[0], eg_sum), "tp")
        r_gate = lax.rsqrt(g_total / inner + EPSILON)
        zeros = jnp.zeros_like(r_gate)
        coef = jnp.stack([r_gate] + [zeros] * 7 + [r_gate**3 * (eg_total / inner)] + [zeros] * (LANES - 9), axis=1)
        yo = (g * r_gate[:, None] * gain_own[None, :]).astype(BF16)

    if tp_count == 4:
        block_out, grad_w_out, dz, gz = second_part(
            x_in, yo, yo_t, grad_gathered, w_out, dyo, g, mixed, zx, coef, prm, gathered
        )
        grad_w_z, grad_xs, grad_bcdt, gl, small = third_part(
            own_cols, heads, zx, bcdt, pos, prm, head_prm, expand, mixed, g, states, dyo, coef, gathered, gz
        )
        grad_w_x, grad_rest, grad_x, sums = fourth_part(
            x_in, d_out, norm_gain[None, :], small, dz, grad_xs, grad_bcdt, w_z, w_x, w_bcdt, gathered, gl
        )
        grad_norm_gain = jnp.sum(sums[:, 0, width + 2 * state_size :], axis=0)
    else:

        def scatter_dp(partial):
            return lax.psum_scatter(partial.astype(BF16), "dp", scatter_dimension=0, tiled=True).astype(F32)

        def scatter_tp(array):
            return lax.psum_scatter(array.astype(BF16), "tp", scatter_dimension=0, tiled=True).astype(F32)

        grad_w_out = scatter_dp(dot(grad_gathered, yo, CONTRACT_FIRST)).T
        z = zx[:, :width].astype(F32)
        sig_z = jax.nn.sigmoid(z)
        dg = coef[:, 0:1] * (dyo.astype(F32) * gain_own[None, :]) - g * coef[:, 8:9]
        dz = (dg * mixed * (sig_z * (1.0 + z * (1.0 - sig_z)))).astype(BF16)
        grad_w_z = scatter_dp(dot(gathered, dz, CONTRACT_FIRST))
        block_out = (x_float + scatter_tp(dot(yo, w_out))).astype(BF16)
        grad_xs, grad_bcdt, small = mixer_backward(
            width, zx, bcdt, pos, prm, head_prm, expand, mixed, g, states, dyo, coef
        )
        d_bc = grad_bcdt[:, : 2 * state_size]
        by_owner = jnp.moveaxis(d_bc.reshape(rows, 2, tp_count, own_cols), 2, 0)
        by_owner = by_owner.reshape(tp_count, rows, 2 * own_cols)
        d_bc_own = lax.psum_scatter(by_owner.astype(F32), "tp", scatter_dimension=0, tiled=False)
        d_rest = jnp.concatenate(
            [
                d_bc_own.astype(BF16),
                grad_bcdt[:, 2 * state_size : 2 * state_size + heads],
                jnp.zeros((rows, (-2 * own_cols - heads) % LANES), BF16),
            ],
            axis=1,
        )
        grad_w_x = scatter_dp(dot(gathered, grad_xs, CONTRACT_FIRST))
        grad_rest = scatter_dp(dot(gathered, d_rest, CONTRACT_FIRST))
        du_part = (
            dot(dz, w_z, CONTRACT_LAST) + dot(grad_xs, w_x, CONTRACT_LAST) + dot(grad_bcdt, w_bcdt)
        )
        gain_part = jnp.sum(du_part * gathered.astype(F32), axis=0) / norm_gain
        du = scatter_tp(du_part)
        e_in = du * norm_gain[None, :]
        grad_x = d_out.astype(F32) + r_in * e_in - x_float * (
            r_in**3 * jnp.mean(e_in * x_float, axis=-1, keepdims=True)
        )
        sums = lax.all_gather(lax.psum(small, "dp"), "tp")
        grad_norm_gain = lax.psum(gain_part, ("dp", "tp"))

    channels = jnp.swapaxes(sums[:, :7, :width], 0, 1).reshape(7, inner)
    shared = jnp.sum(sums[:, :5, width : width + 2 * state_size], axis=0)
    grad_conv = jnp.concatenate([channels[:5], shared], axis=1)
    return (
        block_out,
        grad_x,
        grad_norm_gain,
        grad_w_z,
        grad_w_x,
        grad_rest[:, :own_cols],
        grad_rest[:, own_cols : 2 * own_cols],
        grad_rest[:, 2 * own_cols : 2 * own_cols + heads],
        grad_conv[:4].T,
        grad_conv[4],
        sums[:, 7, :heads].reshape(-1),
        sums[:, 7, LANES : LANES + heads].reshape(-1),
        channels[6].reshape(heads * tp_count, head_size).sum(axis=1),
        channels[5],
        grad_w_out,
    )


def solution(mesh):
    rows = P(("dp", "tp"), None)
    columns = P(None, "tp")
    both = P("dp", "tp")
    none = P()
    return jax.shard_map(
        body,
        mesh=mesh,
        in_specs=(
            rows, none, columns, columns, columns, columns, columns, none, none, none, none, none, none,
            P("tp", None), P("dp", None), rows,
        ),
        out_specs=(
            rows, rows, none, both, both, both, both, both, none, none, none, none, none, none, P("tp", "dp"),
        ),
        check_vma=False,
    )
```

profile of v0, /device:TPU:0, one launch (start us, length us, event | category | flops | bytes accessed | tf_op | source)
XLA Modules:
  0.0 291.9 jit_solution(15767674852416152450)
XLA Ops:
  0.7 0.8 concatenate.10
  1.5 0.6 broadcast_in_dim.12.flat_ref
  2.1 1.8 maximum_bitcast_fusion.small_ref
  3.9 88.6 %shard_map.271 = (bf16[1024,2048]{1,0:T(8,128)(2,1)}, bf16[1024,2048]{1,0:T(8,128)(2,1)}, bf16[1024,384]{1,0:T(8,128)(2,1)}, bf16[384,2048]{1,0:T(8,128)(2,1)}, ...) custom-call(bf16[256,2048]{1,0:T(8,128)(2,1)} %x_ref.5, ...), custom_call_target="tpu_custom_call" | custom-call | tf_op jit(solution)/shard_map/pallas_call | solution.py:692
  92.5 54.5 %shard_map.272 = (bf16[256,2048]{1,0:T(8,128)(2,1)}, f32[1024,256]{1,0:T(8,128)}, bf16[1024,1024]{1,0:T(8,128)(2,1)}, bf16[8,1024,256]{2,1,0:T(8,128)(2,1)}) custom-call(bf16[256,2048]{1,0:T(8,128)(2,1)} %x_ref.5, bf16[1024,1024]{1,0:T(8,128)(2,1)} %get-tuple-element.44.yo_ref, bf16[1024,1024]{1,0:T(8,128)(2,1)} %get-tuple-element.45.yo_t_ref, ...), custom_call_target="tpu_custom_call" | custom-call | tf_op jit(solution)/shard_map/pallas_call | solution.py:1039
  147.0 60.4 %shard_map.273 = (f32[256,1024]{1,0:T(8,128)}, bf16[1024,1024]{1,0:T(8,128)(2,1)}, bf16[1024,384]{1,0:T(8,128)(2,1)}, bf16[8,1152,256]{2,1,0:T(8,128)(2,1)}, f32[8,1280]{1,0:T(8,128)}) custom-call(bf16[1024,2048]{1,0:T(8,128)(2,1)} %get-tuple-element.50.zx_ref, bf16[1024,384]{1,0:T(8,128)(2,1)} %get-tuple-element.55.bcdt_ref, ...), custom_call_target="tpu_custom_call" | custom-call | tf_op jit(solution)/shard_map/pallas_call | solution.py:1180
  207.4 0.0 copy-start.2
  207.4 67.1 %shard_map.274 = (f32[256,1024]{1,0:T(8,128)}, f32[256,128]{1,0:T(8,128)}, f32[256,2048]{1,0:T(8,128)}, f32[4,8,3328]{2,1,0:T(8,128)}) custom-call(bf16[256,2048]{1,0:T(8,128)(2,1)} %x_ref.5, bf16[256,2048]{1,0:T(8,128)(2,1)} %d_own_ref.3, f32[1,2048]{1,0:T(1,128)} %bitcast.15, f32[8,1280]{1,0:T(8,128)} %get-tuple-element.61.small_ref, ...), custom_call_target="tpu_custom_call" | custom-call | tf_op jit(solution)/shard_map/pallas_call | solution.py:1345
  274.5 0.0 copy-start
  274.5 0.9 slice_reduce_fusion.3
  275.4 0.6 reshape_squeeze.10
  276.0 0.6 reshape_squeeze.9
  276.6 0.8 slice_reduce_fusion
  277.4 1.6 slice_reduce_fusion.1
  278.9 0.9 slice_bitcast_fusion
  279.9 0.7 fusion.2
  280.5 0.6 fusion.3
  281.2 0.1 reshape_squeeze.11
  281.2 0.6 reduce_sum.29
  281.9 0.6 fusion.1
  282.5 1.0 slice.47
  283.5 0.7 copy.33
  284.2 1.1 fusion.4
  285.3 0.7 copy.32
  286.0 0.7 copy.31
  286.7 0.0 copy-done.2
  286.7 0.0 copy-start.3
  286.7 0.0 copy-start.4
  286.7 1.0 copy.39
  287.6 0.0 copy-done
  287.6 0.0 copy-start.1
  287.6 1.3 copy.40
  289.0 0.0 copy-done.3
  289.0 1.0 copy.41
  289.9 0.0 copy-done.4
  289.9 1.0 copy.42
  290.9 0.0 copy-done.1
  290.9 1.0 copy.43
  (1 shorter events, 0.0 us)
Async XLA Ops:
  207.4 79.3 %copy-start.2 = (bf16[256,2048]{1,0:T(8,128)(2,1)S(1)}, bf16[256,2048]{1,0:T(8,128)(2,1)}, u32[]{:S(2)}) copy-start(bf16[256,2048]{1,0:T(8,128)(2,1)} %get-tuple-element.109) | copy-start | bytes 3145732
  274.5 13.2 %copy-start = (f32[256,2048]{1,0:T(8,128)S(1)}, f32[256,2048]{1,0:T(8,128)}, u32[]{:S(2)}) copy-start(f32[256,2048]{1,0:T(8,128)} %get-tuple-element.110) | copy-start | bytes 6291460
  286.7 2.3 copy-start.3
  286.7 3.3 %copy-start.4 = (f32[256,1024]{1,0:T(8,128)S(1)}, f32[256,1024]{1,0:T(8,128)}, u32[]{:S(2)}) copy-start(f32[256,1024]{1,0:T(8,128)} %get-tuple-element.113) | copy-start | bytes 3145732
  287.6 3.3 %copy-start.1 = (f32[1024,256]{1,0:T(8,128)S(1)}, f32[1024,256]{1,0:T(8,128)}, u32[]{:S(2)}) copy-start(f32[1024,256]{1,0:T(8,128)} %get-tuple-element.123) | copy-start | bytes 3145732
where the time goes:
time: 292 us
  Pallas kernels  271 us (93%)
  local copies, waits for them, and re-layouts  14.5 us (5%)
  other arithmetic  6.03 us (2%)
    pallas_call x1, Pallas kernels, first_part(): pl.pallas_call(functools.partial(first_kernel, inner, heads, own_cols), o...  88.6 us
    pallas_call x1, Pallas kernels, fourth_part(): pl.pallas_call(fourth_kernel, out_shape=(jax.ShapeDtypeStruct((cut, width...  67.1 us
    pallas_call x1, Pallas kernels, third_part(): pl.pallas_call(functools.partial(third_kernel, own_cols, heads), out_shap...  60.4 us
    pallas_call x1, Pallas kernels, second_part(): pl.pallas_call(second_kernel, out_shape=(jax.ShapeDtypeStruct((rows, mode...  54.5 us
    unnamed x18, local copies, waits for them, and re-layouts  7.28 us

commit v1 on v0

--- a/solution.py
+++ b/solution.py
@@ -153,8 +153,8 @@
 
 
 def backward_chunk(
-    width, tokens, halo_x, halo_bc, held, zx_ref, bcdt_ref, pos_ref, prm_ref, head_ref, expand_ref, mixed_ref, g_ref,
-    dyo_ref, coef_ref, grad_x_ref, grad_bcdt_ref, grad_t_ref, small_ref, ext, d_state, later, later_pos,
+    width, tokens, halo_x, halo_bc, held, x_ref, bcdt_ref, pos_ref, prm_ref, head_ref, expand_ref, mixed_ref,
+    dy_ref, grad_x_ref, grad_bcdt_ref, grad_t_ref, small_ref, ext, d_state, later, later_pos,
 ):
     rows = CHUNK
     ext[:8, :width] = halo_x.astype(F32)[8:, :]
@@ -162,7 +162,7 @@
     pos = pos_ref[tokens, :]
     k = prepare_chunk(
         width,
-        zx_ref[tokens, width:],
+        x_ref[tokens, :],
         bcdt_ref[tokens, : 2 * LANES],
         bcdt_ref[tokens, 2 * LANES :],
         pos,
@@ -172,20 +172,13 @@
         ext,
     )
     xc = k["xc"]
-    z = zx_ref[tokens, :width].astype(F32)
-    r_col = coef_ref[tokens, 0:1]
-    back_col = coef_ref[tokens, 8:9]
-    g = g_ref[tokens, :]
-    dyo = dyo_ref[tokens, :].astype(F32)
     skip = prm_ref[6:7, :width]
     y = mixed_ref[tokens, :] - skip * xc
-    dg = r_col * (dyo * prm_ref[5:6, :width]) - g * back_col
-    dy = dg * (z * jax.nn.sigmoid(z))
-    small_ref[5:6, :width] += jnp.sum(dyo * g * r_col, axis=0, keepdims=True)
+    dy_low = dy_ref[tokens, :]
+    dy = dy_low.astype(F32)
     small_ref[6:7, :width] += jnp.sum(dy * xc, axis=0, keepdims=True)
 
     stepped = (xc * k["dt_w"]).astype(BF16)
-    dy_low = dy.astype(BF16)
     d_held = d_state[...]
     d_held_low = d_held.astype(BF16)
     held_low = held
@@ -218,25 +211,18 @@
         held_low.astype(F32) * d_held, axis=0, keepdims=True
     )
     gathered = two_parts(
-        jnp.concatenate(
-            [
-                d_stepped * xc,
-                dy_low.astype(F32) * y - stepped_f * d_stepped,
-                jnp.broadcast_to(tail_term, (8, width)),
-            ],
-            axis=0,
-        )
+        jnp.concatenate([dy * y - stepped_f * d_stepped, jnp.broadcast_to(tail_term, (8, width))], axis=0)
     )
     expand = expand_ref[:LANES, :]
     narrow = dot(gathered[:, :width], expand, CONTRACT_LAST) + dot(gathered[:, width:], expand, CONTRACT_LAST)
-    d_dt = narrow[:rows]
-    d_cum = narrow[rows : 2 * rows]
+    d_cum = narrow[:rows]
+    d_dt = dot((d_stepped * xc).astype(BF16), expand, CONTRACT_LAST)
     upper = (k["s_idx"] >= k["t_idx"]).astype(F32)
     d_decay = (
         lax.dot_general(
             upper, d_cum, (((1,), (0,)), ((), ())), precision=HIGHEST, preferred_element_type=F32
         )
-        + narrow[2 * rows : 2 * rows + 1]
+        + narrow[rows : rows + 1]
     )
     d_raw = (d_dt - d_decay * head_ref[1:2, :]) * jax.nn.sigmoid(k["raw"])
     small_ref[7:8, :LANES] += jnp.sum(d_raw, axis=0, keepdims=True)
@@ -248,15 +234,14 @@
     small_ref[4:5, :] += jnp.sum(d_pre, axis=0, keepdims=True)
     later[:rows, :] = d_pre
     later_pos[:rows, :] = jnp.broadcast_to(pos, (rows, LANES))
+    x_own = ext[8:, :]
     d_in = prm_ref[3:4, :] * d_pre
-    small_ref[3:4, :] += jnp.sum(d_pre * ext[8:, :], axis=0, keepdims=True)
+    small_ref[3:4, :] += jnp.sum(d_pre * x_own, axis=0, keepdims=True)
     for back in (1, 2, 3):
-        here = (pos >= back).astype(F32)
-        small_ref[3 - back : 4 - back, :] += jnp.sum(
-            d_pre * (ext[8 - back : 8 - back + rows, :] * here), axis=0, keepdims=True
-        )
         there = (later_pos[back : back + rows, 0:1] >= back).astype(F32)
-        d_in = d_in + prm_ref[3 - back : 4 - back, :] * (later[back : back + rows, :] * there)
+        reaching = later[back : back + rows, :] * there
+        small_ref[3 - back : 4 - back, :] += jnp.sum(reaching * x_own, axis=0, keepdims=True)
+        d_in = d_in + prm_ref[3 - back : 4 - back, :] * reaching
     grad_x_ref[tokens, :] = d_in[:, :width].astype(BF16)
     grad_bcdt_ref[tokens, : 2 * LANES] = d_in[:, width:].astype(BF16)
     later[rows:, :] = later[:8, :]
@@ -273,8 +258,8 @@
 
 
 def backward_kernel(
-    width, zx_ref, bcdt_ref, halo_x_ref, halo_bc_ref, pos_ref, prm_ref, head_ref,
-    expand_ref, mixed_ref, g_ref, state_ref, dyo_ref, coef_ref, grad_x_ref, grad_bcdt_ref, small_ref, ext, d_state,
+    width, x_ref, bcdt_ref, halo_x_ref, halo_bc_ref, pos_ref, prm_ref, head_ref,
+    expand_ref, mixed_ref, state_ref, dy_ref, grad_x_ref, grad_bcdt_ref, small_ref, ext, d_state,
     later, later_pos,
 ):
     @pl.when(pl.program_id(0) == 0)
@@ -282,8 +267,8 @@
         backward_start(small_ref, d_state, later, later_pos)
 
     backward_chunk(
-        width, slice(0, CHUNK), halo_x_ref[...], halo_bc_ref[:, : 2 * LANES], state_ref[0], zx_ref, bcdt_ref, pos_ref,
-        prm_ref, head_ref, expand_ref, mixed_ref, g_ref, dyo_ref, coef_ref, grad_x_ref, grad_bcdt_ref, None, small_ref,
+        width, slice(0, CHUNK), halo_x_ref[...], halo_bc_ref[:, : 2 * LANES], state_ref[0], x_ref, bcdt_ref, pos_ref,
+        prm_ref, head_ref, expand_ref, mixed_ref, dy_ref, grad_x_ref, grad_bcdt_ref, None, small_ref,
         ext, d_state, later, later_pos,
     )
 
@@ -324,7 +309,7 @@
     )(zx, bcdt, pos, prm, head_prm, expand)
 
 
-def mixer_backward(width, zx, bcdt, pos, prm, head_prm, expand, mixed, g, states, dyo, coef):
+def mixer_backward(width, zx, bcdt, pos, prm, head_prm, expand, mixed, states, dy):
     rows = zx.shape[0]
     chunks = rows // CHUNK
 
@@ -348,7 +333,7 @@
         ),
         grid=(chunks,),
         in_specs=[
-            tokens(2 * width),
+            pl.BlockSpec((CHUNK, width), lambda i: (chunks - 1 - i, 1)),
             tokens(3 * LANES),
             before(width, 1),
             before(3 * LANES, 0),
@@ -357,10 +342,8 @@
             whole(head_prm),
             whole(expand),
             tokens(width),
-            tokens(width),
             pl.BlockSpec((1, LANES, width), lambda i: (chunks - 1 - i, 0, 0)),
             tokens(width),
-            tokens(LANES),
         ],
         out_specs=(
             tokens(width),
@@ -377,7 +360,7 @@
             dimension_semantics=("arbitrary",), vmem_limit_bytes=48 * 1024 * 1024
         ),
         cost_estimate=pl.CostEstimate(flops=rows * width * 2048, bytes_accessed=rows * width * 20, transcendentals=0),
-    )(zx, bcdt, zx, bcdt, pos, prm, head_prm, expand, mixed, g, states, dyo, coef)
+    )(zx, bcdt, zx, bcdt, pos, prm, head_prm, expand, mixed, states, dy)
 
 
 MESH = pl.DeviceIdType.MESH
@@ -542,11 +525,11 @@
         piece = block(place)
 
         def tile(n, carry):
-            columns = pl.ds(pl.multiple_of(n * 256, 256), 256)
+            columns = pl.ds(pl.multiple_of(n * 512, 512), 512)
             zx[piece, columns] = dot(u[piece, :], weights[:, columns]).astype(BF16)
             return carry
 
-        lax.fori_loop(0, 2 * width // 256, tile, 0)
+        lax.fori_loop(0, 2 * width // 512, tile, 0)
 
     def project_small(place):
         bcdt[block(place), :] = dot(u[block(place), :], wbc[...], CONTRACT_LAST).astype(BF16)
@@ -923,19 +906,40 @@
 
 def second_kernel(
     x_ref, yo_ref, yo_t_ref, d_ref, w_out_ref, dyo_ref, g_ref, mixed_ref, zx_ref, coef_ref, prm_ref, u_ref,
-    block_out, gw_out, dz_out, gz_out,
+    block_out, gw_out, dz_out, dy_out, gz_out, gain_out,
     yo, yo_t, d, w_out, dyo, g, mixed, z, coef, own, gz,
     parts, pair, right, left, pair_sems, right_sems, left_sems,
     away, to_side, to_up, in_half, in_side, in_up, plane_sems, load_sems, store_sems,
 ):
     rows, model = x_ref.shape
     total, width = yo.shape
+    taken = parts.shape[1]
     me, side, up, far = tp_places()
     loads, stores = Copies(load_sems), Copies(store_sems)
     load_yo = loads.start(yo_ref, yo)
     load_w = loads.start(w_out_ref, w_out)
+    line = LineSum(parts, pair, right, left, pair_sems, right_sems, left_sems)
+    plane = PlaneSum(away, to_side, to_up, in_half, in_side, in_up, plane_sems)
+    greet([{"tp": side}, {"tp": up}] + line.peers())
+
+    def out_block(place, target):
+        piece = pl.ds(pl.multiple_of(place * rows, rows), rows)
+
+        def tile(n, carry):
+            columns = pl.ds(pl.multiple_of(n * 512, 512), 512)
+            target[:, columns] = dot(yo[piece, :], w_out[:, columns]).astype(target.dtype)
+            return carry
+
+        lax.fori_loop(0, model // 512, tile, 0)
+
+    load_yo.wait()
+    load_w.wait()
     load_yo_t = loads.start(yo_t_ref, yo_t)
     load_d = loads.start(d_ref, d)
+    out_block(far, away)
+    plane.start_far()
+    load_yo_t.wait()
+    load_d.wait()
     rest = [
         loads.start(dyo_ref, dyo),
         loads.start(g_ref, g),
@@ -943,75 +947,74 @@
         loads.start(zx_ref.at[:, :width], z),
         loads.start(coef_ref, coef),
     ]
-    line = LineSum(parts, pair, right, left, pair_sems, right_sems, left_sems)
-    plane = PlaneSum(away, to_side, to_up, in_half, in_side, in_up, plane_sems)
-    greet([{"tp": side}, {"tp": up}] + line.peers())
-
-    def out_block(place, target):
-        piece = pl.ds(pl.multiple_of(place * rows, rows), rows)
-
-        def tile(n, carry):
-            columns = pl.ds(pl.multiple_of(n * 256, 256), 256)
-            target[:, columns] = dot(yo[piece, :], w_out[:, columns]).astype(target.dtype)
-            return carry
-
-        lax.fori_loop(0, model // 256, tile, 0)
-
-    load_yo.wait()
-    load_w.wait()
-    out_block(far, away)
-    plane.start_far()
-    load_yo_t.wait()
-    load_d.wait()
-    for z_chunk in line.order():
+    order = line.order()
+
+    def products(z_chunk):
         for chunk in (2 * z_chunk + 1 - line.parity, 2 * z_chunk + line.parity):
-            product_chunk(yo_t, d, chunk, parts.at[chunk], width // 2)
+            product_chunk(yo_t, d, chunk, parts.at[chunk], taken // 2)
             if z_chunk not in line.swaps:
                 line.swap(z_chunk)
-    load_u = loads.start(u_ref, d)
-    order = line.order()
+
+    for z_chunk in order[:2]:
+        products(z_chunk)
     for z_chunk in order[:2]:
         line.merge(z_chunk)
     line.move(1)
+    for z_chunk in order[2:]:
+        products(z_chunk)
+
+    def left_over(chunk, carry):
+        columns = pl.ds(pl.multiple_of(chunk * parts.shape[2], parts.shape[2]), parts.shape[2])
+        gz[chunk, width:, :] = dot(yo_t[taken:, :], d[:, columns]).astype(BF16)
+        return carry
+
+    dp_count = parts.shape[0]
     for z_chunk in order[2:]:
         line.merge(z_chunk)
     out_block(side, to_side)
     plane.start_side()
     out_block(up, to_up)
     plane.start_up()
+    lax.fori_loop(0, dp_count, left_over, 0)
+    load_u = loads.start(u_ref, d)
+    line.move(2)
+    plane.pass_on()
     out_block(me, own)
     for copy in rest:
         copy.wait()
+    gain_out[...] = jnp.zeros_like(gain_out)
 
     def gate_back(i, carry):
         piece = pl.ds(pl.multiple_of(i * CHUNK, CHUNK), CHUNK)
         z_piece = z[piece, :].astype(F32)
         sig = jax.nn.sigmoid(z_piece)
-        dg = coef[piece, 0:1] * (dyo[piece, :].astype(F32) * prm_ref[5:6, :width]) - g[piece, :] * coef[piece, 8:9]
+        dyo_piece = dyo[piece, :].astype(F32)
+        g_piece = g[piece, :]
+        scaled = coef[piece, 0:1] * dyo_piece
+        dg = scaled * prm_ref[5:6, :width] - g_piece * coef[piece, 8:9]
+        gain_out[0:1, :] += jnp.sum(scaled * g_piece, axis=0, keepdims=True)
         dz = dg * mixed[piece, :] * (sig * (1.0 + z_piece * (1.0 - sig)))
         yo[piece, :] = dz.astype(BF16)
         yo_t[:, piece] = dz.T.astype(BF16)
+        dyo[piece, :] = (dg * (z_piece * sig)).astype(BF16)
         return carry
 
     chunks = total // CHUNK
     lax.fori_loop(0, chunks, gate_back, 0)
     stores.start(yo, dz_out)
-    line.move(2)
-    plane.pass_on()
-    load_u.wait()
-    dp_count = parts.shape[0]
-
-    def gate_products(first, last):
-        def one(chunk, carry):
-            product_chunk(yo_t, d, chunk, gz.at[chunk], width // 2)
-            return carry
-
-        lax.fori_loop(first, last, one, 0)
-
-    gate_products(0, dp_count)
-    stores.start(gz, gz_out)
+    stores.start(dyo, dy_out)
     for step in range(3, line.count):
         line.move(step)
+    load_u.wait()
+
+    def gate_products(chunk, carry):
+        product_chunk(yo_t, d, chunk, gz.at[chunk, :width], width // 2)
+        return carry
+
+    lax.fori_loop(0, dp_count, gate_products, 0)
+    stores.start(gz, gz_out)
+    sum_ref = line.finish()
+    gw_out[...] = sum_ref[...].astype(F32)
     plane.finish()
 
     def add_own(i, carry):
@@ -1021,8 +1024,6 @@
         return carry
 
     lax.fori_loop(0, rows // 32, add_own, 0)
-    sum_ref = line.finish()
-    gw_out[...] = sum_ref[...].astype(F32)
     line.end()
     plane.end()
     for copy in stores.started:
@@ -1034,18 +1035,21 @@
     total, width = yo.shape
     dp_count = lax.axis_size("dp")
     cut = model // dp_count
+    kept = width // 8
     vmem = pl.BlockSpec(memory_space=pltpu.VMEM)
     anywhere = pl.BlockSpec(memory_space=pl.ANY)
     return pl.pallas_call(
         second_kernel,
         out_shape=(
             jax.ShapeDtypeStruct((rows, model), BF16),
-            jax.ShapeDtypeStruct((width, cut), F32),
+            jax.ShapeDtypeStruct((width - kept, cut), F32),
             jax.ShapeDtypeStruct((total, width), BF16),
-            jax.ShapeDtypeStruct((dp_count, width, cut), BF16),
+            jax.ShapeDtypeStruct((total, width), BF16),
+            jax.ShapeDtypeStruct((dp_count, width + kept, cut), BF16),
+            jax.ShapeDtypeStruct((8, width), F32),
         ),
         in_specs=[vmem] + [anywhere] * 9 + [vmem, anywhere],
-        out_specs=(vmem, vmem, anywhere, anywhere),
+        out_specs=(vmem, vmem, anywhere, anywhere, anywhere, vmem),
         scratch_shapes=[
             pltpu.VMEM((total, width), BF16),
             pltpu.VMEM((width, total), BF16),
@@ -1057,11 +1061,11 @@
             pltpu.VMEM((total, width), BF16),
             pltpu.VMEM((total, LANES), F32),
             pltpu.VMEM((rows, model), F32),
-            pltpu.VMEM((dp_count, width, cut), BF16),
+            pltpu.VMEM((dp_count, width + kept, cut), BF16),
         ]
-        + line_scratch(dp_count, (width, cut))
+        + line_scratch(dp_count, (width - kept, cut))
         + plane_scratch(rows, model)
-        + [pltpu.SemaphoreType.DMA((10,)), pltpu.SemaphoreType.DMA((2,))],
+        + [pltpu.SemaphoreType.DMA((10,)), pltpu.SemaphoreType.DMA((3,))],
         compiler_params=pltpu.CompilerParams(
             collective_id=1, has_side_effects=True, vmem_limit_bytes=60 * 1024 * 1024
         ),
@@ -1069,10 +1073,10 @@
 
 
 def third_kernel(
-    own_cols, heads, zx_ref, bcdt_ref, pos_ref, prm_ref, head_ref, expand_ref, mixed_ref, g_ref, state_ref, dyo_ref,
-    coef_ref, u_ref, gz_ref,
-    gw_z, dx_out, dbcdt_out, gl_out, small_out,
-    zx, bcdt, mixed, g, states, dyo, u, dx, dbcdt, dx_t, gl, bc_in, ext, d_state, later, later_pos,
+    own_cols, heads, zx_ref, bcdt_ref, pos_ref, prm_ref, head_ref, expand_ref, mixed_ref, state_ref, dy_ref,
+    u_ref, gz_ref,
+    gw_z, gw_last, dx_out, dbcdt_out, gl_out, small_out,
+    x, bcdt, mixed, states, dy, u, dx, dbcdt, dx_t, gl, bc_in, ext, d_state, later, later_pos,
     parts, pair, right, left, pair_sems, right_sems, left_sems, bc_sems, load_sems, store_sems,
 ):
     total, width = mixed.shape
@@ -1081,38 +1085,44 @@
     dp_count = parts.shape[0]
     loads, stores = Copies(load_sems), Copies(store_sems)
     load_parts = loads.start(gz_ref, parts)
-    first_loads = [
-        loads.start(zx_ref, zx),
-        loads.start(bcdt_ref, bcdt),
-        loads.start(mixed_ref, mixed),
-        loads.start(g_ref, g),
-        loads.start(state_ref, states),
-        loads.start(dyo_ref, dyo),
-    ]
-    load_u = loads.start(u_ref, u)
     line = LineSum(parts, pair, right, left, pair_sems, right_sems, left_sems)
     greet([{"tp": side}, {"tp": up}, {"tp": far}] + line.peers())
     load_parts.wait()
     order = line.order()
     for z_chunk in order:
         line.swap(z_chunk)
+    halves_of_loads = []
+    for first in (total // 2, 0):
+        piece = pl.ds(first, total // 2)
+        pieces = pl.ds(first // CHUNK, chunks // 2)
+        halves_of_loads.append(
+            [
+                loads.start(zx_ref.at[piece, width:], x.at[piece]),
+                loads.start(bcdt_ref.at[piece], bcdt.at[piece]),
+                loads.start(mixed_ref.at[piece], mixed.at[piece]),
+                loads.start(state_ref.at[pieces], states.at[pieces]),
+                loads.start(dy_ref.at[piece], dy.at[piece]),
+            ]
+        )
+    load_u = loads.start(u_ref, u)
     backward_start(small_out, d_state, later, later_pos)
     for z_chunk in order[:2]:
         line.merge(z_chunk)
     line.move(1)
     for z_chunk in order[2:]:
         line.merge(z_chunk)
-    for copy in first_loads:
-        copy.wait()
-    hooks = {3: 2, 6: 3}
+    for copies in halves_of_loads:
+        for copy in copies:
+            copy.wait()
+    hooks = {3: 2, 7: 3}
 
     def chunk(i, carry):
         at = chunks - 1 - i
         tokens = pl.ds(pl.multiple_of(at * CHUNK, CHUNK), CHUNK)
         halo = pl.ds(pl.multiple_of(lax.rem(at * CHUNK + total - 16, total), 16), 16)
         backward_chunk(
-            width, tokens, zx[halo, width:], bcdt[halo, : 2 * LANES], states[at], zx, bcdt, pos_ref, prm_ref, head_ref,
-            expand_ref, mixed, g, dyo, coef_ref, dx, dbcdt, dx_t, small_out, ext, d_state, later, later_pos,
+            width, tokens, x[halo, :], bcdt[halo, : 2 * LANES], states[at], x, bcdt, pos_ref, prm_ref, head_ref,
+            expand_ref, mixed, dy, dx, dbcdt, dx_t, small_out, ext, d_state, later, later_pos,
         )
         for when, step in hooks.items():
 
@@ -1145,17 +1155,24 @@
         BF16
     )
     load_u.wait()
+
+    def x_product(c, carry):
+        product_chunk(dx_t, u, c, gl.at[c, :width], width // 2)
+        return carry
+
+    lax.fori_loop(0, dp_count, x_product, 0)
     for copy in copies:
         copy.wait()
     for n in range(3):
         own_bc = own_bc + bc_in[3 + n].astype(F32)
     dx_t[width : width + 2 * own_cols, :] = own_bc.astype(BF16)
 
-    def last_product(c, carry):
-        product_chunk(dx_t, u, c, gl.at[c], (width + LANES) // 3)
+    def bc_product(c, carry):
+        columns = pl.ds(pl.multiple_of(c * gl.shape[2], gl.shape[2]), gl.shape[2])
+        gl[c, width:, :] = dot(dx_t[width:, :], u[:, columns]).astype(BF16)
         return carry
 
-    lax.fori_loop(0, dp_count, last_product, 0)
+    lax.fori_loop(0, dp_count, bc_product, 0)
     stores.start(gl, gl_out)
     sum_ref = line.finish()
 
@@ -1165,12 +1182,13 @@
         return carry
 
     lax.fori_loop(0, width // CHUNK, turn, 0)
+    gw_last[...] = sum_ref[width:, :].astype(F32)
     line.end()
     for copy in stores.started:
         copy.wait()
 
 
-def third_part(own_cols, heads, zx, bcdt, pos, prm, head_prm, expand, mixed, g, states, dyo, coef, u, gz):
+def third_part(own_cols, heads, zx, bcdt, pos, prm, head_prm, expand, mixed, states, dy, u, gz):
     total, width = mixed.shape
     model = u.shape[1]
     dp_count = lax.axis_size("dp")
@@ -1181,17 +1199,17 @@
         functools.partial(third_kernel, own_cols, heads),
         out_shape=(
             jax.ShapeDtypeStruct((cut, width), F32),
+            jax.ShapeDtypeStruct((gz.shape[1] - width, cut), F32),
             jax.ShapeDtypeStruct((total, width), BF16),
             jax.ShapeDtypeStruct((total, 3 * LANES), BF16),
             jax.ShapeDtypeStruct((dp_count, width + LANES, cut), BF16),
             jax.ShapeDtypeStruct((8, width + 2 * LANES), F32),
         ),
-        in_specs=[anywhere] * 2 + [vmem] * 4 + [anywhere] * 4 + [vmem] + [anywhere] * 2,
-        out_specs=(vmem, anywhere, anywhere, anywhere, vmem),
+        in_specs=[anywhere] * 2 + [vmem] * 4 + [anywhere] * 5,
+        out_specs=(vmem, vmem, anywhere, anywhere, anywhere, vmem),
         scratch_shapes=[
-            pltpu.VMEM(zx.shape, BF16),
+            pltpu.VMEM((total, width), BF16),
             pltpu.VMEM(bcdt.shape, BF16),
-            pltpu.VMEM((total, width), F32),
             pltpu.VMEM((total, width), F32),
             pltpu.VMEM(states.shape, BF16),
             pltpu.VMEM((total, width), BF16),
@@ -1206,16 +1224,17 @@
             pltpu.VMEM((CHUNK + 8, width + 2 * LANES), F32),
             pltpu.VMEM((CHUNK + 8, LANES), jnp.int32),
         ]
-        + line_scratch(dp_count, (width, cut))
-        + [pltpu.SemaphoreType.DMA((2, 3)), pltpu.SemaphoreType.DMA((8,)), pltpu.SemaphoreType.DMA((3,))],
+        + line_scratch(dp_count, gz.shape[1:])
+        + [pltpu.SemaphoreType.DMA((2, 3)), pltpu.SemaphoreType.DMA((12,)), pltpu.SemaphoreType.DMA((3,))],
         compiler_params=pltpu.CompilerParams(
             collective_id=2, has_side_effects=True, vmem_limit_bytes=60 * 1024 * 1024
         ),
-    )(zx, bcdt, pos, prm, head_prm, expand, mixed, g, states, dyo, coef, u, gz)
+    )(zx, bcdt, pos, prm, head_prm, expand, mixed, states, dy, u, gz)
 
 
 def fourth_kernel(
-    x_ref, d_own_ref, gain_ref, small_ref, dz_ref, dx_ref, dbcdt_ref, wz_ref, wx_ref, wbc_ref, u_ref, gl_ref,
+    heads, x_ref, d_own_ref, gain_ref, small_ref, gain_sum_ref, expand_ref, dz_ref, dx_ref, dbcdt_ref, wz_ref, wx_ref,
+    wbc_ref, u_ref, gl_ref,
     gw_x, gw_rest, grad_x, sums,
     dz, dx, dbcdt, wz, wx, wbc, u, own, gain_part, packed, over_z,
     parts, pair, right, left, pair_sems, right_sems, left_sems,
@@ -1227,15 +1246,6 @@
     dp_count = parts.shape[0]
     loads = Copies(load_sems)
     load_parts = loads.start(gl_ref, parts)
-    first_loads = [
-        loads.start(dz_ref, dz),
-        loads.start(dx_ref, dx),
-        loads.start(dbcdt_ref, dbcdt),
-        loads.start(wz_ref, wz),
-        loads.start(wx_ref, wx),
-        loads.start(wbc_ref, wbc),
-        loads.start(u_ref, u),
-    ]
     line = LineSum(parts, pair, right, left, pair_sems, right_sems, left_sems)
     plane = PlaneSum(away, to_side, to_up, in_half, in_side, in_up, plane_sems)
     others = [{"dp": lax.rem(line.dp + 2 * n, dp_count)} for n in range(1, dp_count // 2)]
@@ -1244,13 +1254,23 @@
     order = line.order()
     for z_chunk in order:
         line.swap(z_chunk)
+    loads_of = {}
+    weights = [loads.start(wz_ref, wz), loads.start(wx_ref, wx), loads.start(wbc_ref, wbc)]
+    for name, place in (("far", far), ("side", side), ("up", up), ("me", me)):
+        piece = pl.ds(pl.multiple_of(place * rows, rows), rows)
+        loads_of[name] = [
+            loads.start(source.at[piece], target.at[piece])
+            for source, target in ((dz_ref, dz), (dx_ref, dx), (dbcdt_ref, dbcdt), (u_ref, u))
+        ]
     gain_part[...] = jnp.zeros_like(gain_part)
 
-    def du_block(place, target):
+    def du_block(name, place, target):
+        for copy in loads_of[name]:
+            copy.wait()
         piece = pl.ds(pl.multiple_of(place * rows, rows), rows)
 
         def tile(n, carry):
-            columns = pl.ds(pl.multiple_of(n * 256, 256), 256)
+            columns = pl.ds(pl.multiple_of(n * 512, 512), 512)
             du = (
                 dot(dz[piece, :], wz[columns, :], CONTRACT_LAST)
                 + dot(dx[piece, :], wx[columns, :], CONTRACT_LAST)
@@ -1260,30 +1280,46 @@
             gain_part[0:1, columns] += jnp.sum(du * u[piece, columns].astype(F32), axis=0, keepdims=True)
             return carry
 
-        lax.fori_loop(0, model // 256, tile, 0)
-
-    for copy in first_loads:
-        copy.wait()
-    du_block(far, away)
-    plane.start_far()
+        lax.fori_loop(0, model // 512, tile, 0)
+
     for z_chunk in order[:2]:
         line.merge(z_chunk)
     line.move(1)
+    for copy in weights:
+        copy.wait()
+    du_block("far", far, away)
+    plane.start_far()
     for z_chunk in order[2:]:
         line.merge(z_chunk)
-    du_block(side, to_side)
+    du_block("side", side, to_side)
     plane.start_side()
-    du_block(up, to_up)
+    du_block("up", up, to_up)
     plane.start_up()
-    du_block(me, own)
+    line.move(2)
+    du_block("me", me, own)
+    plane.pass_on()
 
     wide = width + 2 * LANES
+    shift = (
+        lax.broadcasted_iota(jnp.int32, (LANES, LANES), 1)
+        == lax.broadcasted_iota(jnp.int32, (LANES, LANES), 0) + me * heads
+    ).astype(F32)
+    shift = jnp.where(lax.broadcasted_iota(jnp.int32, (LANES, LANES), 0) < heads, shift, 0.0)
+    skip_rows = two_parts(jnp.broadcast_to(small_ref[6:7, :width], (8, width)))
+    expand = expand_ref[:LANES, :]
+    per_head = dot(skip_rows[:, :width], expand, CONTRACT_LAST) + dot(skip_rows[:, width:], expand, CONTRACT_LAST)
+    tiles = jnp.concatenate([small_ref[:, :LANES], small_ref[:, LANES : 2 * LANES], per_head], axis=0)
+    placed = lax.dot_general(
+        tiles, shift, (((1,), (0,)), ((), ())), precision=HIGHEST, preferred_element_type=F32
+    )
     packed[0, :, :wide] = small_ref[...]
+    packed[0, 5:6, :width] = gain_sum_ref[0:1, :]
+    packed[0, 6:7, width : width + LANES] = placed[16:17]
+    packed[0, 7:8, :LANES] = placed[7:8]
+    packed[0, 7:8, LANES : 2 * LANES] = placed[15:16]
     packed[0, :, wide:] = jnp.concatenate([gain_part[0:1, :] / gain_ref[...], jnp.zeros((7, model), F32)], axis=0)
     trade = send(packed.at[0], packed.at[1], z_sems.at[0, 0], z_sems.at[1, 0], line.partner)
     trade.start()
-    plane.pass_on()
-    line.move(2)
     trade.wait()
     over_z[0] = packed[0] + packed[1]
     copies = [
@@ -1292,6 +1328,8 @@
     ]
     for copy in copies:
         copy.start()
+    for step in range(3, line.count):
+        line.move(step)
     for copy in copies:
         copy.wait()
     everything = over_z[0]
@@ -1304,8 +1342,6 @@
     ]
     for copy in copies:
         copy.start()
-    for step in range(3, line.count):
-        line.move(step)
     plane.finish()
 
     def norm_back(i, carry):
@@ -1329,12 +1365,12 @@
         return carry
 
     lax.fori_loop(0, width // CHUNK, turn, 0)
-    gw_rest[...] = sum_ref[width:, :].astype(F32).T
+    gw_rest[...] = sum_ref[width:, :].astype(F32)
     line.end()
     plane.end()
 
 
-def fourth_part(x_in, d_out, gain, small, dz, dx, dbcdt, w_z, w_x, wbc, u, gl):
+def fourth_part(heads, x_in, d_out, gain, small, gain_sum, expand, dz, dx, dbcdt, w_z, w_x, wbc, u, gl):
     rows, model = x_in.shape
     total, width = dz.shape
     dp_count = lax.axis_size("dp")
@@ -1343,14 +1379,14 @@
     vmem = pl.BlockSpec(memory_space=pltpu.VMEM)
     anywhere = pl.BlockSpec(memory_space=pl.ANY)
     return pl.pallas_call(
-        fourth_kernel,
+        functools.partial(fourth_kernel, heads),
         out_shape=(
             jax.ShapeDtypeStruct((cut, width), F32),
-            jax.ShapeDtypeStruct((cut, LANES), F32),
+            jax.ShapeDtypeStruct((LANES, cut), F32),
             jax.ShapeDtypeStruct((rows, model), F32),
             jax.ShapeDtypeStruct((4, 8, wide), F32),
         ),
-        in_specs=[vmem] * 4 + [anywhere] * 8,
+        in_specs=[vmem] * 6 + [anywhere] * 8,
         out_specs=(vmem,) * 4,
         scratch_shapes=[
             pltpu.VMEM((total, width), BF16),
@@ -1370,12 +1406,93 @@
         + [
             pltpu.SemaphoreType.DMA((2, dp_count // 2)),
             pltpu.SemaphoreType.DMA((2, 3)),
-            pltpu.SemaphoreType.DMA((8,)),
+            pltpu.SemaphoreType.DMA((20,)),
         ],
         compiler_params=pltpu.CompilerParams(
             collective_id=3, has_side_effects=True, vmem_limit_bytes=60 * 1024 * 1024
         ),
-    )(x_in, d_out, gain, small, dz, dx, dbcdt, w_z, w_x, wbc, u, gl)
+    )(x_in, d_out, gain, small, gain_sum, expand, dz, dx, dbcdt, w_z, w_x, wbc, u, gl)
+
+
+def results_kernel(
+    own_cols, heads, block_ref, grad_x_ref, first_ref, last_ref, z_ref, x_ref, rest_ref, sums_ref,
+    block_out, grad_x, gw_z, gw_x, gw_b, gw_c, gw_dt, gw_out, conv_w, conv_b, gate, norm, dt_bias, a_log, skip,
+    held_block, held_grad_x, held_z, held_x, held_first, held_last, load_sems, sems,
+):
+    taken = first_ref.shape[0]
+    loads, copies = Copies(load_sems), Copies(sems)
+    held = (held_block, held_grad_x, held_z, held_x, held_first, held_last)
+    targets = (block_out, grad_x, gw_z, gw_x, gw_out.at[:taken], gw_out.at[taken:])
+    for source, target in zip((block_ref, grad_x_ref, z_ref, x_ref, first_ref, last_ref), held):
+        loads.start(source, target)
+    for load, source, target in zip(loads.started, held, targets):
+        load.wait()
+        copies.start(source, target)
+    width = z_ref.shape[1]
+    count = sums_ref.shape[0]
+    inner = gate.shape[1]
+    wide = width + 2 * LANES
+    gw_b[...] = rest_ref[:own_cols, :]
+    gw_c[...] = rest_ref[own_cols : 2 * own_cols, :]
+    gw_dt[...] = rest_ref[2 * own_cols : 2 * own_cols + heads, :]
+
+    def over_tp(rows, columns):
+        total = sums_ref[0, rows, columns]
+        for n in range(1, count):
+            total = total + sums_ref[n, rows, columns]
+        return total
+
+    for n in range(count):
+        own = slice(n * width, (n + 1) * width)
+        conv_w[:, own] = sums_ref[n, 0:4, :width]
+        conv_b[:, own] = sums_ref[n, 4:5, :width]
+        gate[:, own] = sums_ref[n, 5:6, :width]
+    conv_w[:, inner:] = over_tp(slice(0, 4), slice(width, wide))
+    conv_b[:, inner:] = over_tp(slice(4, 5), slice(width, wide))
+    norm[...] = over_tp(slice(0, 1), slice(wide, None))
+    total_heads = dt_bias.shape[1]
+    dt_bias[...] = over_tp(slice(7, 8), slice(0, LANES))[:, :total_heads]
+    a_log[...] = over_tp(slice(7, 8), slice(LANES, 2 * LANES))[:, :total_heads]
+    skip[...] = over_tp(slice(6, 7), slice(width, width + LANES))[:, :total_heads]
+    for copy in copies.started:
+        copy.wait()
+
+
+def results_part(own_cols, heads, block_out, grad_x, first, last, gw_z, gw_x, rest, sums):
+    cut, width = gw_z.shape
+    count = sums.shape[0]
+    inner = width * count
+    model = grad_x.shape[1]
+    vmem = pl.BlockSpec(memory_space=pltpu.VMEM)
+    anywhere = pl.BlockSpec(memory_space=pl.ANY)
+    shapes = [
+        ((own_cols, cut), F32),
+        ((own_cols, cut), F32),
+        ((heads, cut), F32),
+        ((first.shape[0] + last.shape[0], cut), F32),
+        ((4, inner + 2 * LANES), F32),
+        ((1, inner + 2 * LANES), F32),
+        ((1, inner), F32),
+        ((1, model), F32),
+        ((1, heads * count), F32),
+        ((1, heads * count), F32),
+        ((1, heads * count), F32),
+    ]
+    return pl.pallas_call(
+        functools.partial(results_kernel, own_cols, heads),
+        out_shape=[
+            jax.ShapeDtypeStruct(block_out.shape, BF16),
+            jax.ShapeDtypeStruct(grad_x.shape, F32),
+            jax.ShapeDtypeStruct(gw_z.shape, F32),
+            jax.ShapeDtypeStruct(gw_x.shape, F32),
+        ]
+        + [jax.ShapeDtypeStruct(*shape) for shape in shapes],
+        in_specs=[anywhere] * 6 + [vmem] * 2,
+        out_specs=[anywhere] * 4 + [vmem] * 3 + [anywhere] + [vmem] * 7,
+        scratch_shapes=[pltpu.VMEM(large.shape, large.dtype) for large in (block_out, grad_x, gw_z, gw_x, first, last)]
+        + [pltpu.SemaphoreType.DMA((6,)), pltpu.SemaphoreType.DMA((6,))],
+        compiler_params=pltpu.CompilerParams(vmem_limit_bytes=60 * 1024 * 1024),
+    )(block_out, grad_x, first, last, gw_z, gw_x, rest, sums)
 
 
 def in_norm_scale(values):
@@ -1471,16 +1588,26 @@
         yo = (g * r_gate[:, None] * gain_own[None, :]).astype(BF16)
 
     if tp_count == 4:
-        block_out, grad_w_out, dz, gz = second_part(
+        block_out, gw_first, dz, dy, gz, gain_sum = second_part(
             x_in, yo, yo_t, grad_gathered, w_out, dyo, g, mixed, zx, coef, prm, gathered
         )
-        grad_w_z, grad_xs, grad_bcdt, gl, small = third_part(
-            own_cols, heads, zx, bcdt, pos, prm, head_prm, expand, mixed, g, states, dyo, coef, gathered, gz
-        )
-        grad_w_x, grad_rest, grad_x, sums = fourth_part(
-            x_in, d_out, norm_gain[None, :], small, dz, grad_xs, grad_bcdt, w_z, w_x, w_bcdt, gathered, gl
-        )
-        grad_norm_gain = jnp.sum(sums[:, 0, width + 2 * state_size :], axis=0)
+        gw_z, gw_last, grad_xs, grad_bcdt, gl, small = third_part(
+            own_cols, heads, zx, bcdt, pos, prm, head_prm, expand, mixed, states, dy, gathered, gz
+        )
+        gw_x, gw_rest, grad_x, sums = fourth_part(
+            heads, x_in, d_out, norm_gain[None, :], small, gain_sum, expand, dz, grad_xs, grad_bcdt, w_z, w_x, w_bcdt,
+            gathered, gl
+        )
+        (
+            block_out, grad_x, gw_z, gw_x, gw_b, gw_c, gw_dt, gw_out, g_conv_w, g_conv_b, g_gate, g_norm, g_dt_bias,
+            g_a_log, g_skip
+        ) = results_part(
+            own_cols, heads, block_out, grad_x, gw_first, gw_last, gw_z, gw_x, gw_rest, sums
+        )
+        return (
+            block_out, grad_x, g_norm[0], gw_z, gw_x, gw_b.T, gw_c.T, gw_dt.T, g_conv_w.T, g_conv_b[0], g_dt_bias[0],
+            g_a_log[0], g_skip[0], g_gate[0], gw_out
+        )
     else:
 
         def scatter_dp(partial):
@@ -1494,11 +1621,14 @@
         sig_z = jax.nn.sigmoid(z)
         dg = coef[:, 0:1] * (dyo.astype(F32) * gain_own[None, :]) - g * coef[:, 8:9]
         dz = (dg * mixed * (sig_z * (1.0 + z * (1.0 - sig_z)))).astype(BF16)
+        dy = (dg * (z * sig_z)).astype(BF16)
+        gain_sum = jnp.sum(dyo.astype(F32) * g * coef[:, 0:1], axis=0)
         grad_w_z = scatter_dp(dot(gathered, dz, CONTRACT_FIRST))
         block_out = (x_float + scatter_tp(dot(yo, w_out))).astype(BF16)
         grad_xs, grad_bcdt, small = mixer_backward(
-            width, zx, bcdt, pos, prm, head_prm, expand, mixed, g, states, dyo, coef
-        )
+            width, zx, bcdt, pos, prm, head_prm, expand, mixed, states, dy
+        )
+        small = small.at[5, :width].set(gain_sum)
         d_bc = grad_bcdt[:, : 2 * state_size]
         by_owner = jnp.moveaxis(d_bc.reshape(rows, 2, tp_count, own_cols), 2, 0)
         by_owner = by_owner.reshape(tp_count, rows, 2 * own_cols)

time: 292 us -> 263 us (0.901)
  Pallas kernels: 271 us -> 257 us
  local copies, waits for them, and re-layouts: 14.5 us -> 1.46 us
    pallas_call x1, Pallas kernels: 60.4 us -> 52.7 us  [third_part(): pl.pallas_call(functools.partial(third_kernel, own_cols, heads), out_shap...]
    unnamed x18 -> x0, local copies, waits for them, and re-layouts: 7.28 us -> none
    pallas_call x1, Pallas kernels: 54.5 us -> 49.9 us  [second_part(): pl.pallas_call(second_kernel, out_shape=(jax.ShapeDtypeStruct((rows, mode...]
    slice x4 -> x0, local copies, waits for them, and re-layouts: 3.6 us -> none  [the longest x1 1.07 us: body(): grad_rest[:, own_cols:2 * own_cols]]
    reduce_sum x3 -> x0, other arithmetic: 2.97 us -> none  [the longest x1 1.58 us: body(): grad_norm_gain = jnp.sum(sums[:, 0, width + 2 * state_size:], axis=0)]
    pallas_call x1 -> x2, Pallas kernels: 67.1 us -> 65.9 us  [the longest x1 59.3 us: fourth_part(): pl.pallas_call(functools.partial(fourth_kernel, heads), out_shape=(jax.Sh...]
where the time goes in v1:
time: 263 us; the launch traced here: 262 us
  Pallas kernels  257 us (98%)
  other arithmetic  3.12 us (1%)
    pallas_call x1, Pallas kernels, first_part(): pl.pallas_call(functools.partial(first_kernel, inner, heads, own_cols), o...  88.7 us
    pallas_call x1, Pallas kernels, fourth_part(): pl.pallas_call(functools.partial(fourth_kernel, heads), out_shape=(jax.Sh...  59.3 us
    pallas_call x1, Pallas kernels, third_part(): pl.pallas_call(functools.partial(third_kernel, own_cols, heads), out_shap...  52.7 us
    pallas_call x1, Pallas kernels, second_part(): pl.pallas_call(second_kernel, out_shape=(jax.ShapeDtypeStruct((rows, mode...  49.9 us
    pallas_call x1, Pallas kernels, results_part(): pl.pallas_call(functools.partial(results_kernel, own_cols, heads), out_sh...  6.59 us

profile of v1, /device:TPU:0, one launch (start us, length us, event | category | flops | bytes accessed | tf_op | source)
XLA Modules:
  0.0 262.4 jit_solution(10104396823697353794)
XLA Ops:
  0.7 0.8 concatenate.7
  1.5 0.6 broadcast_in_dim.12.flat_ref
  2.1 1.8 maximum_bitcast_fusion.small_ref
  3.9 88.7 %shard_map.271 = (bf16[1024,2048]{1,0:T(8,128)(2,1)}, bf16[1024,2048]{1,0:T(8,128)(2,1)}, bf16[1024,384]{1,0:T(8,128)(2,1)}, bf16[384,2048]{1,0:T(8,128)(2,1)}, ...) custom-call(bf16[256,2048]{1,0:T(8,128)(2,1)} %x_ref.5, ...), custom_call_target="tpu_custom_call" | custom-call | tf_op jit(solution)/shard_map/pallas_call | solution.py:675
  92.6 49.9 %shard_map.272 = (bf16[256,2048]{1,0:T(8,128)(2,1)}, f32[896,256]{1,0:T(8,128)}, bf16[1024,1024]{1,0:T(8,128)(2,1)}, bf16[1024,1024]{1,0:T(8,128)(2,1)}, bf16[8,...) custom-call(bf16[256,2048]{1,0:T(8,128)(2,1)} %x_ref.5, bf16[1024,1024]{1,0:T(8,128)(2,1)} %get-tuple-element.62.yo_ref, ...), custom_call_target="tpu_custom_call" | custom-call | tf_op jit(solution)/shard_map/pallas_call | solution.py:1041
  142.4 52.7 %shard_map.273 = (f32[256,1024]{1,0:T(8,128)}, f32[128,256]{1,0:T(8,128)}, bf16[1024,1024]{1,0:T(8,128)(2,1)}, bf16[1024,384]{1,0:T(8,128)(2,1)}, bf16[8,1152,256]{2,1,0:T(8,128)(2,1)}, /*index=5*/f32[8,1280]{1,0:T(8,128)}) custom-call(bf16[1024,2048]{1,0:T(8,128)(2,1)} %get-tuple-element.68.zx_ref, bf16[1024,384]{1,0:T(8,128)(2,1)} %get-tuple-element.73.bcdt_ref, ...), custom_call_target="tpu_custom_call" | custom-call | tf_op jit(solution)/shard_map/pallas_call | solution.py:1198
  195.1 59.3 %shard_map.274 = (f32[256,1024]{1,0:T(8,128)}, f32[128,256]{1,0:T(8,128)}, f32[256,2048]{1,0:T(8,128)}, f32[4,8,3328]{2,1,0:T(8,128)}) custom-call(bf16[256,2048]{1,0:T(8,128)(2,1)} %x_ref.5, bf16[256,2048]{1,0:T(8,128)(2,1)} %d_own_ref.3, f32[1,2048]{1,0:T(1,128)} %bitcast.15, f32[8,1280]{1,0:T(8,128)} %get-tuple-element.80.small_ref, ...), custom_call_target="tpu_custom_call" | custom-call | tf_op jit(solution)/shard_map/pallas_call | solution.py:1381
  254.5 6.6 %shard_map.275 = (bf16[256,2048]{1,0:T(8,128)(2,1)}, f32[256,2048]{1,0:T(8,128)}, f32[256,1024]{1,0:T(8,128)}, f32[256,1024]{1,0:T(8,128)}, f32[32,256]{1,0:T(8,...) custom-call(bf16[256,2048]{1,0:T(8,128)(2,1)} %get-tuple-element.72., ...), custom_call_target="tpu_custom_call" | custom-call | tf_op jit(solution)/shard_map/pallas_call | solution.py:1481
  261.1 1.4 reduce
  (1 shorter events, 0.0 us)

commit v2 on v1

--- a/solution.py
+++ b/solution.py
@@ -389,35 +389,46 @@
         me, side, up, _ = tp_places()
         half = rows // 2
 
-        def part(place, start, count):
-            return whole.at[pl.ds(pl.multiple_of(place * rows + start, half), count)]
-
-        own = part(me, 0, rows) if own is None else own
-        self.to_side = send(own, part(me, 0, rows), send_sems.at[0], recv_sems.at[0], {"tp": side})
-        self.to_up = send(own, part(me, 0, rows), send_sems.at[1], recv_sems.at[1], {"tp": up})
-        self.pass_up = send(
-            part(side, 0, half), part(side, 0, half), send_sems.at[2], recv_sems.at[2], {"tp": up}
-        )
-        self.pass_side = send(
-            part(up, half, half), part(up, half, half), send_sems.at[3], recv_sems.at[3], {"tp": side}
-        )
+        def part(place, which):
+            return whole.at[pl.ds(pl.multiple_of(place * rows + which * half, half), half)]
+
+        def one(n, place, which, peer):
+            return send(part(place, which), part(place, which), send_sems.at[n], recv_sems.at[n], {"tp": peer})
+
+        def quarter(n, which, late, peer):
+            start = pl.multiple_of(me * rows + which * half + late * (half // 2), half // 2)
+            piece = whole.at[pl.ds(start, half // 2)]
+            return send(piece, piece, send_sems.at[n], recv_sems.at[n], {"tp": peer})
+
+        self.side_first, self.up_first = one(0, me, 0, side), one(1, me, 1, up)
+        self.side_then = [quarter(2, 1, 0, side), quarter(3, 1, 1, side)]
+        self.up_then = [quarter(4, 0, 0, up), quarter(5, 0, 1, up)]
+        self.pass_up, self.pass_side = one(6, side, 0, up), one(7, up, 1, side)
 
     def start(self):
-        self.to_side.start()
-        self.to_up.start()
+        for copy in (self.side_first, self.up_first, self.side_then[0], self.up_then[0]):
+            copy.start()
+
+    def start_rest(self):
+        self.side_then[1].start()
+        self.up_then[1].start()
 
     def forward(self):
-        self.to_side.wait_recv()
+        self.side_first.wait_recv()
         self.pass_up.start()
-        self.to_up.wait_recv()
+        self.up_first.wait_recv()
         self.pass_side.start()
+
+    def neighbours(self):
+        for copy in self.side_then + self.up_then:
+            copy.wait_recv()
 
     def finish(self):
         self.pass_up.wait_recv()
         self.pass_side.wait_recv()
 
     def end(self):
-        for copy in (self.to_side, self.to_up, self.pass_up, self.pass_side):
+        for copy in [self.side_first, self.up_first, self.pass_up, self.pass_side] + self.side_then + self.up_then:
             copy.wait_send()
 
 
@@ -463,7 +474,7 @@
 def first_kernel(
     inner, heads, own_cols, x_ref, gain_ref, small_ref, taps_ref, flat_ref, lens_ref, wz_ref, wx_ref, w_out_ref, d_own_ref,
     u_out, zx_out, bcdt_out, wbc_out, mixed_out, g_out, yo_out, yo_t_out, state_out, d_out, dyo_out, coef_out, pos_out,
-    prm_out, head_out, expand_out,
+    prm_out, head_out, expand_out, cross_out,
     weights, w_out, u, zx, bcdt, wbc, mixed, g, yo, yo_t, states, d, dyo, coef, pos, prm, head, expand, ext, state, sums,
     acc, sems, sum_sems, load_sems, store_sems,
 ):
@@ -500,6 +511,7 @@
     greet([{"tp": side}, {"tp": up}, {"tp": far}, partner])
     small_gather = Gather(wbc.at[bc_own], own_cols, sems.at[0], sems.at[1])
     small_gather.start()
+    small_gather.start_rest()
 
     def norm(i, carry):
         piece = pl.ds(pl.multiple_of(i * 32, 32), 32)
@@ -509,8 +521,10 @@
         return carry
 
     lax.fori_loop(0, rows // 32, norm, 0)
+    small_gather.forward()
     gather = Gather(u, rows, sems.at[2], sems.at[3])
     gather.start()
+    gather.start_rest()
     wbc[2 * LANES :, :] = jnp.zeros((LANES, model), BF16)
     wbc[2 * LANES : 2 * LANES + heads, :] = small_ref[2 * own_cols :, :]
     set_up(width, heads, inner, taps_ref, flat_ref, lens_ref, prm, head, expand, pos)
@@ -534,23 +548,24 @@
     def project_small(place):
         bcdt[block(place), :] = dot(u[block(place), :], wbc[...], CONTRACT_LAST).astype(BF16)
 
-    small_gather.forward()
     project(me)
+    small_gather.neighbours()
     small_gather.finish()
     trade = send(wbc.at[bc_own], wbc.at[bc_own], sems.at[6, 0], sems.at[6, 1], partner)
     trade.start()
     gather.forward()
-    project(side)
-    project(up)
+    loads[3].wait()
+    d_gather = Gather(d, rows, sems.at[4], sems.at[5])
+    d_gather.start()
     trade.wait()
     keep(wbc, wbc_out)
     project_small(me)
+    gather.neighbours()
+    project(side)
+    project(up)
     project_small(side)
     project_small(up)
     gather.finish()
-    loads[3].wait()
-    d_gather = Gather(d, rows, sems.at[4], sems.at[5])
-    d_gather.start()
     keep(u, u_out)
     project(far)
     project_small(far)
@@ -562,24 +577,19 @@
 
     def chunk(i, carry):
         forward_chunk(
-            width, i, zx, bcdt, pos, prm, head, expand, mixed, g, sums.at[0, 0], states, ext, state
+            width, i, zx, bcdt, pos, prm, head, expand, mixed, g, sums.at[0], states, ext, state
         )
         return carry
 
     lax.fori_loop(0, chunks, chunk, 0)
 
-    def exchange(which):
-        copies = [
-            send(
-                sums.at[which, 0], sums.at[which, 1 + n], sum_sems.at[which, 0, n], sum_sems.at[which, 1, n], {"tp": peer}
-            )
-            for n, peer in enumerate((side, up, far))
-        ]
-        for copy in copies:
-            copy.start()
-        return copies
-
-    copies = exchange(0)
+    copies = [
+        send(sums.at[0], sums.at[2 + n], sum_sems.at[0, n], sum_sems.at[1, n], {"tp": peer})
+        for n, peer in enumerate((side, up, far))
+    ]
+    for copy in copies:
+        copy.start()
+    d_gather.start_rest()
     keep(mixed, mixed_out)
     keep(g, g_out)
     keep(states, state_out)
@@ -599,7 +609,7 @@
 
         lax.fori_loop(0, width // 256, tile, 0)
         column = jnp.sum(acc[...], axis=1, keepdims=True)
-        sums[1, 0, :, piece] = jnp.broadcast_to(column, (rows, LANES)).T[:8, :]
+        sums[1, :, piece] = jnp.broadcast_to(column, (rows, LANES)).T[:8, :]
         keep(dyo.at[piece], dyo_out.at[piece])
 
     d_gather.forward()
@@ -609,37 +619,26 @@
 
     def gate(i, carry):
         piece = pl.ds(pl.multiple_of(i * CHUNK, CHUNK), CHUNK)
-        squares = sums[0, 0, :, piece] + sums[0, 1, :, piece] + sums[0, 2, :, piece] + sums[0, 3, :, piece]
+        squares = sums[0, :, piece] + sums[2, :, piece] + sums[3, :, piece] + sums[4, :, piece]
         scale = lax.rsqrt(squares / inner + EPSILON)
         columns = jnp.concatenate([scale, jnp.zeros((LANES - 8, LANES), F32)], axis=0).T
+        coef[piece, :] = columns
         gated = g[piece, :] * columns[:, 0:1] * prm[5:6, :width]
         yo[piece, :] = gated.astype(BF16)
         yo_t[:, piece] = gated.T.astype(BF16)
         return carry
 
     lax.fori_loop(0, chunks, gate, 0)
+    keep(coef, coef_out)
     keep(yo, yo_out)
     keep(yo_t, yo_t_out)
+    d_gather.neighbours()
     back_to_heads(side)
     back_to_heads(up)
     d_gather.finish()
     keep(d, d_out)
     back_to_heads(far)
-    copies = exchange(1)
-    for copy in copies:
-        copy.wait()
-
-    def weigh(i, carry):
-        piece = pl.ds(pl.multiple_of(i * CHUNK, CHUNK), CHUNK)
-        squares = sums[0, 0, :, piece] + sums[0, 1, :, piece] + sums[0, 2, :, piece] + sums[0, 3, :, piece]
-        cross = sums[1, 0, :, piece] + sums[1, 1, :, piece] + sums[1, 2, :, piece] + sums[1, 3, :, piece]
-        scale = lax.rsqrt(squares / inner + EPSILON)
-        back = scale * scale * scale * (cross / inner)
-        coef[piece, :] = jnp.concatenate([scale, back, jnp.zeros((LANES - 16, LANES), F32)], axis=0).T
-        return carry
-
-    lax.fori_loop(0, chunks, weigh, 0)
-    keep(coef, coef_out)
+    keep(sums.at[1], cross_out)
     small_gather.end()
     gather.end()
     d_gather.end()
@@ -672,20 +671,21 @@
         ((8, LANES), F32),
         ((2 * LANES, width), BF16),
     ]
+    cross = jax.ShapeDtypeStruct((8, total), F32)
     return pl.pallas_call(
         functools.partial(first_kernel, inner, heads, own_cols),
-        out_shape=[jax.ShapeDtypeStruct(*result) for result in results],
+        out_shape=[jax.ShapeDtypeStruct(*result) for result in results] + [cross],
         in_specs=[vmem] * 5 + [pl.BlockSpec(memory_space=pltpu.SMEM)] + [anywhere] * 4,
-        out_specs=[anywhere] * len(results),
+        out_specs=[anywhere] * (len(results) + 1),
         scratch_shapes=[pltpu.VMEM((model, 2 * width), BF16), pltpu.VMEM((width, model), BF16)]
         + [pltpu.VMEM(*result) for result in results]
         + [
             pltpu.VMEM((CHUNK + 8, width + 2 * LANES), F32),
             pltpu.VMEM((LANES, width), F32),
-            pltpu.VMEM((2, 4, 8, total), F32),
+            pltpu.VMEM((5, 8, total), F32),
             pltpu.VMEM((rows, LANES), F32),
-            pltpu.SemaphoreType.DMA((7, 4)),
-            pltpu.SemaphoreType.DMA((2, 2, 3)),
+            pltpu.SemaphoreType.DMA((7, 8)),
+            pltpu.SemaphoreType.DMA((2, 3)),
             pltpu.SemaphoreType.DMA((4,)),
             pltpu.SemaphoreType.DMA((24,)),
         ],
@@ -696,105 +696,117 @@
 
 
 def add_into(target, other):
-    tile = 128
+    rows = target.shape[0]
+    tile = max(t for t in range(16, 257, 16) if rows % t == 0)
 
     def one(i, carry):
         piece = pl.ds(pl.multiple_of(i * tile, tile), tile)
         target[piece, :] = (target[piece, :].astype(F32) + other[piece, :].astype(F32)).astype(BF16)
         return carry
 
-    lax.fori_loop(0, target.shape[0] // tile, one, 0)
+    lax.fori_loop(0, rows // tile, one, 0)
+
+
+def line_order(count):
+    low, high, out = 0, count - 1, []
+    while low <= high:
+        out += [high, low] if low < high else [low]
+        low, high = low + 1, high - 1
+    return out
+
+
+class PairSum:
+    def __init__(self, parts, pair, sems):
+        dp = lax.axis_index("dp")
+        self.parity = lax.rem(dp, 2)
+        self.partner = {"dp": dp + 1 - 2 * self.parity}
+        self.parts, self.pair, self.sems, self.swaps = parts, pair, sems, {}
+
+    def theirs(self, z):
+        return 2 * z + 1 - self.parity
+
+    def ours(self, z):
+        return 2 * z + self.parity
+
+    def swap(self, z):
+        copy = send(
+            self.parts.at[self.theirs(z)], self.pair.at[z], self.sems.at[0, z], self.sems.at[1, z], self.partner
+        )
+        copy.start()
+        self.swaps[z] = copy
+
+    def merge(self, z):
+        self.swaps[z].wait()
+        add_into(self.parts.at[self.ours(z)], self.pair.at[z])
 
 
 class LineSum:
-    def __init__(self, parts, pair, right, left, pair_sems, right_sems, left_sems):
+    def __init__(self, parts, at, right, left, right_sems, left_sems):
         dp = lax.axis_index("dp")
         self.dp = dp
-        self.count = parts.shape[0] // 2
+        self.count = lax.axis_size("dp") // 2
         self.z = dp // 2
-        self.parity = lax.rem(dp, 2)
-        self.partner = {"dp": dp + 1 - 2 * self.parity}
-        self.parts, self.pair = parts, pair
+        self.parts, self.at = parts, at
         self.lines = {1: (right, right_sems), -1: (left, left_sems)}
-        self.swaps = {}
-        self.pair_sems = pair_sems
 
     def peers(self):
         n = 2 * self.count
-        return [self.partner, {"dp": lax.rem(self.dp + 2, n)}, {"dp": lax.rem(self.dp + n - 2, n)}]
-
-    def order(self):
-        low, high, out = 0, self.count - 1, []
-        while low <= high:
-            out += [high, low] if low < high else [low]
-            low, high = low + 1, high - 1
-        return out
-
-    def swap(self, z):
-        copy = send(
-            self.parts.at[2 * z + 1 - self.parity], self.pair.at[z], self.pair_sems.at[0, z], self.pair_sems.at[1, z],
-            self.partner,
-        )
-        copy.start()
-        self.swaps[z] = copy
-
-    def merge(self, z):
-        self.swaps[z].wait()
-        add_into(self.parts.at[2 * z + self.parity], self.pair.at[z])
+        return [{"dp": lax.rem(self.dp + 2, n)}, {"dp": lax.rem(self.dp + n - 2, n)}]
 
     def away(self, way):
         return self.z if way == 1 else self.count - 1 - self.z
 
-    def copy(self, way, step):
+    def copies(self, way, step):
         line, line_sems = self.lines[way]
         far = self.count - step + self.away(way)
         z = far if way == 1 else self.count - 1 - far
-        chunk = self.parts.at[2 * z + self.parity]
-        return chunk, send(
-            chunk, line.at[step - 1], line_sems.at[0, step - 1], line_sems.at[1, step - 1],
-            {"dp": self.dp + 2 * way},
-        )
-
-    def arrived(self, way, step):
+        chunk = self.parts.at[self.at(z)]
+        return lambda piece: self.piece(chunk, line, line_sems, step, piece, {"dp": self.dp + 2 * way})
+
+    def piece(self, chunk, line, line_sems, step, piece, peer):
+        half = chunk.shape[0] // 2
+        rows = pl.ds(piece * half, half)
+        copy = send(
+            chunk.at[rows], line.at[step - 1, rows], line_sems.at[0, step - 1, piece], line_sems.at[1, step - 1, piece],
+            peer,
+        )
+        return chunk.at[rows], copy
+
+    def add_arrived(self, way, step, piece, target):
         line, line_sems = self.lines[way]
-        return send(
-            self.parts.at[self.dp], line.at[step - 1], line_sems.at[0, step - 1], line_sems.at[1, step - 1],
-            self.partner,
-        )
-
-    def move(self, step):
+        chunk = self.parts.at[self.at(self.z)]
+        self.piece(chunk, line, line_sems, step, piece, self.peers()[0])[1].wait_recv()
+        half = chunk.shape[0] // 2
+        add_into(target, line.at[step - 1, pl.ds(piece * half, half)])
+
+    def lead(self, *steps):
+        for way in (1, -1):
+
+            @pl.when(self.away(way) == 0)
+            def _():
+                for step in steps:
+                    for piece in range(2):
+                        self.copies(way, step)(piece)[1].start()
+
+    def relay(self, step, piece):
         for way in (1, -1):
             away = self.away(way)
 
-            @pl.when(away == 0)
+            @pl.when((away >= 1) & (away <= min(step - 1, self.count - 2)))
             def _():
-                if step > 1:
-                    self.copy(way, step - 1)[1].wait_send()
-                self.copy(way, step)[1].start()
-
-            if step > 1:
-
-                @pl.when((away >= 1) & (away <= min(step - 1, self.count - 2)))
+                chunk, copy = self.copies(way, step)(piece)
+                self.add_arrived(way, step - 1, piece, chunk)
+                copy.start()
+
+    def finish(self):
+        total = self.parts.at[self.at(self.z)]
+        half = total.shape[0] // 2
+        for piece in range(2):
+            for way in (1, -1):
+
+                @pl.when(self.away(way) >= 1)
                 def _():
-                    chunk, copy = self.copy(way, step)
-                    self.arrived(way, step - 1).wait_recv()
-                    add_into(chunk, self.lines[way][0].at[step - 2])
-                    copy.start()
-
-    def finish(self):
-        last = self.count - 1
-        for way in (1, -1):
-
-            @pl.when(self.away(way) >= 1)
-            def _():
-                self.arrived(way, last).wait_recv()
-
-        total = self.parts.at[self.dp]
-        for way in (1, -1):
-
-            @pl.when(self.away(way) >= 1)
-            def _():
-                add_into(total, self.lines[way][0].at[last - 1])
+                    self.add_arrived(way, self.count - 1, piece, total.at[pl.ds(piece * half, half)])
 
         return total
 
@@ -803,9 +815,10 @@
             away = self.away(way)
             for step in range(1, self.count):
 
-                @pl.when((away <= step - 1) & (away <= self.count - 2) & ((away >= 1) | (step == self.count - 1)))
+                @pl.when(away <= min(step - 1, self.count - 2))
                 def _():
-                    self.copy(way, step)[1].wait_send()
+                    for piece in range(2):
+                        self.copies(way, step)(piece)[1].wait_send()
 
 
 class PlaneSum:
@@ -869,16 +882,20 @@
     ]
 
 
+def pair_scratch(dp_count, shape):
+    return [
+        pltpu.VMEM((dp_count // 2,) + shape, BF16),
+        pltpu.SemaphoreType.DMA((2, dp_count // 2)),
+    ]
+
+
 def line_scratch(dp_count, shape):
-    z = dp_count // 2
+    steps = dp_count // 2 - 1
     return [
-        pltpu.VMEM((dp_count,) + shape, BF16),
-        pltpu.VMEM((z,) + shape, BF16),
-        pltpu.VMEM((z - 1,) + shape, BF16),
-        pltpu.VMEM((z - 1,) + shape, BF16),
-        pltpu.SemaphoreType.DMA((2, z)),
-        pltpu.SemaphoreType.DMA((2, z - 1)),
-        pltpu.SemaphoreType.DMA((2, z - 1)),
+        pltpu.VMEM((steps,) + shape, BF16),
+        pltpu.VMEM((steps,) + shape, BF16),
+        pltpu.SemaphoreType.DMA((2, steps, 2)),
+        pltpu.SemaphoreType.DMA((2, steps, 2)),
     ]
 
 
@@ -905,11 +922,11 @@
 
 
 def second_kernel(
-    x_ref, yo_ref, yo_t_ref, d_ref, w_out_ref, dyo_ref, g_ref, mixed_ref, zx_ref, coef_ref, prm_ref, u_ref,
-    block_out, gw_out, dz_out, dy_out, gz_out, gain_out,
-    yo, yo_t, d, w_out, dyo, g, mixed, z, coef, own, gz,
-    parts, pair, right, left, pair_sems, right_sems, left_sems,
-    away, to_side, to_up, in_half, in_side, in_up, plane_sems, load_sems, store_sems,
+    inner, x_ref, cross_ref, yo_ref, yo_t_ref, d_ref, w_out_ref, dyo_ref, g_ref, mixed_ref, zx_ref, coef_ref, prm_ref,
+    u_ref, block_out, gw_out, dz_out, dy_out, gz_out, gain_out,
+    yo, yo_t, d, w_out, dyo, g, mixed, z, coef, own, gz, parts, pair, pair_sems, gz_pair, gz_pair_sems,
+    right, left, right_sems, left_sems,
+    away, to_side, to_up, in_half, in_side, in_up, plane_sems, cross, cross_sems, load_sems, store_sems,
 ):
     rows, model = x_ref.shape
     total, width = yo.shape
@@ -918,9 +935,17 @@
     loads, stores = Copies(load_sems), Copies(store_sems)
     load_yo = loads.start(yo_ref, yo)
     load_w = loads.start(w_out_ref, w_out)
-    line = LineSum(parts, pair, right, left, pair_sems, right_sems, left_sems)
+    cores = PairSum(parts, pair, pair_sems)
+    gz_cores = PairSum(gz, gz_pair, gz_pair_sems)
+    line = LineSum(parts, cores.ours, right, left, right_sems, left_sems)
     plane = PlaneSum(away, to_side, to_up, in_half, in_side, in_up, plane_sems)
-    greet([{"tp": side}, {"tp": up}] + line.peers())
+    greet([{"tp": side}, {"tp": up}, {"tp": far}, cores.partner] + line.peers())
+    crossing = [
+        send(cross_ref, cross.at[n], cross_sems.at[0, n], cross_sems.at[1, n], {"tp": peer})
+        for n, peer in enumerate((side, up, far))
+    ]
+    for copy in crossing:
+        copy.start()
 
     def out_block(place, target):
         piece = pl.ds(pl.multiple_of(place * rows, rows), rows)
@@ -947,19 +972,18 @@
         loads.start(zx_ref.at[:, :width], z),
         loads.start(coef_ref, coef),
     ]
-    order = line.order()
+    order = line_order(line.count)
 
     def products(z_chunk):
-        for chunk in (2 * z_chunk + 1 - line.parity, 2 * z_chunk + line.parity):
-            product_chunk(yo_t, d, chunk, parts.at[chunk], taken // 2)
-            if z_chunk not in line.swaps:
-                line.swap(z_chunk)
+        product_chunk(yo_t, d, cores.theirs(z_chunk), parts.at[cores.theirs(z_chunk)], taken // 2)
+        cores.swap(z_chunk)
+        product_chunk(yo_t, d, cores.ours(z_chunk), parts.at[cores.ours(z_chunk)], taken // 2)
 
     for z_chunk in order[:2]:
         products(z_chunk)
     for z_chunk in order[:2]:
-        line.merge(z_chunk)
-    line.move(1)
+        cores.merge(z_chunk)
+    line.lead(1)
     for z_chunk in order[2:]:
         products(z_chunk)
 
@@ -968,30 +992,37 @@
         gz[chunk, width:, :] = dot(yo_t[taken:, :], d[:, columns]).astype(BF16)
         return carry
 
-    dp_count = parts.shape[0]
     for z_chunk in order[2:]:
-        line.merge(z_chunk)
+        cores.merge(z_chunk)
+    line.lead(*range(2, line.count))
     out_block(side, to_side)
     plane.start_side()
     out_block(up, to_up)
     plane.start_up()
-    lax.fori_loop(0, dp_count, left_over, 0)
+    line.relay(2, 0)
+    plane.pass_on()
+    lax.fori_loop(0, parts.shape[0], left_over, 0)
     load_u = loads.start(u_ref, d)
-    line.move(2)
-    plane.pass_on()
     out_block(me, own)
+    line.relay(2, 1)
     for copy in rest:
         copy.wait()
+    for copy in crossing:
+        copy.wait()
     gain_out[...] = jnp.zeros_like(gain_out)
 
     def gate_back(i, carry):
         piece = pl.ds(pl.multiple_of(i * CHUNK, CHUNK), CHUNK)
+        crossed = cross_ref[:, piece] + cross[0, :, piece] + cross[1, :, piece] + cross[2, :, piece]
+        crossed = jnp.concatenate([crossed, jnp.zeros((LANES - 8, LANES), F32)], axis=0).T[:, 0:1]
+        scale = coef[piece, 0:1]
+        back = scale * scale * scale * (crossed / inner)
         z_piece = z[piece, :].astype(F32)
         sig = jax.nn.sigmoid(z_piece)
         dyo_piece = dyo[piece, :].astype(F32)
         g_piece = g[piece, :]
-        scaled = coef[piece, 0:1] * dyo_piece
-        dg = scaled * prm_ref[5:6, :width] - g_piece * coef[piece, 8:9]
+        scaled = scale * dyo_piece
+        dg = scaled * prm_ref[5:6, :width] - g_piece * back
         gain_out[0:1, :] += jnp.sum(scaled * g_piece, axis=0, keepdims=True)
         dz = dg * mixed[piece, :] * (sig * (1.0 + z_piece * (1.0 - sig)))
         yo[piece, :] = dz.astype(BF16)
@@ -1004,17 +1035,23 @@
     stores.start(yo, dz_out)
     stores.start(dyo, dy_out)
     for step in range(3, line.count):
-        line.move(step)
+        line.relay(step, 0)
     load_u.wait()
 
-    def gate_products(chunk, carry):
+    def gate_product(chunk):
         product_chunk(yo_t, d, chunk, gz.at[chunk, :width], width // 2)
-        return carry
-
-    lax.fori_loop(0, dp_count, gate_products, 0)
-    stores.start(gz, gz_out)
+
+    for z_chunk in order:
+        gate_product(gz_cores.theirs(z_chunk))
+        gz_cores.swap(z_chunk)
+    for step in range(3, line.count):
+        line.relay(step, 1)
+    for z_chunk in order:
+        gate_product(gz_cores.ours(z_chunk))
+        gz_cores.merge(z_chunk)
+        stores.start(gz.at[gz_cores.ours(z_chunk)], gz_out.at[z_chunk])
     sum_ref = line.finish()
-    gw_out[...] = sum_ref[...].astype(F32)
+    gw_out[...] = sum_ref[...]
     plane.finish()
 
     def add_own(i, carry):
@@ -1030,7 +1067,7 @@
         copy.wait()
 
 
-def second_part(x_in, yo, yo_t, d, w_out, dyo, g, mixed, zx, coef, prm, u):
+def second_part(inner, x_in, cross, yo, yo_t, d, w_out, dyo, g, mixed, zx, coef, prm, u):
     rows, model = x_in.shape
     total, width = yo.shape
     dp_count = lax.axis_size("dp")
@@ -1039,16 +1076,16 @@
     vmem = pl.BlockSpec(memory_space=pltpu.VMEM)
     anywhere = pl.BlockSpec(memory_space=pl.ANY)
     return pl.pallas_call(
-        second_kernel,
+        functools.partial(second_kernel, inner),
         out_shape=(
             jax.ShapeDtypeStruct((rows, model), BF16),
-            jax.ShapeDtypeStruct((width - kept, cut), F32),
+            jax.ShapeDtypeStruct((width - kept, cut), BF16),
             jax.ShapeDtypeStruct((total, width), BF16),
             jax.ShapeDtypeStruct((total, width), BF16),
-            jax.ShapeDtypeStruct((dp_count, width + kept, cut), BF16),
+            jax.ShapeDtypeStruct((dp_count // 2, width + kept, cut), BF16),
             jax.ShapeDtypeStruct((8, width), F32),
         ),
-        in_specs=[vmem] + [anywhere] * 9 + [vmem, anywhere],
+        in_specs=[vmem] * 2 + [anywhere] * 9 + [vmem, anywhere],
         out_specs=(vmem, vmem, anywhere, anywhere, anywhere, vmem),
         scratch_shapes=[
             pltpu.VMEM((total, width), BF16),
@@ -1062,35 +1099,39 @@
             pltpu.VMEM((total, LANES), F32),
             pltpu.VMEM((rows, model), F32),
             pltpu.VMEM((dp_count, width + kept, cut), BF16),
+            pltpu.VMEM((dp_count, width - kept, cut), BF16),
         ]
+        + pair_scratch(dp_count, (width - kept, cut))
+        + pair_scratch(dp_count, (width + kept, cut))
         + line_scratch(dp_count, (width - kept, cut))
         + plane_scratch(rows, model)
-        + [pltpu.SemaphoreType.DMA((10,)), pltpu.SemaphoreType.DMA((3,))],
+        + [
+            pltpu.VMEM((3, 8, total), F32),
+            pltpu.SemaphoreType.DMA((2, 3)),
+            pltpu.SemaphoreType.DMA((10,)),
+            pltpu.SemaphoreType.DMA((2 + dp_count // 2,)),
+        ],
         compiler_params=pltpu.CompilerParams(
             collective_id=1, has_side_effects=True, vmem_limit_bytes=60 * 1024 * 1024
         ),
-    )(x_in, yo, yo_t, d, w_out, dyo, g, mixed, zx, coef, prm, u)
+    )(x_in, cross, yo, yo_t, d, w_out, dyo, g, mixed, zx, coef, prm, u)
 
 
 def third_kernel(
     own_cols, heads, zx_ref, bcdt_ref, pos_ref, prm_ref, head_ref, expand_ref, mixed_ref, state_ref, dy_ref,
     u_ref, gz_ref,
-    gw_z, gw_last, dx_out, dbcdt_out, gl_out, small_out,
+    gw_z, dx_out, dbcdt_out, gl_out, small_out,
     x, bcdt, mixed, states, dy, u, dx, dbcdt, dx_t, gl, bc_in, ext, d_state, later, later_pos,
-    parts, pair, right, left, pair_sems, right_sems, left_sems, bc_sems, load_sems, store_sems,
+    pair, pair_sems, parts, right, left, right_sems, left_sems, bc_sems, load_sems, store_sems,
 ):
     total, width = mixed.shape
     chunks = total // CHUNK
     me, side, up, far = tp_places()
-    dp_count = parts.shape[0]
     loads, stores = Copies(load_sems), Copies(store_sems)
     load_parts = loads.start(gz_ref, parts)
-    line = LineSum(parts, pair, right, left, pair_sems, right_sems, left_sems)
-    greet([{"tp": side}, {"tp": up}, {"tp": far}] + line.peers())
-    load_parts.wait()
-    order = line.order()
-    for z_chunk in order:
-        line.swap(z_chunk)
+    cores = PairSum(gl, pair, pair_sems)
+    line = LineSum(parts, lambda z: z, right, left, right_sems, left_sems)
+    order = line_order(line.count)
     halves_of_loads = []
     for first in (total // 2, 0):
         piece = pl.ds(first, total // 2)
@@ -1105,16 +1146,14 @@
             ]
         )
     load_u = loads.start(u_ref, u)
+    greet([{"tp": side}, {"tp": up}, {"tp": far}, cores.partner] + line.peers())
     backward_start(small_out, d_state, later, later_pos)
-    for z_chunk in order[:2]:
-        line.merge(z_chunk)
-    line.move(1)
-    for z_chunk in order[2:]:
-        line.merge(z_chunk)
+    load_parts.wait()
+    line.lead(*range(1, line.count))
     for copies in halves_of_loads:
         for copy in copies:
             copy.wait()
-    hooks = {3: 2, 7: 3}
+    hooks = {3: (2, 0), 5: (2, 1), 7: (3, 0), chunks: (3, 1)}
 
     def chunk(i, carry):
         at = chunks - 1 - i
@@ -1124,11 +1163,11 @@
             width, tokens, x[halo, :], bcdt[halo, : 2 * LANES], states[at], x, bcdt, pos_ref, prm_ref, head_ref,
             expand_ref, mixed, dy, dx, dbcdt, dx_t, small_out, ext, d_state, later, later_pos,
         )
-        for when, step in hooks.items():
+        for when, turn in hooks.items():
 
             @pl.when(i == when - 1)
             def _():
-                line.move(step)
+                line.relay(*turn)
 
         return carry
 
@@ -1156,33 +1195,33 @@
     )
     load_u.wait()
 
-    def x_product(c, carry):
-        product_chunk(dx_t, u, c, gl.at[c, :width], width // 2)
-        return carry
-
-    lax.fori_loop(0, dp_count, x_product, 0)
+    def x_product(chunk):
+        product_chunk(dx_t, u, chunk, gl.at[chunk, :width], width // 2)
+
+    def bc_product(chunk):
+        columns = pl.ds(pl.multiple_of(chunk * gl.shape[2], gl.shape[2]), gl.shape[2])
+        gl[chunk, width:, :] = dot(dx_t[width:, :], u[:, columns]).astype(BF16)
+
+    for z_chunk in order[:2]:
+        x_product(cores.theirs(z_chunk))
     for copy in copies:
         copy.wait()
     for n in range(3):
         own_bc = own_bc + bc_in[3 + n].astype(F32)
     dx_t[width : width + 2 * own_cols, :] = own_bc.astype(BF16)
-
-    def bc_product(c, carry):
-        columns = pl.ds(pl.multiple_of(c * gl.shape[2], gl.shape[2]), gl.shape[2])
-        gl[c, width:, :] = dot(dx_t[width:, :], u[:, columns]).astype(BF16)
-        return carry
-
-    lax.fori_loop(0, dp_count, bc_product, 0)
-    stores.start(gl, gl_out)
+    for z_chunk in order:
+        if z_chunk not in order[:2]:
+            x_product(cores.theirs(z_chunk))
+        bc_product(cores.theirs(z_chunk))
+        cores.swap(z_chunk)
+    for z_chunk in order:
+        x_product(cores.ours(z_chunk))
+        bc_product(cores.ours(z_chunk))
+        cores.merge(z_chunk)
+        stores.start(gl.at[cores.ours(z_chunk)], gl_out.at[z_chunk])
     sum_ref = line.finish()
 
-    def turn(i, carry):
-        piece = pl.ds(pl.multiple_of(i * CHUNK, CHUNK), CHUNK)
-        gw_z[:, piece] = sum_ref[piece, :].astype(F32).T
-        return carry
-
-    lax.fori_loop(0, width // CHUNK, turn, 0)
-    gw_last[...] = sum_ref[width:, :].astype(F32)
+    gw_z[...] = sum_ref[...]
     line.end()
     for copy in stores.started:
         copy.wait()
@@ -1198,15 +1237,14 @@
     return pl.pallas_call(
         functools.partial(third_kernel, own_cols, heads),
         out_shape=(
-            jax.ShapeDtypeStruct((cut, width), F32),
-            jax.ShapeDtypeStruct((gz.shape[1] - width, cut), F32),
+            jax.ShapeDtypeStruct(gz.shape[1:], BF16),
             jax.ShapeDtypeStruct((total, width), BF16),
             jax.ShapeDtypeStruct((total, 3 * LANES), BF16),
-            jax.ShapeDtypeStruct((dp_count, width + LANES, cut), BF16),
+            jax.ShapeDtypeStruct((dp_count // 2, width + LANES, cut), BF16),
             jax.ShapeDtypeStruct((8, width + 2 * LANES), F32),
         ),
         in_specs=[anywhere] * 2 + [vmem] * 4 + [anywhere] * 5,
-        out_specs=(vmem, vmem, anywhere, anywhere, anywhere, vmem),
+        out_specs=(vmem, anywhere, anywhere, anywhere, vmem),
         scratch_shapes=[
             pltpu.VMEM((total, width), BF16),
             pltpu.VMEM(bcdt.shape, BF16),
@@ -1224,8 +1262,10 @@
             pltpu.VMEM((CHUNK + 8, width + 2 * LANES), F32),
             pltpu.VMEM((CHUNK + 8, LANES), jnp.int32),
         ]
+        + pair_scratch(dp_count, (width + LANES, cut))
+        + [pltpu.VMEM(gz.shape, BF16)]
         + line_scratch(dp_count, gz.shape[1:])
-        + [pltpu.SemaphoreType.DMA((2, 3)), pltpu.SemaphoreType.DMA((12,)), pltpu.SemaphoreType.DMA((3,))],
+        + [pltpu.SemaphoreType.DMA((2, 3)), pltpu.SemaphoreType.DMA((12,)), pltpu.SemaphoreType.DMA((2 + dp_count // 2,))],
         compiler_params=pltpu.CompilerParams(
             collective_id=2, has_side_effects=True, vmem_limit_bytes=60 * 1024 * 1024
         ),
@@ -1235,33 +1275,37 @@
 def fourth_kernel(
     heads, x_ref, d_own_ref, gain_ref, small_ref, gain_sum_ref, expand_ref, dz_ref, dx_ref, dbcdt_ref, wz_ref, wx_ref,
     wbc_ref, u_ref, gl_ref,
-    gw_x, gw_rest, grad_x, sums,
-    dz, dx, dbcdt, wz, wx, wbc, u, own, gain_part, packed, over_z,
-    parts, pair, right, left, pair_sems, right_sems, left_sems,
+    gw_x, grad_x, sums,
+    dz, dx, dbcdt, wz, wx, wbc, u, own, gain_part, packed, over_z, parts,
+    right, left, right_sems, left_sems,
     away, to_side, to_up, in_half, in_side, in_up, plane_sems, z_sems, tp_sems, load_sems,
 ):
     rows, model = x_ref.shape
     width = dz.shape[1]
     me, side, up, far = tp_places()
-    dp_count = parts.shape[0]
+    dp_count = 2 * parts.shape[0]
     loads = Copies(load_sems)
-    load_parts = loads.start(gl_ref, parts)
-    line = LineSum(parts, pair, right, left, pair_sems, right_sems, left_sems)
-    plane = PlaneSum(away, to_side, to_up, in_half, in_side, in_up, plane_sems)
-    others = [{"dp": lax.rem(line.dp + 2 * n, dp_count)} for n in range(1, dp_count // 2)]
-    greet([{"tp": side}, {"tp": up}, {"tp": far}, line.partner] + others)
-    load_parts.wait()
-    order = line.order()
-    for z_chunk in order:
-        line.swap(z_chunk)
+    weights = [loads.start(wz_ref, wz), loads.start(wx_ref, wx), loads.start(wbc_ref, wbc)]
     loads_of = {}
-    weights = [loads.start(wz_ref, wz), loads.start(wx_ref, wx), loads.start(wbc_ref, wbc)]
-    for name, place in (("far", far), ("side", side), ("up", up), ("me", me)):
+
+    def load_block(name, place):
         piece = pl.ds(pl.multiple_of(place * rows, rows), rows)
         loads_of[name] = [
             loads.start(source.at[piece], target.at[piece])
             for source, target in ((dz_ref, dz), (dx_ref, dx), (dbcdt_ref, dbcdt), (u_ref, u))
         ]
+
+    load_block("far", far)
+    load_parts = loads.start(gl_ref, parts)
+    line = LineSum(parts, lambda z: z, right, left, right_sems, left_sems)
+    plane = PlaneSum(away, to_side, to_up, in_half, in_side, in_up, plane_sems)
+    partner = {"dp": line.dp + 1 - 2 * lax.rem(line.dp, 2)}
+    others = [{"dp": lax.rem(line.dp + 2 * n, dp_count)} for n in range(1, dp_count // 2)]
+    greet([{"tp": side}, {"tp": up}, {"tp": far}, partner] + others)
+    load_parts.wait()
+    line.lead(*range(1, line.count - 1))
+    for name, place in (("side", side), ("up", up), ("me", me)):
+        load_block(name, place)
     gain_part[...] = jnp.zeros_like(gain_part)
 
     def du_block(name, place, target):
@@ -1282,22 +1326,20 @@
 
         lax.fori_loop(0, model // 512, tile, 0)
 
-    for z_chunk in order[:2]:
-        line.merge(z_chunk)
-    line.move(1)
     for copy in weights:
         copy.wait()
     du_block("far", far, away)
     plane.start_far()
-    for z_chunk in order[2:]:
-        line.merge(z_chunk)
     du_block("side", side, to_side)
     plane.start_side()
+    line.relay(2, 0)
     du_block("up", up, to_up)
     plane.start_up()
-    line.move(2)
+    line.relay(2, 1)
+    plane.pass_on()
     du_block("me", me, own)
-    plane.pass_on()
+    for step in range(3, line.count):
+        line.relay(step, 0)
 
     wide = width + 2 * LANES
     shift = (
@@ -1318,7 +1360,7 @@
     packed[0, 7:8, :LANES] = placed[7:8]
     packed[0, 7:8, LANES : 2 * LANES] = placed[15:16]
     packed[0, :, wide:] = jnp.concatenate([gain_part[0:1, :] / gain_ref[...], jnp.zeros((7, model), F32)], axis=0)
-    trade = send(packed.at[0], packed.at[1], z_sems.at[0, 0], z_sems.at[1, 0], line.partner)
+    trade = send(packed.at[0], packed.at[1], z_sems.at[0, 0], z_sems.at[1, 0], partner)
     trade.start()
     trade.wait()
     over_z[0] = packed[0] + packed[1]
@@ -1328,8 +1370,9 @@
     ]
     for copy in copies:
         copy.start()
+    line.lead(line.count - 1)
     for step in range(3, line.count):
-        line.move(step)
+        line.relay(step, 1)
     for copy in copies:
         copy.wait()
     everything = over_z[0]
@@ -1359,13 +1402,7 @@
         copy.wait()
     sum_ref = line.finish()
 
-    def turn(i, carry):
-        piece = pl.ds(pl.multiple_of(i * CHUNK, CHUNK), CHUNK)
-        gw_x[:, piece] = sum_ref[piece, :].astype(F32).T
-        return carry
-
-    lax.fori_loop(0, width // CHUNK, turn, 0)
-    gw_rest[...] = sum_ref[width:, :].astype(F32)
+    gw_x[...] = sum_ref[...]
     line.end()
     plane.end()
 
@@ -1381,13 +1418,12 @@
     return pl.pallas_call(
         functools.partial(fourth_kernel, heads),
         out_shape=(
-            jax.ShapeDtypeStruct((cut, width), F32),
-            jax.ShapeDtypeStruct((LANES, cut), F32),
+            jax.ShapeDtypeStruct(gl.shape[1:], BF16),
             jax.ShapeDtypeStruct((rows, model), F32),
             jax.ShapeDtypeStruct((4, 8, wide), F32),
         ),
         in_specs=[vmem] * 6 + [anywhere] * 8,
-        out_specs=(vmem,) * 4,
+        out_specs=(vmem,) * 3,
         scratch_shapes=[
             pltpu.VMEM((total, width), BF16),
             pltpu.VMEM((total, width), BF16),
@@ -1400,8 +1436,9 @@
             pltpu.VMEM((8, model), F32),
             pltpu.VMEM((2, 8, wide), F32),
             pltpu.VMEM((dp_count // 2, 8, wide), F32),
+            pltpu.VMEM(gl.shape, BF16),
         ]
-        + line_scratch(dp_count, (width + LANES, cut))
+        + line_scratch(dp_count, gl.shape[1:])
         + plane_scratch(rows, model)
         + [
             pltpu.SemaphoreType.DMA((2, dp_count // 2)),
@@ -1415,26 +1452,19 @@
 
 
 def results_kernel(
-    own_cols, heads, block_ref, grad_x_ref, first_ref, last_ref, z_ref, x_ref, rest_ref, sums_ref,
+    own_cols, heads, block_ref, grad_x_ref, first_ref, z_ref, x_ref, sums_ref,
     block_out, grad_x, gw_z, gw_x, gw_b, gw_c, gw_dt, gw_out, conv_w, conv_b, gate, norm, dt_bias, a_log, skip,
-    held_block, held_grad_x, held_z, held_x, held_first, held_last, load_sems, sems,
+    held_block, held_grad_x, first, z, x, load_sems, sems,
 ):
-    taken = first_ref.shape[0]
     loads, copies = Copies(load_sems), Copies(sems)
-    held = (held_block, held_grad_x, held_z, held_x, held_first, held_last)
-    targets = (block_out, grad_x, gw_z, gw_x, gw_out.at[:taken], gw_out.at[taken:])
-    for source, target in zip((block_ref, grad_x_ref, z_ref, x_ref, first_ref, last_ref), held):
+    for source, target in ((first_ref, first), (z_ref, z), (x_ref, x), (grad_x_ref, held_grad_x), (block_ref, held_block)):
         loads.start(source, target)
-    for load, source, target in zip(loads.started, held, targets):
-        load.wait()
-        copies.start(source, target)
-    width = z_ref.shape[1]
+    load_first, load_z, load_x, load_grad_x, load_block = loads.started
+    taken = first.shape[0]
+    width = gw_z.shape[1]
     count = sums_ref.shape[0]
     inner = gate.shape[1]
     wide = width + 2 * LANES
-    gw_b[...] = rest_ref[:own_cols, :]
-    gw_c[...] = rest_ref[own_cols : 2 * own_cols, :]
-    gw_dt[...] = rest_ref[2 * own_cols : 2 * own_cols + heads, :]
 
     def over_tp(rows, columns):
         total = sums_ref[0, rows, columns]
@@ -1454,45 +1484,69 @@
     dt_bias[...] = over_tp(slice(7, 8), slice(0, LANES))[:, :total_heads]
     a_log[...] = over_tp(slice(7, 8), slice(LANES, 2 * LANES))[:, :total_heads]
     skip[...] = over_tp(slice(6, 7), slice(width, width + LANES))[:, :total_heads]
+    load_grad_x.wait()
+    copies.start(held_grad_x, grad_x)
+    load_block.wait()
+    copies.start(held_block, block_out)
+    load_first.wait()
+    gw_out[:taken, :] = first[...].astype(F32)
+    load_z.wait()
+    gw_out[taken:, :] = z[width:, :].astype(F32)
+
+    def turn(source, target):
+        def one(i, carry):
+            piece = pl.ds(pl.multiple_of(i * CHUNK, CHUNK), CHUNK)
+            target[:, piece] = source[piece, :].T.astype(F32)
+            return carry
+
+        lax.fori_loop(0, width // CHUNK, one, 0)
+
+    turn(z, gw_z)
+    load_x.wait()
+    turn(x, gw_x)
+    gw_b[...] = x[width : width + own_cols, :].astype(F32)
+    gw_c[...] = x[width + own_cols : width + 2 * own_cols, :].astype(F32)
+    gw_dt[...] = x[width + 2 * own_cols : width + 2 * own_cols + heads, :].astype(F32)
     for copy in copies.started:
         copy.wait()
 
 
-def results_part(own_cols, heads, block_out, grad_x, first, last, gw_z, gw_x, rest, sums):
-    cut, width = gw_z.shape
+def results_part(own_cols, heads, block_out, grad_x, first, gw_z, gw_x, sums):
+    cut = first.shape[1]
     count = sums.shape[0]
+    width = gw_x.shape[0] - LANES
     inner = width * count
     model = grad_x.shape[1]
     vmem = pl.BlockSpec(memory_space=pltpu.VMEM)
     anywhere = pl.BlockSpec(memory_space=pl.ANY)
     shapes = [
-        ((own_cols, cut), F32),
-        ((own_cols, cut), F32),
-        ((heads, cut), F32),
-        ((first.shape[0] + last.shape[0], cut), F32),
-        ((4, inner + 2 * LANES), F32),
-        ((1, inner + 2 * LANES), F32),
-        ((1, inner), F32),
-        ((1, model), F32),
-        ((1, heads * count), F32),
-        ((1, heads * count), F32),
-        ((1, heads * count), F32),
+        (cut, width),
+        (cut, width),
+        (own_cols, cut),
+        (own_cols, cut),
+        (heads, cut),
+        (width, cut),
+        (4, inner + 2 * LANES),
+        (1, inner + 2 * LANES),
+        (1, inner),
+        (1, model),
+        (1, heads * count),
+        (1, heads * count),
+        (1, heads * count),
     ]
     return pl.pallas_call(
         functools.partial(results_kernel, own_cols, heads),
         out_shape=[
             jax.ShapeDtypeStruct(block_out.shape, BF16),
             jax.ShapeDtypeStruct(grad_x.shape, F32),
-            jax.ShapeDtypeStruct(gw_z.shape, F32),
-            jax.ShapeDtypeStruct(gw_x.shape, F32),
         ]
-        + [jax.ShapeDtypeStruct(*shape) for shape in shapes],
-        in_specs=[anywhere] * 6 + [vmem] * 2,
-        out_specs=[anywhere] * 4 + [vmem] * 3 + [anywhere] + [vmem] * 7,
-        scratch_shapes=[pltpu.VMEM(large.shape, large.dtype) for large in (block_out, grad_x, gw_z, gw_x, first, last)]
-        + [pltpu.SemaphoreType.DMA((6,)), pltpu.SemaphoreType.DMA((6,))],
+        + [jax.ShapeDtypeStruct(shape, F32) for shape in shapes],
+        in_specs=[anywhere] * 5 + [vmem],
+        out_specs=[anywhere] * 2 + [vmem] * len(shapes),
+        scratch_shapes=[pltpu.VMEM(large.shape, large.dtype) for large in (block_out, grad_x, first, gw_z, gw_x)]
+        + [pltpu.SemaphoreType.DMA((5,)), pltpu.SemaphoreType.DMA((2,))],
         compiler_params=pltpu.CompilerParams(vmem_limit_bytes=60 * 1024 * 1024),
-    )(block_out, grad_x, first, last, gw_z, gw_x, rest, sums)
+    )(block_out, grad_x, first, gw_z, gw_x, sums)
 
 
 def in_norm_scale(values):
@@ -1504,6 +1558,7 @@
     doc_lens, d_out,
 ):
     tp_count = lax.axis_size("tp")
+    in_planes = tp_count == 4 and lax.axis_size("dp") == 8
     rank = lax.axis_index("tp")
     dev_rows, model = x_in.shape
     rows = dev_rows * tp_count
@@ -1517,11 +1572,12 @@
     x_float = x_in.astype(F32)
     r_in = in_norm_scale(x_float)
     small_weights = jnp.concatenate([w_b, w_c, w_dt], axis=1).T
-    if tp_count == 4:
+    if in_planes:
         lanes = jnp.zeros((LANES - d_skip.shape[0],), F32)
         flat = jnp.concatenate([conv_b, gate_gain, dt_bias, lanes, a_log, lanes, d_skip, lanes])[None, :]
         (
-            gathered, zx, bcdt, w_bcdt, mixed, g, yo, yo_t, states, grad_gathered, dyo, coef, pos, prm, head_prm, expand
+            gathered, zx, bcdt, w_bcdt, mixed, g, yo, yo_t, states, grad_gathered, dyo, coef, pos, prm, head_prm, expand,
+            cross,
         ) = first_part(
             inner, heads, own_cols, x_in, norm_gain[None, :], small_weights, conv_w.T, flat, doc_lens, w_z, w_x, w_out,
             d_out,
@@ -1587,14 +1643,14 @@
         coef = jnp.stack([r_gate] + [zeros] * 7 + [r_gate**3 * (eg_total / inner)] + [zeros] * (LANES - 9), axis=1)
         yo = (g * r_gate[:, None] * gain_own[None, :]).astype(BF16)
 
-    if tp_count == 4:
+    if in_planes:
         block_out, gw_first, dz, dy, gz, gain_sum = second_part(
-            x_in, yo, yo_t, grad_gathered, w_out, dyo, g, mixed, zx, coef, prm, gathered
-        )
-        gw_z, gw_last, grad_xs, grad_bcdt, gl, small = third_part(
+            inner, x_in, cross, yo, yo_t, grad_gathered, w_out, dyo, g, mixed, zx, coef, prm, gathered
+        )
+        gw_z, grad_xs, grad_bcdt, gl, small = third_part(
             own_cols, heads, zx, bcdt, pos, prm, head_prm, expand, mixed, states, dy, gathered, gz
         )
-        gw_x, gw_rest, grad_x, sums = fourth_part(
+        gw_x, grad_x, sums = fourth_part(
             heads, x_in, d_out, norm_gain[None, :], small, gain_sum, expand, dz, grad_xs, grad_bcdt, w_z, w_x, w_bcdt,
             gathered, gl
         )
@@ -1602,7 +1658,7 @@
             block_out, grad_x, gw_z, gw_x, gw_b, gw_c, gw_dt, gw_out, g_conv_w, g_conv_b, g_gate, g_norm, g_dt_bias,
             g_a_log, g_skip
         ) = results_part(
-            own_cols, heads, block_out, grad_x, gw_first, gw_last, gw_z, gw_x, gw_rest, sums
+            own_cols, heads, block_out, grad_x, gw_first, gw_z, gw_x, sums
         )
         return (
             block_out, grad_x, g_norm[0], gw_z, gw_x, gw_b.T, gw_c.T, gw_dt.T, g_conv_w.T, g_conv_b[0], g_dt_bias[0],

time: 263 us -> 249 us (0.947)
  Pallas kernels: 257 us -> 243 us
    pallas_call x1, Pallas kernels: 59.3 us -> 53.6 us  [fourth_part(): pl.pallas_call(functools.partial(fourth_kernel, heads), out_shape=(jax.Sh...]
    pallas_call x1, Pallas kernels: 88.7 us -> 83.1 us  [first_part(): pl.pallas_call(functools.partial(first_kernel, inner, heads, own_cols), o...]
    pallas_call x1, Pallas kernels: 49.9 us -> 46.7 us  [second_part(): pl.pallas_call(functools.partial(second_kernel, inner), out_shape=(jax.Sh...]
where the time goes in v2:
time: 249 us
  Pallas kernels  243 us (98%)
  other arithmetic  3.12 us (1%)
    pallas_call x1, Pallas kernels, first_part(): pl.pallas_call(functools.partial(first_kernel, inner, heads, own_cols), o...  83.1 us
    pallas_call x1, Pallas kernels, fourth_part(): pl.pallas_call(functools.partial(fourth_kernel, heads), out_shape=(jax.Sh...  53.6 us
    pallas_call x1, Pallas kernels, third_part(): pl.pallas_call(functools.partial(third_kernel, own_cols, heads), out_shap...  53.2 us
    pallas_call x1, Pallas kernels, second_part(): pl.pallas_call(functools.partial(second_kernel, inner), out_shape=(jax.Sh...  46.7 us
    pallas_call x1, Pallas kernels, results_part(): pl.pallas_call(functools.partial(results_kernel, own_cols, heads), out_sh...  6.56 us

profile of v2, /device:TPU:0, one launch (start us, length us, event | category | flops | bytes accessed | tf_op | source)
XLA Modules:
  0.0 248.5 jit_solution(7042464034024239693)
XLA Ops:
  0.7 0.8 concatenate.7
  1.5 0.6 broadcast_in_dim.12.flat_ref
  2.1 1.8 maximum_bitcast_fusion.small_ref
  3.9 83.1 %shard_map.271 = (bf16[1024,2048]{1,0:T(8,128)(2,1)}, bf16[1024,2048]{1,0:T(8,128)(2,1)}, bf16[1024,384]{1,0:T(8,128)(2,1)}, bf16[384,2048]{1,0:T(8,128)(2,1)}, ...) custom-call(bf16[256,2048]{1,0:T(8,128)(2,1)} %x_ref.5, ...), custom_call_target="tpu_custom_call" | custom-call | tf_op jit(solution)/shard_map/pallas_call | solution.py:675
  87.0 46.7 %shard_map.272 = (bf16[256,2048]{1,0:T(8,128)(2,1)}, bf16[896,256]{1,0:T(8,128)(2,1)}, bf16[1024,1024]{1,0:T(8,128)(2,1)}, bf16[1024,1024]{1,0:T(8,128)(2,1)}, b...) custom-call(bf16[256,2048]{1,0:T(8,128)(2,1)} %x_ref.5, f32[8,1024]{1,0:T(8,128)} %get-tuple-element.61.cross_ref, ...), custom_call_target="tpu_custom_call" | custom-call | tf_op jit(solution)/shard_map/pallas_call | solution.py:1078
  133.7 53.2 %shard_map.273 = (bf16[1152,256]{1,0:T(8,128)(2,1)}, bf16[1024,1024]{1,0:T(8,128)(2,1)}, bf16[1024,384]{1,0:T(8,128)(2,1)}, bf16[4,1152,256]{2,1,0:T(8,128)(2,1)}, f32[8,1280]{1,0:T(8,128)}) custom-call(bf16[1024,2048]{1,0:T(8,128)(2,1)} %get-tuple-element.68.zx_ref, bf16[1024,384]{1,0:T(8,128)(2,1)} %get-tuple-element.73.bcdt_ref, ...), custom_call_target="tpu_custom_call" | custom-call | tf_op jit(solution)/shard_map/pallas_call | solution.py:1237
  186.9 53.6 %shard_map.274 = (bf16[1152,256]{1,0:T(8,128)(2,1)}, f32[256,2048]{1,0:T(8,128)}, f32[4,8,3328]{2,1,0:T(8,128)}) custom-call(bf16[256,2048]{1,0:T(8,128)(2,1)} %x_ref.5, bf16[256,2048]{1,0:T(8,128)(2,1)} %d_own_ref.3, f32[1,2048]{1,0:T(1,128)} %bitcast.15, f32[8,1280]{1,0:T(8,128)} %get-tuple-element.80.small_ref, f32[8,1024]{1,0:T(8,128)} %get-tuple-element.81.gain_sum_ref, ...), custom_call_target="tpu_custom_call" | custom-call | tf_op jit(solution)/shard_map/pallas_call | solution.py:1418
  240.6 6.6 %shard_map.275 = (bf16[256,2048]{1,0:T(8,128)(2,1)}, f32[256,2048]{1,0:T(8,128)}, f32[256,1024]{1,0:T(8,128)}, f32[256,1024]{1,0:T(8,128)}, f32[32,256]{1,0:T(8,...) custom-call(bf16[256,2048]{1,0:T(8,128)(2,1)} %get-tuple-element.72., ...), custom_call_target="tpu_custom_call" | custom-call | tf_op jit(solution)/shard_map/pallas_call | solution.py:1537
  247.2 1.4 reduce
  (1 shorter events, 0.0 us)

commit v3 on v2

--- a/solution.py
+++ b/solution.py
@@ -26,14 +26,18 @@
     return jnp.concatenate([high, (v - high.astype(F32)).astype(BF16)], axis=1)
 
 
-def prepare_chunk(width, x, bc, raw_dt, pos, prm_ref, head_ref, expand_ref, ext):
-    rows = CHUNK
+def convolve(width, x, bc, pos, prm_ref, ext):
     ext[8:, :width] = x.astype(F32)
     ext[8:, width:] = bc.astype(F32)
     pre = prm_ref[3:4, :] * ext[8:, :] + prm_ref[4:5, :]
     for back in (1, 2, 3):
         here = (pos >= back).astype(F32)
-        pre = pre + prm_ref[3 - back : 4 - back, :] * (ext[8 - back : 8 - back + rows, :] * here)
+        pre = pre + prm_ref[3 - back : 4 - back, :] * (ext[8 - back : 8 - back + CHUNK, :] * here)
+    return pre
+
+
+def prepare_chunk(width, pre, raw_dt, pos, head_ref, expand_ref):
+    rows = CHUNK
     sig = jax.nn.sigmoid(pre)
     act = pre * sig
     xc = act[:, :width]
@@ -62,7 +66,6 @@
         expand_ref[...],
     )
     return dict(
-        pre=pre,
         sig=sig,
         xc=xc,
         b=b_rows,
@@ -95,25 +98,18 @@
 
 
 def forward_chunk(
-    width, at, zx_ref, bcdt_ref, pos_ref, prm_ref, head_ref, expand_ref, mixed_ref, g_ref, sum_ref, state_ref, ext,
-    state,
+    width, at, zx_ref, bcdt_ref, pos_ref, prm_ref, head_ref, expand_ref, mixed_ref, g_ref, sum_ref, state_ref,
+    pre_ref, ext, state,
 ):
     if isinstance(at, int):
         rows = slice(at * CHUNK, (at + 1) * CHUNK)
     else:
         rows = pl.ds(pl.multiple_of(at * CHUNK, CHUNK), CHUNK)
     ext[:8, :] = ext[CHUNK:, :]
-    k = prepare_chunk(
-        width,
-        zx_ref[rows, width:],
-        bcdt_ref[rows, : 2 * LANES],
-        bcdt_ref[rows, 2 * LANES :],
-        pos_ref[rows, :],
-        prm_ref,
-        head_ref,
-        expand_ref,
-        ext,
-    )
+    pos = pos_ref[rows, :]
+    pre = convolve(width, zx_ref[rows, width:], bcdt_ref[rows, : 2 * LANES], pos, prm_ref, ext)
+    pre_ref[rows, :] = pre
+    k = prepare_chunk(width, pre, bcdt_ref[rows, 2 * LANES :], pos, head_ref, expand_ref)
     stepped = (k["xc"] * k["dt_w"]).astype(BF16)
     held = state[...]
     held_low = held.astype(BF16)
@@ -139,7 +135,8 @@
 
 
 def forward_kernel(
-    width, zx_ref, bcdt_ref, pos_ref, prm_ref, head_ref, expand_ref, mixed_ref, g_ref, sum_ref, state_ref, ext, state
+    width, zx_ref, bcdt_ref, pos_ref, prm_ref, head_ref, expand_ref, mixed_ref, g_ref, sum_ref, state_ref,
+    pre_ref, ext, state,
 ):
     @pl.when(pl.program_id(0) == 0)
     def _():
@@ -147,30 +144,19 @@
         ext[...] = jnp.zeros_like(ext)
 
     forward_chunk(
-        width, 0, zx_ref, bcdt_ref, pos_ref, prm_ref, head_ref, expand_ref, mixed_ref, g_ref, sum_ref, state_ref, ext,
-        state,
+        width, 0, zx_ref, bcdt_ref, pos_ref, prm_ref, head_ref, expand_ref, mixed_ref, g_ref, sum_ref, state_ref,
+        pre_ref, ext, state,
     )
 
 
 def backward_chunk(
-    width, tokens, halo_x, halo_bc, held, x_ref, bcdt_ref, pos_ref, prm_ref, head_ref, expand_ref, mixed_ref,
-    dy_ref, grad_x_ref, grad_bcdt_ref, grad_t_ref, small_ref, ext, d_state, later, later_pos,
+    width, tokens, held, pre_ref, x_ref, bcdt_ref, pos_ref, prm_ref, head_ref, expand_ref, mixed_ref,
+    dy_ref, grad_x_ref, grad_bcdt_ref, grad_t_ref, small_ref, d_state, later, later_pos,
 ):
     rows = CHUNK
-    ext[:8, :width] = halo_x.astype(F32)[8:, :]
-    ext[:8, width:] = halo_bc.astype(F32)[8:, :]
     pos = pos_ref[tokens, :]
-    k = prepare_chunk(
-        width,
-        x_ref[tokens, :],
-        bcdt_ref[tokens, : 2 * LANES],
-        bcdt_ref[tokens, 2 * LANES :],
-        pos,
-        prm_ref,
-        head_ref,
-        expand_ref,
-        ext,
-    )
+    pre = pre_ref[tokens, :]
+    k = prepare_chunk(width, pre, bcdt_ref[tokens, 2 * LANES :], pos, head_ref, expand_ref)
     xc = k["xc"]
     skip = prm_ref[6:7, :width]
     y = mixed_ref[tokens, :] - skip * xc
@@ -229,17 +215,17 @@
     small_ref[7:8, LANES : 2 * LANES] += jnp.sum(d_decay * k["log_decay"], axis=0, keepdims=True)
     grad_bcdt_ref[tokens, 2 * LANES :] = d_raw.astype(BF16)
 
-    pre, sig = k["pre"], k["sig"]
+    sig = k["sig"]
     d_pre = jnp.concatenate([dxc, db, dc], axis=1) * (sig * (1.0 + pre * (1.0 - sig)))
     small_ref[4:5, :] += jnp.sum(d_pre, axis=0, keepdims=True)
     later[:rows, :] = d_pre
     later_pos[:rows, :] = jnp.broadcast_to(pos, (rows, LANES))
-    x_own = ext[8:, :]
+    x_own = jnp.concatenate([x_ref[tokens, :], bcdt_ref[tokens, : 2 * LANES]], axis=1).astype(F32)
     d_in = prm_ref[3:4, :] * d_pre
     small_ref[3:4, :] += jnp.sum(d_pre * x_own, axis=0, keepdims=True)
     for back in (1, 2, 3):
-        there = (later_pos[back : back + rows, 0:1] >= back).astype(F32)
-        reaching = later[back : back + rows, :] * there
+        there = (later_pos[back : back + rows, :] >= back).astype(F32)
+        reaching = later[back : back + rows, :] * jnp.concatenate([there] * (later.shape[1] // LANES), axis=1)
         small_ref[3 - back : 4 - back, :] += jnp.sum(reaching * x_own, axis=0, keepdims=True)
         d_in = d_in + prm_ref[3 - back : 4 - back, :] * reaching
     grad_x_ref[tokens, :] = d_in[:, :width].astype(BF16)
@@ -258,18 +244,16 @@
 
 
 def backward_kernel(
-    width, x_ref, bcdt_ref, halo_x_ref, halo_bc_ref, pos_ref, prm_ref, head_ref,
-    expand_ref, mixed_ref, state_ref, dy_ref, grad_x_ref, grad_bcdt_ref, small_ref, ext, d_state,
-    later, later_pos,
+    width, pre_ref, x_ref, bcdt_ref, pos_ref, prm_ref, head_ref, expand_ref, mixed_ref, state_ref, dy_ref, grad_x_ref,
+    grad_bcdt_ref, small_ref, d_state, later, later_pos,
 ):
     @pl.when(pl.program_id(0) == 0)
     def _():
         backward_start(small_ref, d_state, later, later_pos)
 
     backward_chunk(
-        width, slice(0, CHUNK), halo_x_ref[...], halo_bc_ref[:, : 2 * LANES], state_ref[0], x_ref, bcdt_ref, pos_ref,
-        prm_ref, head_ref, expand_ref, mixed_ref, dy_ref, grad_x_ref, grad_bcdt_ref, None, small_ref,
-        ext, d_state, later, later_pos,
+        width, slice(0, CHUNK), state_ref[0], pre_ref, x_ref, bcdt_ref, pos_ref, prm_ref, head_ref, expand_ref, mixed_ref,
+        dy_ref, grad_x_ref, grad_bcdt_ref, None, small_ref, d_state, later, later_pos,
     )
 
 
@@ -290,6 +274,7 @@
             jax.ShapeDtypeStruct((rows, width), F32),
             jax.ShapeDtypeStruct((8, rows), F32),
             jax.ShapeDtypeStruct((chunks, LANES, width), BF16),
+            jax.ShapeDtypeStruct((rows, width + 2 * LANES), F32),
         ),
         grid=(chunks,),
         in_specs=[tokens(2 * width), tokens(3 * LANES), tokens(1), whole(prm), whole(head_prm), whole(expand)],
@@ -298,6 +283,7 @@
             tokens(width),
             pl.BlockSpec((8, CHUNK), lambda i: (0, i)),
             pl.BlockSpec((1, LANES, width), lambda i: (i, 0, 0)),
+            tokens(width + 2 * LANES),
         ),
         scratch_shapes=[
             pltpu.VMEM((CHUNK + 8, width + 2 * LANES), F32),
@@ -309,17 +295,12 @@
     )(zx, bcdt, pos, prm, head_prm, expand)
 
 
-def mixer_backward(width, zx, bcdt, pos, prm, head_prm, expand, mixed, states, dy):
+def mixer_backward(width, pre, zx, bcdt, pos, prm, head_prm, expand, mixed, states, dy):
     rows = zx.shape[0]
     chunks = rows // CHUNK
 
     def tokens(columns):
         return pl.BlockSpec((CHUNK, columns), lambda i: (chunks - 1 - i, 0))
-
-    def before(columns, place):
-        return pl.BlockSpec(
-            (16, columns), lambda i: (jnp.maximum((chunks - 1 - i) * (CHUNK // 16) - 1, 0), place)
-        )
 
     def whole(array):
         return pl.BlockSpec(array.shape, lambda i: (0, 0))
@@ -333,10 +314,9 @@
         ),
         grid=(chunks,),
         in_specs=[
+            tokens(width + 2 * LANES),
             pl.BlockSpec((CHUNK, width), lambda i: (chunks - 1 - i, 1)),
             tokens(3 * LANES),
-            before(width, 1),
-            before(3 * LANES, 0),
             tokens(1),
             whole(prm),
             whole(head_prm),
@@ -351,7 +331,6 @@
             pl.BlockSpec((8, width + 2 * LANES), lambda i: (0, 0)),
         ),
         scratch_shapes=[
-            pltpu.VMEM((CHUNK + 8, width + 2 * LANES), F32),
             pltpu.VMEM((LANES, width), F32),
             pltpu.VMEM((CHUNK + 8, width + 2 * LANES), F32),
             pltpu.VMEM((CHUNK + 8, LANES), jnp.int32),
@@ -360,7 +339,7 @@
             dimension_semantics=("arbitrary",), vmem_limit_bytes=48 * 1024 * 1024
         ),
         cost_estimate=pl.CostEstimate(flops=rows * width * 2048, bytes_accessed=rows * width * 20, transcendentals=0),
-    )(zx, bcdt, zx, bcdt, pos, prm, head_prm, expand, mixed, states, dy)
+    )(pre, zx, bcdt, pos, prm, head_prm, expand, mixed, states, dy)
 
 
 MESH = pl.DeviceIdType.MESH
@@ -474,8 +453,8 @@
 def first_kernel(
     inner, heads, own_cols, x_ref, gain_ref, small_ref, taps_ref, flat_ref, lens_ref, wz_ref, wx_ref, w_out_ref, d_own_ref,
     u_out, zx_out, bcdt_out, wbc_out, mixed_out, g_out, yo_out, yo_t_out, state_out, d_out, dyo_out, coef_out, pos_out,
-    prm_out, head_out, expand_out, cross_out,
-    weights, w_out, u, zx, bcdt, wbc, mixed, g, yo, yo_t, states, d, dyo, coef, pos, prm, head, expand, ext, state, sums,
+    prm_out, head_out, expand_out, pre_out, cross_out,
+    weights, w_out, u, zx, bcdt, wbc, mixed, g, yo, yo_t, states, d, dyo, coef, pos, prm, head, expand, pre, ext, state, sums,
     acc, sems, sum_sems, load_sems, store_sems,
 ):
     rows, model = x_ref.shape
@@ -577,7 +556,7 @@
 
     def chunk(i, carry):
         forward_chunk(
-            width, i, zx, bcdt, pos, prm, head, expand, mixed, g, sums.at[0], states, ext, state
+            width, i, zx, bcdt, pos, prm, head, expand, mixed, g, sums.at[0], states, pre, ext, state
         )
         return carry
 
@@ -593,6 +572,7 @@
     keep(mixed, mixed_out)
     keep(g, g_out)
     keep(states, state_out)
+    keep(pre, pre_out)
     loads[2].wait()
 
     def back_to_heads(place):
@@ -670,6 +650,7 @@
         ((8, width + 2 * LANES), F32),
         ((8, LANES), F32),
         ((2 * LANES, width), BF16),
+        ((total, width + 2 * LANES), F32),
     ]
     cross = jax.ShapeDtypeStruct((8, total), F32)
     return pl.pallas_call(
@@ -720,7 +701,7 @@
         dp = lax.axis_index("dp")
         self.parity = lax.rem(dp, 2)
         self.partner = {"dp": dp + 1 - 2 * self.parity}
-        self.parts, self.pair, self.sems, self.swaps = parts, pair, sems, {}
+        self.parts, self.pair, self.sems = parts, pair, sems
 
     def theirs(self, z):
         return 2 * z + 1 - self.parity
@@ -728,15 +709,16 @@
     def ours(self, z):
         return 2 * z + self.parity
 
+    def copy(self, z):
+        return send(
+            self.parts.at[self.theirs(z)], self.pair.at[z], self.sems.at[0, z], self.sems.at[1, z], self.partner
+        )
+
     def swap(self, z):
-        copy = send(
-            self.parts.at[self.theirs(z)], self.pair.at[z], self.sems.at[0, z], self.sems.at[1, z], self.partner
-        )
-        copy.start()
-        self.swaps[z] = copy
+        self.copy(z).start()
 
     def merge(self, z):
-        self.swaps[z].wait()
+        self.copy(z).wait()
         add_into(self.parts.at[self.ours(z)], self.pair.at[z])
 
 
@@ -822,64 +804,47 @@
 
 
 class PlaneSum:
-    def __init__(self, away, to_side, to_up, in_half, in_side, in_up, sems):
+    def __init__(self, away, to_side, to_up, in_far, in_side, in_up, sems):
         _, side, up, _ = tp_places()
-        side, up = {"tp": side}, {"tp": up}
-        rows = to_side.shape[0]
-        half = rows // 2
-        self.to_side, self.to_up, self.in_half, self.half = to_side, to_up, in_half, half
-        self.in_side, self.in_up = in_side, in_up
-        low, high = pl.ds(0, half), pl.ds(half, half)
-
-        def one(n, source, target, peer):
-            return send(source, target, sems.at[0, n], sems.at[1, n], peer)
-
-        self.away_side = one(0, away.at[low], in_half.at[0], side)
-        self.away_up = one(1, away.at[high], in_half.at[1], up)
-        self.side_low = one(2, to_side.at[low], in_side.at[low], side)
-        self.side_high = one(3, to_side.at[high], in_side.at[high], side)
-        self.up_low = one(4, to_up.at[low], in_up.at[low], up)
-        self.up_high = one(5, to_up.at[high], in_up.at[high], up)
-        self.low, self.high = low, high
-
-    def start_far(self):
-        self.away_side.start()
-        self.away_up.start()
-
-    def start_side(self):
-        self.side_low.start()
-
-    def start_up(self):
-        self.up_high.start()
+        peers = ({"tp": side}, {"tp": up})
+        self.to, self.in_far, self.into = (to_side, to_up), in_far, (in_side, in_up)
+
+        def one(kind, n, source, target, peer):
+            return send(source.at[n], target.at[n], sems.at[0, kind, n], sems.at[1, kind, n], peer)
+
+        self.one, self.peers, self.away = one, peers, away
+        self.far = [one(0, n, away, in_far, peers[n % 2]) for n in range(4)]
+        self.near = [[one(1 + w, n, self.to[w], self.into[w], peers[w]) for n in range(4)] for w in range(2)]
+
+    def start_far(self, n, odd):
+        self.one(0, n, self.away, self.in_far, self.peers[odd]).start()
+
+    def start_near(self, way, n, odd):
+        if odd == way:
+            self.one(1 + way, n, self.to[way], self.into[way], self.peers[way]).start()
 
     def pass_on(self):
-        self.away_side.wait_recv()
-        add_into(self.to_up.at[self.low], self.in_half.at[0])
-        self.up_low.start()
-        self.away_up.wait_recv()
-        add_into(self.to_side.at[self.high], self.in_half.at[1])
-        self.side_high.start()
+        for n in range(4):
+            way = 1 - n % 2
+            self.far[n].wait_recv()
+            add_into(self.to[way].at[n], self.in_far.at[n])
+            self.near[way][n].start()
 
     def finish(self):
-        for copy in (self.side_low, self.up_high, self.side_high, self.up_low):
+        for copy in self.near[0] + self.near[1]:
             copy.wait_recv()
 
+    def received(self, piece):
+        side, up = (jnp.concatenate([into[n, piece, :] for n in range(4)], axis=1) for into in self.into)
+        return side.astype(F32) + up.astype(F32)
+
     def end(self):
-        for copy in (self.away_side, self.away_up, self.side_low, self.side_high, self.up_low, self.up_high):
+        for copy in self.far + self.near[0] + self.near[1]:
             copy.wait_send()
 
 
 def plane_scratch(rows, model):
-    half = rows // 2
-    return [
-        pltpu.VMEM((rows, model), BF16),
-        pltpu.VMEM((rows, model), BF16),
-        pltpu.VMEM((rows, model), BF16),
-        pltpu.VMEM((2, half, model), BF16),
-        pltpu.VMEM((rows, model), BF16),
-        pltpu.VMEM((rows, model), BF16),
-        pltpu.SemaphoreType.DMA((2, 6)),
-    ]
+    return [pltpu.VMEM((4, rows, model // 4), BF16) for _ in range(6)] + [pltpu.SemaphoreType.DMA((2, 3, 4))]
 
 
 def pair_scratch(dp_count, shape):
@@ -926,7 +891,7 @@
     u_ref, block_out, gw_out, dz_out, dy_out, gz_out, gain_out,
     yo, yo_t, d, w_out, dyo, g, mixed, z, coef, own, gz, parts, pair, pair_sems, gz_pair, gz_pair_sems,
     right, left, right_sems, left_sems,
-    away, to_side, to_up, in_half, in_side, in_up, plane_sems, cross, cross_sems, load_sems, store_sems,
+    away, to_side, to_up, in_far, in_side, in_up, plane_sems, cross, cross_sems, load_sems, store_sems,
 ):
     rows, model = x_ref.shape
     total, width = yo.shape
@@ -938,7 +903,7 @@
     cores = PairSum(parts, pair, pair_sems)
     gz_cores = PairSum(gz, gz_pair, gz_pair_sems)
     line = LineSum(parts, cores.ours, right, left, right_sems, left_sems)
-    plane = PlaneSum(away, to_side, to_up, in_half, in_side, in_up, plane_sems)
+    plane = PlaneSum(away, to_side, to_up, in_far, in_side, in_up, plane_sems)
     greet([{"tp": side}, {"tp": up}, {"tp": far}, cores.partner] + line.peers())
     crossing = [
         send(cross_ref, cross.at[n], cross_sems.at[0, n], cross_sems.at[1, n], {"tp": peer})
@@ -947,22 +912,30 @@
     for copy in crossing:
         copy.start()
 
-    def out_block(place, target):
+    quarter = model // 4
+
+    def out_block(place, target, started=None):
         piece = pl.ds(pl.multiple_of(place * rows, rows), rows)
 
-        def tile(n, carry):
-            columns = pl.ds(pl.multiple_of(n * 512, 512), 512)
-            target[:, columns] = dot(yo[piece, :], w_out[:, columns]).astype(target.dtype)
+        def two(m, carry):
+            for odd in range(2):
+                n = 2 * m + odd
+                columns = pl.ds(pl.multiple_of(n * quarter, quarter), quarter)
+                value = dot(yo[piece, :], w_out[:, columns])
+                if started is None:
+                    target[:, columns] = value
+                else:
+                    target[n] = value.astype(BF16)
+                    started(n, odd)
             return carry
 
-        lax.fori_loop(0, model // 512, tile, 0)
+        lax.fori_loop(0, 2, two, 0)
 
     load_yo.wait()
     load_w.wait()
     load_yo_t = loads.start(yo_t_ref, yo_t)
     load_d = loads.start(d_ref, d)
-    out_block(far, away)
-    plane.start_far()
+    out_block(far, away, plane.start_far)
     load_yo_t.wait()
     load_d.wait()
     rest = [
@@ -974,18 +947,21 @@
     ]
     order = line_order(line.count)
 
-    def products(z_chunk):
-        product_chunk(yo_t, d, cores.theirs(z_chunk), parts.at[cores.theirs(z_chunk)], taken // 2)
-        cores.swap(z_chunk)
-        product_chunk(yo_t, d, cores.ours(z_chunk), parts.at[cores.ours(z_chunk)], taken // 2)
-
-    for z_chunk in order[:2]:
-        products(z_chunk)
+    def products(first, step):
+        def one(i, carry):
+            z_chunk = first + step * i
+            product_chunk(yo_t, d, cores.theirs(z_chunk), parts.at[cores.theirs(z_chunk)], taken // 2)
+            cores.swap(z_chunk)
+            product_chunk(yo_t, d, cores.ours(z_chunk), parts.at[cores.ours(z_chunk)], taken // 2)
+            return carry
+
+        lax.fori_loop(0, 2, one, 0)
+
+    products(order[0], order[1] - order[0])
     for z_chunk in order[:2]:
         cores.merge(z_chunk)
     line.lead(1)
-    for z_chunk in order[2:]:
-        products(z_chunk)
+    products(order[2], order[3] - order[2])
 
     def left_over(chunk, carry):
         columns = pl.ds(pl.multiple_of(chunk * parts.shape[2], parts.shape[2]), parts.shape[2])
@@ -995,10 +971,8 @@
     for z_chunk in order[2:]:
         cores.merge(z_chunk)
     line.lead(*range(2, line.count))
-    out_block(side, to_side)
-    plane.start_side()
-    out_block(up, to_up)
-    plane.start_up()
+    out_block(side, to_side, functools.partial(plane.start_near, 0))
+    out_block(up, to_up, functools.partial(plane.start_near, 1))
     line.relay(2, 0)
     plane.pass_on()
     lax.fori_loop(0, parts.shape[0], left_over, 0)
@@ -1041,13 +1015,21 @@
     def gate_product(chunk):
         product_chunk(yo_t, d, chunk, gz.at[chunk, :width], width // 2)
 
-    for z_chunk in order:
+    def theirs(z_chunk, carry):
         gate_product(gz_cores.theirs(z_chunk))
         gz_cores.swap(z_chunk)
+        return carry
+
+    lax.fori_loop(0, line.count, theirs, 0)
     for step in range(3, line.count):
         line.relay(step, 1)
-    for z_chunk in order:
+
+    def ours(z_chunk, carry):
         gate_product(gz_cores.ours(z_chunk))
+        return carry
+
+    lax.fori_loop(0, line.count, ours, 0)
+    for z_chunk in range(line.count):
         gz_cores.merge(z_chunk)
         stores.start(gz.at[gz_cores.ours(z_chunk)], gz_out.at[z_chunk])
     sum_ref = line.finish()
@@ -1056,7 +1038,7 @@
 
     def add_own(i, carry):
         piece = pl.ds(pl.multiple_of(i * 32, 32), 32)
-        total_out = own[piece, :] + in_side[piece, :].astype(F32) + in_up[piece, :].astype(F32)
+        total_out = own[piece, :] + plane.received(piece)
         block_out[piece, :] = (x_ref[piece, :].astype(F32) + total_out).astype(BF16)
         return carry
 
@@ -1119,9 +1101,9 @@
 
 def third_kernel(
     own_cols, heads, zx_ref, bcdt_ref, pos_ref, prm_ref, head_ref, expand_ref, mixed_ref, state_ref, dy_ref,
-    u_ref, gz_ref,
+    pre_ref, u_ref, gz_ref,
     gw_z, dx_out, dbcdt_out, gl_out, small_out,
-    x, bcdt, mixed, states, dy, u, dx, dbcdt, dx_t, gl, bc_in, ext, d_state, later, later_pos,
+    x, bcdt, mixed, states, dy, pre, u, dx, dbcdt, dx_t, gl, bc_in, d_state, later, later_pos,
     pair, pair_sems, parts, right, left, right_sems, left_sems, bc_sems, load_sems, store_sems,
 ):
     total, width = mixed.shape
@@ -1131,7 +1113,6 @@
     load_parts = loads.start(gz_ref, parts)
     cores = PairSum(gl, pair, pair_sems)
     line = LineSum(parts, lambda z: z, right, left, right_sems, left_sems)
-    order = line_order(line.count)
     halves_of_loads = []
     for first in (total // 2, 0):
         piece = pl.ds(first, total // 2)
@@ -1143,6 +1124,7 @@
                 loads.start(mixed_ref.at[piece], mixed.at[piece]),
                 loads.start(state_ref.at[pieces], states.at[pieces]),
                 loads.start(dy_ref.at[piece], dy.at[piece]),
+                loads.start(pre_ref.at[piece], pre.at[piece]),
             ]
         )
     load_u = loads.start(u_ref, u)
@@ -1150,18 +1132,22 @@
     backward_start(small_out, d_state, later, later_pos)
     load_parts.wait()
     line.lead(*range(1, line.count))
-    for copies in halves_of_loads:
-        for copy in copies:
-            copy.wait()
+    for copy in halves_of_loads[0]:
+        copy.wait()
     hooks = {3: (2, 0), 5: (2, 1), 7: (3, 0), chunks: (3, 1)}
 
     def chunk(i, carry):
         at = chunks - 1 - i
         tokens = pl.ds(pl.multiple_of(at * CHUNK, CHUNK), CHUNK)
-        halo = pl.ds(pl.multiple_of(lax.rem(at * CHUNK + total - 16, total), 16), 16)
+
+        @pl.when(i == chunks // 2)
+        def _():
+            for copy in halves_of_loads[1]:
+                copy.wait()
+
         backward_chunk(
-            width, tokens, x[halo, :], bcdt[halo, : 2 * LANES], states[at], x, bcdt, pos_ref, prm_ref, head_ref,
-            expand_ref, mixed, dy, dx, dbcdt, dx_t, small_out, ext, d_state, later, later_pos,
+            width, tokens, states[at], pre, x, bcdt, pos_ref, prm_ref, head_ref, expand_ref, mixed, dy, dx, dbcdt, dx_t,
+            small_out, d_state, later, later_pos,
         )
         for when, turn in hooks.items():
 
@@ -1202,21 +1188,29 @@
         columns = pl.ds(pl.multiple_of(chunk * gl.shape[2], gl.shape[2]), gl.shape[2])
         gl[chunk, width:, :] = dot(dx_t[width:, :], u[:, columns]).astype(BF16)
 
-    for z_chunk in order[:2]:
+    def their_x(z_chunk, carry):
         x_product(cores.theirs(z_chunk))
+        return carry
+
+    def their_bc(z_chunk, carry):
+        bc_product(cores.theirs(z_chunk))
+        cores.swap(z_chunk)
+        return carry
+
+    def ours(z_chunk, carry):
+        x_product(cores.ours(z_chunk))
+        bc_product(cores.ours(z_chunk))
+        return carry
+
+    lax.fori_loop(0, line.count, their_x, 0)
     for copy in copies:
         copy.wait()
     for n in range(3):
         own_bc = own_bc + bc_in[3 + n].astype(F32)
     dx_t[width : width + 2 * own_cols, :] = own_bc.astype(BF16)
-    for z_chunk in order:
-        if z_chunk not in order[:2]:
-            x_product(cores.theirs(z_chunk))
-        bc_product(cores.theirs(z_chunk))
-        cores.swap(z_chunk)
-    for z_chunk in order:
-        x_product(cores.ours(z_chunk))
-        bc_product(cores.ours(z_chunk))
+    lax.fori_loop(0, line.count, their_bc, 0)
+    lax.fori_loop(0, line.count, ours, 0)
+    for z_chunk in range(line.count):
         cores.merge(z_chunk)
         stores.start(gl.at[cores.ours(z_chunk)], gl_out.at[z_chunk])
     sum_ref = line.finish()
@@ -1227,7 +1221,7 @@
         copy.wait()
 
 
-def third_part(own_cols, heads, zx, bcdt, pos, prm, head_prm, expand, mixed, states, dy, u, gz):
+def third_part(own_cols, heads, zx, bcdt, pos, prm, head_prm, expand, mixed, states, dy, pre, u, gz):
     total, width = mixed.shape
     model = u.shape[1]
     dp_count = lax.axis_size("dp")
@@ -1243,7 +1237,7 @@
             jax.ShapeDtypeStruct((dp_count // 2, width + LANES, cut), BF16),
             jax.ShapeDtypeStruct((8, width + 2 * LANES), F32),
         ),
-        in_specs=[anywhere] * 2 + [vmem] * 4 + [anywhere] * 5,
+        in_specs=[anywhere] * 2 + [vmem] * 4 + [anywhere] * 6,
         out_specs=(vmem, anywhere, anywhere, anywhere, vmem),
         scratch_shapes=[
             pltpu.VMEM((total, width), BF16),
@@ -1251,13 +1245,13 @@
             pltpu.VMEM((total, width), F32),
             pltpu.VMEM(states.shape, BF16),
             pltpu.VMEM((total, width), BF16),
+            pltpu.VMEM((total, width + 2 * LANES), F32),
             pltpu.VMEM((total, model), BF16),
             pltpu.VMEM((total, width), BF16),
             pltpu.VMEM((total, 3 * LANES), BF16),
             pltpu.VMEM((width + LANES, total), BF16),
             pltpu.VMEM((dp_count, width + LANES, cut), BF16),
             pltpu.VMEM((6, 2 * own_cols, total), BF16),
-            pltpu.VMEM((CHUNK + 8, width + 2 * LANES), F32),
             pltpu.VMEM((LANES, width), F32),
             pltpu.VMEM((CHUNK + 8, width + 2 * LANES), F32),
             pltpu.VMEM((CHUNK + 8, LANES), jnp.int32),
@@ -1265,11 +1259,11 @@
         + pair_scratch(dp_count, (width + LANES, cut))
         + [pltpu.VMEM(gz.shape, BF16)]
         + line_scratch(dp_count, gz.shape[1:])
-        + [pltpu.SemaphoreType.DMA((2, 3)), pltpu.SemaphoreType.DMA((12,)), pltpu.SemaphoreType.DMA((2 + dp_count // 2,))],
+        + [pltpu.SemaphoreType.DMA((2, 3)), pltpu.SemaphoreType.DMA((14,)), pltpu.SemaphoreType.DMA((2 + dp_count // 2,))],
         compiler_params=pltpu.CompilerParams(
             collective_id=2, has_side_effects=True, vmem_limit_bytes=60 * 1024 * 1024
         ),
-    )(zx, bcdt, pos, prm, head_prm, expand, mixed, states, dy, u, gz)
+    )(zx, bcdt, pos, prm, head_prm, expand, mixed, states, dy, pre, u, gz)
 
 
 def fourth_kernel(
@@ -1278,7 +1272,7 @@
     gw_x, grad_x, sums,
     dz, dx, dbcdt, wz, wx, wbc, u, own, gain_part, packed, over_z, parts,
     right, left, right_sems, left_sems,
-    away, to_side, to_up, in_half, in_side, in_up, plane_sems, z_sems, tp_sems, load_sems,
+    away, to_side, to_up, in_far, in_side, in_up, plane_sems, z_sems, tp_sems, load_sems,
 ):
     rows, model = x_ref.shape
     width = dz.shape[1]
@@ -1298,7 +1292,7 @@
     load_block("far", far)
     load_parts = loads.start(gl_ref, parts)
     line = LineSum(parts, lambda z: z, right, left, right_sems, left_sems)
-    plane = PlaneSum(away, to_side, to_up, in_half, in_side, in_up, plane_sems)
+    plane = PlaneSum(away, to_side, to_up, in_far, in_side, in_up, plane_sems)
     partner = {"dp": line.dp + 1 - 2 * lax.rem(line.dp, 2)}
     others = [{"dp": lax.rem(line.dp + 2 * n, dp_count)} for n in range(1, dp_count // 2)]
     greet([{"tp": side}, {"tp": up}, {"tp": far}, partner] + others)
@@ -1308,38 +1302,40 @@
         load_block(name, place)
     gain_part[...] = jnp.zeros_like(gain_part)
 
-    def du_block(name, place, target):
+    quarter = model // 4
+
+    def du_block(name, place, target, started=None):
         for copy in loads_of[name]:
             copy.wait()
         piece = pl.ds(pl.multiple_of(place * rows, rows), rows)
 
-        def tile(n, carry):
-            columns = pl.ds(pl.multiple_of(n * 512, 512), 512)
-            du = (
-                dot(dz[piece, :], wz[columns, :], CONTRACT_LAST)
-                + dot(dx[piece, :], wx[columns, :], CONTRACT_LAST)
-                + dot(dbcdt[piece, :], wbc[:, columns])
-            )
-            target[:, columns] = du.astype(target.dtype)
-            gain_part[0:1, columns] += jnp.sum(du * u[piece, columns].astype(F32), axis=0, keepdims=True)
+        def two(m, carry):
+            for odd in range(2):
+                n = 2 * m + odd
+                columns = pl.ds(pl.multiple_of(n * quarter, quarter), quarter)
+                du = (
+                    dot(dz[piece, :], wz[columns, :], CONTRACT_LAST)
+                    + dot(dx[piece, :], wx[columns, :], CONTRACT_LAST)
+                    + dot(dbcdt[piece, :], wbc[:, columns])
+                )
+                if started is None:
+                    target[:, columns] = du
+                else:
+                    target[n] = du.astype(BF16)
+                    started(n, odd)
+                gain_part[pl.ds(n, 1), :] += jnp.sum(du * u[piece, columns].astype(F32), axis=0, keepdims=True)
             return carry
 
-        lax.fori_loop(0, model // 512, tile, 0)
+        lax.fori_loop(0, 2, two, 0)
 
     for copy in weights:
         copy.wait()
-    du_block("far", far, away)
-    plane.start_far()
-    du_block("side", side, to_side)
-    plane.start_side()
+    du_block("far", far, away, plane.start_far)
+    du_block("side", side, to_side, functools.partial(plane.start_near, 0))
     line.relay(2, 0)
-    du_block("up", up, to_up)
-    plane.start_up()
+    du_block("up", up, to_up, functools.partial(plane.start_near, 1))
     line.relay(2, 1)
-    plane.pass_on()
     du_block("me", me, own)
-    for step in range(3, line.count):
-        line.relay(step, 0)
 
     wide = width + 2 * LANES
     shift = (
@@ -1359,9 +1355,12 @@
     packed[0, 6:7, width : width + LANES] = placed[16:17]
     packed[0, 7:8, :LANES] = placed[7:8]
     packed[0, 7:8, LANES : 2 * LANES] = placed[15:16]
-    packed[0, :, wide:] = jnp.concatenate([gain_part[0:1, :] / gain_ref[...], jnp.zeros((7, model), F32)], axis=0)
+    packed[0, :, wide:] = jnp.zeros((8, quarter), F32)
+    for n in range(4):
+        packed[0, n : n + 1, wide:] = gain_part[n : n + 1, :] / gain_ref[:, n * quarter : (n + 1) * quarter]
     trade = send(packed.at[0], packed.at[1], z_sems.at[0, 0], z_sems.at[1, 0], partner)
     trade.start()
+    plane.pass_on()
     trade.wait()
     over_z[0] = packed[0] + packed[1]
     copies = [
@@ -1372,6 +1371,7 @@
         copy.start()
     line.lead(line.count - 1)
     for step in range(3, line.count):
+        line.relay(step, 0)
         line.relay(step, 1)
     for copy in copies:
         copy.wait()
@@ -1391,7 +1391,7 @@
         piece = pl.ds(pl.multiple_of(i * 32, 32), 32)
         x = x_ref[piece, :].astype(F32)
         r_in = lax.rsqrt(jnp.mean(x * x, axis=-1, keepdims=True) + EPSILON)
-        du = own[piece, :] + in_side[piece, :].astype(F32) + in_up[piece, :].astype(F32)
+        du = own[piece, :] + plane.received(piece)
         e_in = du * gain_ref[...]
         back = r_in * r_in * r_in * jnp.mean(e_in * x, axis=-1, keepdims=True)
         grad_x[piece, :] = d_own_ref[piece, :].astype(F32) + r_in * e_in - x * back
@@ -1412,7 +1412,7 @@
     total, width = dz.shape
     dp_count = lax.axis_size("dp")
     cut = model // dp_count
-    wide = width + 2 * LANES + model
+    wide = width + 2 * LANES + model // 4
     vmem = pl.BlockSpec(memory_space=pltpu.VMEM)
     anywhere = pl.BlockSpec(memory_space=pl.ANY)
     return pl.pallas_call(
@@ -1433,7 +1433,7 @@
             pltpu.VMEM((3 * LANES, model), BF16),
             pltpu.VMEM((total, model), BF16),
             pltpu.VMEM((rows, model), F32),
-            pltpu.VMEM((8, model), F32),
+            pltpu.VMEM((8, model // 4), F32),
             pltpu.VMEM((2, 8, wide), F32),
             pltpu.VMEM((dp_count // 2, 8, wide), F32),
             pltpu.VMEM(gl.shape, BF16),
@@ -1454,7 +1454,7 @@
 def results_kernel(
     own_cols, heads, block_ref, grad_x_ref, first_ref, z_ref, x_ref, sums_ref,
     block_out, grad_x, gw_z, gw_x, gw_b, gw_c, gw_dt, gw_out, conv_w, conv_b, gate, norm, dt_bias, a_log, skip,
-    held_block, held_grad_x, first, z, x, load_sems, sems,
+    held_block, held_grad_x, first, z, x, held_z, held_x, held_out, load_sems, sems,
 ):
     loads, copies = Copies(load_sems), Copies(sems)
     for source, target in ((first_ref, first), (z_ref, z), (x_ref, x), (grad_x_ref, held_grad_x), (block_ref, held_block)):
@@ -1479,7 +1479,9 @@
         gate[:, own] = sums_ref[n, 5:6, :width]
     conv_w[:, inner:] = over_tp(slice(0, 4), slice(width, wide))
     conv_b[:, inner:] = over_tp(slice(4, 5), slice(width, wide))
-    norm[...] = over_tp(slice(0, 1), slice(wide, None))
+    quarter = norm.shape[1] // 4
+    for n in range(4):
+        norm[:, n * quarter : (n + 1) * quarter] = over_tp(slice(n, n + 1), slice(wide, None))
     total_heads = dt_bias.shape[1]
     dt_bias[...] = over_tp(slice(7, 8), slice(0, LANES))[:, :total_heads]
     a_log[...] = over_tp(slice(7, 8), slice(LANES, 2 * LANES))[:, :total_heads]
@@ -1488,22 +1490,24 @@
     copies.start(held_grad_x, grad_x)
     load_block.wait()
     copies.start(held_block, block_out)
-    load_first.wait()
-    gw_out[:taken, :] = first[...].astype(F32)
-    load_z.wait()
-    gw_out[taken:, :] = z[width:, :].astype(F32)
-
-    def turn(source, target):
+
+    def turn(source, held, target):
         def one(i, carry):
             piece = pl.ds(pl.multiple_of(i * CHUNK, CHUNK), CHUNK)
-            target[:, piece] = source[piece, :].T.astype(F32)
+            held[:, piece] = source[piece, :].T.astype(F32)
             return carry
 
         lax.fori_loop(0, width // CHUNK, one, 0)
-
-    turn(z, gw_z)
+        copies.start(held, target)
+
+    load_first.wait()
+    load_z.wait()
+    held_out[:taken, :] = first[...].astype(F32)
+    held_out[taken:, :] = z[width:, :].astype(F32)
+    copies.start(held_out, gw_out)
+    turn(z, held_z, gw_z)
     load_x.wait()
-    turn(x, gw_x)
+    turn(x, held_x, gw_x)
     gw_b[...] = x[width : width + own_cols, :].astype(F32)
     gw_c[...] = x[width + own_cols : width + 2 * own_cols, :].astype(F32)
     gw_dt[...] = x[width + 2 * own_cols : width + 2 * own_cols + heads, :].astype(F32)
@@ -1542,9 +1546,10 @@
         ]
         + [jax.ShapeDtypeStruct(shape, F32) for shape in shapes],
         in_specs=[anywhere] * 5 + [vmem],
-        out_specs=[anywhere] * 2 + [vmem] * len(shapes),
+        out_specs=[anywhere] * 4 + [vmem] * 3 + [anywhere] + [vmem] * 7,
         scratch_shapes=[pltpu.VMEM(large.shape, large.dtype) for large in (block_out, grad_x, first, gw_z, gw_x)]
-        + [pltpu.SemaphoreType.DMA((5,)), pltpu.SemaphoreType.DMA((2,))],
+        + [pltpu.VMEM((cut, width), F32), pltpu.VMEM((cut, width), F32), pltpu.VMEM((width, cut), F32)]
+        + [pltpu.SemaphoreType.DMA((5,)), pltpu.SemaphoreType.DMA((5,))],
         compiler_params=pltpu.CompilerParams(vmem_limit_bytes=60 * 1024 * 1024),
     )(block_out, grad_x, first, gw_z, gw_x, sums)
 
@@ -1577,7 +1582,7 @@
         flat = jnp.concatenate([conv_b, gate_gain, dt_bias, lanes, a_log, lanes, d_skip, lanes])[None, :]
         (
             gathered, zx, bcdt, w_bcdt, mixed, g, yo, yo_t, states, grad_gathered, dyo, coef, pos, prm, head_prm, expand,
-            cross,
+            pre, cross,
         ) = first_part(
             inner, heads, own_cols, x_in, norm_gain[None, :], small_weights, conv_w.T, flat, doc_lens, w_z, w_x, w_out,
             d_out,
@@ -1633,7 +1638,7 @@
         expand = (
             (jnp.arange(2 * LANES) % LANES)[:, None] == (jnp.arange(width) // head_size)[None, :]
         ).astype(BF16)
-        mixed, g, g_sum, states = mixer_forward(width, zx, bcdt, pos, prm, head_prm, expand)
+        mixed, g, g_sum, states, pre = mixer_forward(width, zx, bcdt, pos, prm, head_prm, expand)
         grad_gathered = lax.all_gather(d_out, "tp", axis=0, tiled=True)
         dyo = dot(grad_gathered, w_out, CONTRACT_LAST).astype(BF16)
         eg_sum = jnp.sum(dyo.astype(F32) * gain_own[None, :] * g, axis=1)
@@ -1648,7 +1653,7 @@
             inner, x_in, cross, yo, yo_t, grad_gathered, w_out, dyo, g, mixed, zx, coef, prm, gathered
         )
         gw_z, grad_xs, grad_bcdt, gl, small = third_part(
-            own_cols, heads, zx, bcdt, pos, prm, head_prm, expand, mixed, states, dy, gathered, gz
+            own_cols, heads, zx, bcdt, pos, prm, head_prm, expand, mixed, states, dy, pre, gathered, gz
         )
         gw_x, grad_x, sums = fourth_part(
             heads, x_in, d_out, norm_gain[None, :], small, gain_sum, expand, dz, grad_xs, grad_bcdt, w_z, w_x, w_bcdt,
@@ -1682,7 +1687,7 @@
         grad_w_z = scatter_dp(dot(gathered, dz, CONTRACT_FIRST))
         block_out = (x_float + scatter_tp(dot(yo, w_out))).astype(BF16)
         grad_xs, grad_bcdt, small = mixer_backward(
-            width, zx, bcdt, pos, prm, head_prm, expand, mixed, states, dy
+            width, pre, zx, bcdt, pos, prm, head_prm, expand, mixed, states, dy
         )
         small = small.at[5, :width].set(gain_sum)
         d_bc = grad_bcdt[:, : 2 * state_size]

time: 249 us -> 240 us (0.964)
  Pallas kernels: 243 us -> 234 us
    pallas_call x1, Pallas kernels: 53.2 us -> 48.1 us  [third_part(): pl.pallas_call(functools.partial(third_kernel, own_cols, heads), out_shap...]
    pallas_call x1, Pallas kernels: 53.6 us -> 50.4 us  [fourth_part(): pl.pallas_call(functools.partial(fourth_kernel, heads), out_shape=(jax.Sh...]
where the time goes in v3:
time: 240 us; the launch traced here: 239 us
  Pallas kernels  234 us (98%)
  other arithmetic  3.12 us (1%)
    pallas_call x1, Pallas kernels, first_part(): pl.pallas_call(functools.partial(first_kernel, inner, heads, own_cols), o...  83.1 us
    pallas_call x1, Pallas kernels, fourth_part(): pl.pallas_call(functools.partial(fourth_kernel, heads), out_shape=(jax.Sh...  50.4 us
    pallas_call x1, Pallas kernels, third_part(): pl.pallas_call(functools.partial(third_kernel, own_cols, heads), out_shap...  48.1 us
    pallas_call x1, Pallas kernels, second_part(): pl.pallas_call(functools.partial(second_kernel, inner), out_shape=(jax.Sh...  45.8 us
    pallas_call x1, Pallas kernels, results_part(): pl.pallas_call(functools.partial(results_kernel, own_cols, heads), out_sh...  6.48 us

profile of v3, /device:TPU:0, one launch (start us, length us, event | category | flops | bytes accessed | tf_op | source)
XLA Modules:
  0.0 239.2 jit_solution(6774826424699270351)
XLA Ops:
  0.7 0.8 concatenate.7
  1.5 0.6 broadcast_in_dim.12.flat_ref
  2.1 1.8 maximum_bitcast_fusion.small_ref
  3.9 83.1 %shard_map.271 = (bf16[1024,2048]{1,0:T(8,128)(2,1)}, bf16[1024,2048]{1,0:T(8,128)(2,1)}, bf16[1024,384]{1,0:T(8,128)(2,1)}, bf16[384,2048]{1,0:T(8,128)(2,1)}, ...) custom-call(bf16[256,2048]{1,0:T(8,128)(2,1)} %x_ref.5, ...), custom_call_target="tpu_custom_call" | custom-call | tf_op jit(solution)/shard_map/pallas_call | solution.py:656
  87.0 45.8 %shard_map.272 = (bf16[256,2048]{1,0:T(8,128)(2,1)}, bf16[896,256]{1,0:T(8,128)(2,1)}, bf16[1024,1024]{1,0:T(8,128)(2,1)}, bf16[1024,1024]{1,0:T(8,128)(2,1)}, b...) custom-call(bf16[256,2048]{1,0:T(8,128)(2,1)} %x_ref.5, f32[8,1024]{1,0:T(8,128)} %get-tuple-element.62.cross_ref, ...), custom_call_target="tpu_custom_call" | custom-call | tf_op jit(solution)/shard_map/pallas_call | solution.py:1060
  132.8 48.1 %shard_map.273 = (bf16[1152,256]{1,0:T(8,128)(2,1)}, bf16[1024,1024]{1,0:T(8,128)(2,1)}, bf16[1024,384]{1,0:T(8,128)(2,1)}, bf16[4,1152,256]{2,1,0:T(8,128)(2,1)}, f32[8,1280]{1,0:T(8,128)}) custom-call(bf16[1024,2048]{1,0:T(8,128)(2,1)} %get-tuple-element.69.zx_ref, bf16[1024,384]{1,0:T(8,128)(2,1)} %get-tuple-element.74.bcdt_ref, ...), custom_call_target="tpu_custom_call" | custom-call | tf_op jit(solution)/shard_map/pallas_call | solution.py:1231
  180.9 50.4 %shard_map.274 = (bf16[1152,256]{1,0:T(8,128)(2,1)}, f32[256,2048]{1,0:T(8,128)}, f32[4,8,1792]{2,1,0:T(8,128)}) custom-call(bf16[256,2048]{1,0:T(8,128)(2,1)} %x_ref.5, bf16[256,2048]{1,0:T(8,128)(2,1)} %d_own_ref.3, f32[1,2048]{1,0:T(1,128)} %bitcast.15, f32[8,1280]{1,0:T(8,128)} %get-tuple-element.82.small_ref, f32[8,1024]{1,0:T(8,128)} %get-tuple-element.83.gain_sum_ref, ...), custom_call_target="tpu_custom_call" | custom-call | tf_op jit(solution)/shard_map/pallas_call | solution.py:1418
  231.3 6.5 %shard_map.275 = (bf16[256,2048]{1,0:T(8,128)(2,1)}, f32[256,2048]{1,0:T(8,128)}, f32[256,1024]{1,0:T(8,128)}, f32[256,1024]{1,0:T(8,128)}, f32[32,256]{1,0:T(8,...) custom-call(bf16[256,2048]{1,0:T(8,128)(2,1)} %get-tuple-element.73., ...), custom_call_target="tpu_custom_call" | custom-call | tf_op jit(solution)/shard_map/pallas_call | solution.py:1541
  237.8 1.4 reduce
  (1 shorter events, 0.0 us)

commit v4 on v3

--- a/solution.py
+++ b/solution.py
@@ -451,9 +451,9 @@
 
 
 def first_kernel(
-    inner, heads, own_cols, x_ref, gain_ref, small_ref, taps_ref, flat_ref, lens_ref, wz_ref, wx_ref, w_out_ref, d_own_ref,
+    inner, heads, own_cols, x_ref, gain_ref, wb_ref, wc_ref, wdt_ref, taps_ref, flat_ref, lens_ref, wz_ref, wx_ref, w_out_ref, d_own_ref,
     u_out, zx_out, bcdt_out, wbc_out, mixed_out, g_out, yo_out, yo_t_out, state_out, d_out, dyo_out, coef_out, pos_out,
-    prm_out, head_out, expand_out, pre_out, cross_out,
+    prm_out, head_out, expand_out, pre_out, cross_out, branch_out,
     weights, w_out, u, zx, bcdt, wbc, mixed, g, yo, yo_t, states, d, dyo, coef, pos, prm, head, expand, pre, ext, state, sums,
     acc, sems, sum_sems, load_sems, store_sems,
 ):
@@ -484,9 +484,9 @@
         stores.append(copy)
 
     bc_own = pl.ds(pl.multiple_of(parity * LANES, LANES), LANES)
-    wbc[pl.ds(pl.multiple_of(parity * LANES + me * own_cols, own_cols), own_cols), :] = small_ref[
-        pl.ds(pl.multiple_of(parity * own_cols, own_cols), own_cols), :
-    ]
+    wbc[pl.ds(pl.multiple_of(parity * LANES + me * own_cols, own_cols), own_cols), :] = jnp.where(
+        parity == 0, wb_ref[...], wc_ref[...]
+    )
     greet([{"tp": side}, {"tp": up}, {"tp": far}, partner])
     small_gather = Gather(wbc.at[bc_own], own_cols, sems.at[0], sems.at[1])
     small_gather.start()
@@ -505,7 +505,7 @@
     gather.start()
     gather.start_rest()
     wbc[2 * LANES :, :] = jnp.zeros((LANES, model), BF16)
-    wbc[2 * LANES : 2 * LANES + heads, :] = small_ref[2 * own_cols :, :]
+    wbc[2 * LANES : 2 * LANES + heads, :] = wdt_ref[...]
     set_up(width, heads, inner, taps_ref, flat_ref, lens_ref, prm, head, expand, pos)
     keep(pos, pos_out)
     keep(prm, prm_out)
@@ -612,9 +612,26 @@
     keep(coef, coef_out)
     keep(yo, yo_out)
     keep(yo_t, yo_t_out)
+    branch = weights.at[:total, :]
+
+    def out_block(place):
+        piece = block(place)
+
+        def tile(n, carry):
+            columns = pl.ds(pl.multiple_of(n * 512, 512), 512)
+            branch[piece, columns] = dot(yo[piece, :], w_out[:, columns]).astype(BF16)
+            return carry
+
+        lax.fori_loop(0, model // 512, tile, 0)
+        keep(branch.at[piece], branch_out.at[piece])
+
+    out_block(far)
+    out_block(side)
     d_gather.neighbours()
     back_to_heads(side)
     back_to_heads(up)
+    out_block(up)
+    out_block(me)
     d_gather.finish()
     keep(d, d_out)
     back_to_heads(far)
@@ -626,7 +643,7 @@
         copy.wait()
 
 
-def first_part(inner, heads, own_cols, x_in, gain, small, taps, flat, lens, w_z, w_x, w_out, d_out):
+def first_part(inner, heads, own_cols, x_in, gain, w_b, w_c, w_dt, taps, flat, lens, w_z, w_x, w_out, d_out):
     rows, model = x_in.shape
     total = 4 * rows
     width = w_z.shape[1]
@@ -652,12 +669,12 @@
         ((2 * LANES, width), BF16),
         ((total, width + 2 * LANES), F32),
     ]
-    cross = jax.ShapeDtypeStruct((8, total), F32)
+    cross = [jax.ShapeDtypeStruct((8, total), F32), jax.ShapeDtypeStruct((total, model), BF16)]
     return pl.pallas_call(
         functools.partial(first_kernel, inner, heads, own_cols),
-        out_shape=[jax.ShapeDtypeStruct(*result) for result in results] + [cross],
-        in_specs=[vmem] * 5 + [pl.BlockSpec(memory_space=pltpu.SMEM)] + [anywhere] * 4,
-        out_specs=[anywhere] * (len(results) + 1),
+        out_shape=[jax.ShapeDtypeStruct(*result) for result in results] + cross,
+        in_specs=[vmem] * 7 + [pl.BlockSpec(memory_space=pltpu.SMEM)] + [anywhere] * 4,
+        out_specs=[anywhere] * (len(results) + 2),
         scratch_shapes=[pltpu.VMEM((model, 2 * width), BF16), pltpu.VMEM((width, model), BF16)]
         + [pltpu.VMEM(*result) for result in results]
         + [
@@ -668,12 +685,12 @@
             pltpu.SemaphoreType.DMA((7, 8)),
             pltpu.SemaphoreType.DMA((2, 3)),
             pltpu.SemaphoreType.DMA((4,)),
-            pltpu.SemaphoreType.DMA((24,)),
+            pltpu.SemaphoreType.DMA((30,)),
         ],
         compiler_params=pltpu.CompilerParams(
             collective_id=0, has_side_effects=True, vmem_limit_bytes=60 * 1024 * 1024
         ),
-    )(x_in, gain, small, taps, flat, lens, w_z, w_x, w_out, d_out)
+    )(x_in, gain, w_b, w_c, w_dt, taps, flat, lens, w_z, w_x, w_out, d_out)
 
 
 def add_into(target, other):
@@ -887,19 +904,28 @@
 
 
 def second_kernel(
-    inner, x_ref, cross_ref, yo_ref, yo_t_ref, d_ref, w_out_ref, dyo_ref, g_ref, mixed_ref, zx_ref, coef_ref, prm_ref,
+    inner, x_ref, cross_ref, branch_ref, yo_t_ref, d_ref, dyo_ref, g_ref, mixed_ref, zx_ref, coef_ref, prm_ref,
     u_ref, block_out, gw_out, dz_out, dy_out, gz_out, gain_out,
-    yo, yo_t, d, w_out, dyo, g, mixed, z, coef, own, gz, parts, pair, pair_sems, gz_pair, gz_pair_sems,
+    dz, yo_t, d, dyo, g, mixed, z, coef, own, gz, parts, pair, pair_sems, gz_pair, gz_pair_sems,
     right, left, right_sems, left_sems,
     away, to_side, to_up, in_far, in_side, in_up, plane_sems, cross, cross_sems, load_sems, store_sems,
 ):
     rows, model = x_ref.shape
-    total, width = yo.shape
+    total, width = dz.shape
     taken = parts.shape[1]
     me, side, up, far = tp_places()
     loads, stores = Copies(load_sems), Copies(store_sems)
-    load_yo = loads.start(yo_ref, yo)
-    load_w = loads.start(w_out_ref, w_out)
+    quarter = model // 4
+
+    def load_block(place, target):
+        piece = pl.ds(pl.multiple_of(place * rows, rows), rows)
+        return [
+            loads.start(branch_ref.at[piece, n * quarter : (n + 1) * quarter], target.at[n]) for n in range(4)
+        ]
+
+    load_far = load_block(far, away)
+    load_yo_t = loads.start(yo_t_ref, yo_t)
+    load_d = loads.start(d_ref, d)
     cores = PairSum(parts, pair, pair_sems)
     gz_cores = PairSum(gz, gz_pair, gz_pair_sems)
     line = LineSum(parts, cores.ours, right, left, right_sems, left_sems)
@@ -912,32 +938,13 @@
     for copy in crossing:
         copy.start()
 
-    quarter = model // 4
-
-    def out_block(place, target, started=None):
-        piece = pl.ds(pl.multiple_of(place * rows, rows), rows)
-
-        def two(m, carry):
-            for odd in range(2):
-                n = 2 * m + odd
-                columns = pl.ds(pl.multiple_of(n * quarter, quarter), quarter)
-                value = dot(yo[piece, :], w_out[:, columns])
-                if started is None:
-                    target[:, columns] = value
-                else:
-                    target[n] = value.astype(BF16)
-                    started(n, odd)
-            return carry
-
-        lax.fori_loop(0, 2, two, 0)
-
-    load_yo.wait()
-    load_w.wait()
-    load_yo_t = loads.start(yo_t_ref, yo_t)
-    load_d = loads.start(d_ref, d)
-    out_block(far, away, plane.start_far)
+    for n, copy in enumerate(load_far):
+        copy.wait()
+        plane.start_far(n, n % 2)
     load_yo_t.wait()
     load_d.wait()
+    load_side, load_up = load_block(side, to_side), load_block(up, to_up)
+    load_own = loads.start(branch_ref.at[pl.ds(pl.multiple_of(me * rows, rows), rows)], own)
     rest = [
         loads.start(dyo_ref, dyo),
         loads.start(g_ref, g),
@@ -971,13 +978,15 @@
     for z_chunk in order[2:]:
         cores.merge(z_chunk)
     line.lead(*range(2, line.count))
-    out_block(side, to_side, functools.partial(plane.start_near, 0))
-    out_block(up, to_up, functools.partial(plane.start_near, 1))
+    for copy in load_side + load_up:
+        copy.wait()
+    for n in range(4):
+        plane.start_near(n % 2, n, n % 2)
     line.relay(2, 0)
     plane.pass_on()
     lax.fori_loop(0, parts.shape[0], left_over, 0)
     load_u = loads.start(u_ref, d)
-    out_block(me, own)
+    load_own.wait()
     line.relay(2, 1)
     for copy in rest:
         copy.wait()
@@ -998,15 +1007,15 @@
         scaled = scale * dyo_piece
         dg = scaled * prm_ref[5:6, :width] - g_piece * back
         gain_out[0:1, :] += jnp.sum(scaled * g_piece, axis=0, keepdims=True)
-        dz = dg * mixed[piece, :] * (sig * (1.0 + z_piece * (1.0 - sig)))
-        yo[piece, :] = dz.astype(BF16)
-        yo_t[:, piece] = dz.T.astype(BF16)
+        d_z = dg * mixed[piece, :] * (sig * (1.0 + z_piece * (1.0 - sig)))
+        dz[piece, :] = d_z.astype(BF16)
+        yo_t[:, piece] = d_z.T.astype(BF16)
         dyo[piece, :] = (dg * (z_piece * sig)).astype(BF16)
         return carry
 
     chunks = total // CHUNK
     lax.fori_loop(0, chunks, gate_back, 0)
-    stores.start(yo, dz_out)
+    stores.start(dz, dz_out)
     stores.start(dyo, dy_out)
     for step in range(3, line.count):
         line.relay(step, 0)
@@ -1038,7 +1047,7 @@
 
     def add_own(i, carry):
         piece = pl.ds(pl.multiple_of(i * 32, 32), 32)
-        total_out = own[piece, :] + plane.received(piece)
+        total_out = own[piece, :].astype(F32) + plane.received(piece)
         block_out[piece, :] = (x_ref[piece, :].astype(F32) + total_out).astype(BF16)
         return carry
 
@@ -1049,9 +1058,9 @@
         copy.wait()
 
 
-def second_part(inner, x_in, cross, yo, yo_t, d, w_out, dyo, g, mixed, zx, coef, prm, u):
+def second_part(inner, x_in, cross, branch, yo_t, d, dyo, g, mixed, zx, coef, prm, u):
     rows, model = x_in.shape
-    total, width = yo.shape
+    width, total = yo_t.shape
     dp_count = lax.axis_size("dp")
     cut = model // dp_count
     kept = width // 8
@@ -1067,19 +1076,18 @@
             jax.ShapeDtypeStruct((dp_count // 2, width + kept, cut), BF16),
             jax.ShapeDtypeStruct((8, width), F32),
         ),
-        in_specs=[vmem] * 2 + [anywhere] * 9 + [vmem, anywhere],
+        in_specs=[vmem] * 2 + [anywhere] * 8 + [vmem, anywhere],
         out_specs=(vmem, vmem, anywhere, anywhere, anywhere, vmem),
         scratch_shapes=[
             pltpu.VMEM((total, width), BF16),
             pltpu.VMEM((width, total), BF16),
             pltpu.VMEM((total, model), BF16),
-            pltpu.VMEM((width, model), BF16),
             pltpu.VMEM((total, width), BF16),
             pltpu.VMEM((total, width), F32),
             pltpu.VMEM((total, width), F32),
             pltpu.VMEM((total, width), BF16),
             pltpu.VMEM((total, LANES), F32),
-            pltpu.VMEM((rows, model), F32),
+            pltpu.VMEM((rows, model), BF16),
             pltpu.VMEM((dp_count, width + kept, cut), BF16),
             pltpu.VMEM((dp_count, width - kept, cut), BF16),
         ]
@@ -1090,13 +1098,13 @@
         + [
             pltpu.VMEM((3, 8, total), F32),
             pltpu.SemaphoreType.DMA((2, 3)),
-            pltpu.SemaphoreType.DMA((10,)),
+            pltpu.SemaphoreType.DMA((22,)),
             pltpu.SemaphoreType.DMA((2 + dp_count // 2,)),
         ],
         compiler_params=pltpu.CompilerParams(
             collective_id=1, has_side_effects=True, vmem_limit_bytes=60 * 1024 * 1024
         ),
-    )(x_in, cross, yo, yo_t, d, w_out, dyo, g, mixed, zx, coef, prm, u)
+    )(x_in, cross, branch, yo_t, d, dyo, g, mixed, zx, coef, prm, u)
 
 
 def third_kernel(
@@ -1175,7 +1183,7 @@
         copies.append(send(bc_in.at[n], bc_in.at[3 + n], bc_sems.at[0, n], bc_sems.at[1, n], {"tp": peer}))
         copies[-1].start()
     own_bc = columns_of(me)
-    dx_t[width:, :] = jnp.zeros((LANES, total), BF16)
+    dx_t[width:, :] = jnp.zeros((dx_t.shape[0] - width, total), BF16)
     dx_t[width + 2 * own_cols : width + 2 * own_cols + heads, :] = dbcdt[:, 2 * LANES :].astype(F32).T[:heads, :].astype(
         BF16
     )
@@ -1226,6 +1234,7 @@
     model = u.shape[1]
     dp_count = lax.axis_size("dp")
     cut = model // dp_count
+    all_rows = width + -(-(2 * own_cols + heads) // 32) * 32
     vmem = pl.BlockSpec(memory_space=pltpu.VMEM)
     anywhere = pl.BlockSpec(memory_space=pl.ANY)
     return pl.pallas_call(
@@ -1234,7 +1243,7 @@
             jax.ShapeDtypeStruct(gz.shape[1:], BF16),
             jax.ShapeDtypeStruct((total, width), BF16),
             jax.ShapeDtypeStruct((total, 3 * LANES), BF16),
-            jax.ShapeDtypeStruct((dp_count // 2, width + LANES, cut), BF16),
+            jax.ShapeDtypeStruct((dp_count // 2, all_rows, cut), BF16),
             jax.ShapeDtypeStruct((8, width + 2 * LANES), F32),
         ),
         in_specs=[anywhere] * 2 + [vmem] * 4 + [anywhere] * 6,
@@ -1249,14 +1258,14 @@
             pltpu.VMEM((total, model), BF16),
             pltpu.VMEM((total, width), BF16),
             pltpu.VMEM((total, 3 * LANES), BF16),
-            pltpu.VMEM((width + LANES, total), BF16),
-            pltpu.VMEM((dp_count, width + LANES, cut), BF16),
+            pltpu.VMEM((all_rows, total), BF16),
+            pltpu.VMEM((dp_count, all_rows, cut), BF16),
             pltpu.VMEM((6, 2 * own_cols, total), BF16),
             pltpu.VMEM((LANES, width), F32),
             pltpu.VMEM((CHUNK + 8, width + 2 * LANES), F32),
             pltpu.VMEM((CHUNK + 8, LANES), jnp.int32),
         ]
-        + pair_scratch(dp_count, (width + LANES, cut))
+        + pair_scratch(dp_count, (all_rows, cut))
         + [pltpu.VMEM(gz.shape, BF16)]
         + line_scratch(dp_count, gz.shape[1:])
         + [pltpu.SemaphoreType.DMA((2, 3)), pltpu.SemaphoreType.DMA((14,)), pltpu.SemaphoreType.DMA((2 + dp_count // 2,))],
@@ -1515,10 +1524,9 @@
         copy.wait()
 
 
-def results_part(own_cols, heads, block_out, grad_x, first, gw_z, gw_x, sums):
+def results_part(own_cols, heads, width, block_out, grad_x, first, gw_z, gw_x, sums):
     cut = first.shape[1]
     count = sums.shape[0]
-    width = gw_x.shape[0] - LANES
     inner = width * count
     model = grad_x.shape[1]
     vmem = pl.BlockSpec(memory_space=pltpu.VMEM)
@@ -1582,10 +1590,10 @@
         flat = jnp.concatenate([conv_b, gate_gain, dt_bias, lanes, a_log, lanes, d_skip, lanes])[None, :]
         (
             gathered, zx, bcdt, w_bcdt, mixed, g, yo, yo_t, states, grad_gathered, dyo, coef, pos, prm, head_prm, expand,
-            pre, cross,
+            pre, cross, branch,
         ) = first_part(
-            inner, heads, own_cols, x_in, norm_gain[None, :], small_weights, conv_w.T, flat, doc_lens, w_z, w_x, w_out,
-            d_out,
+            inner, heads, own_cols, x_in, norm_gain[None, :], w_b.T, w_c.T, w_dt.T, conv_w.T, flat, doc_lens, w_z, w_x,
+            w_out, d_out,
         )
         gain_own = prm[5, :width]
     else:
@@ -1650,7 +1658,7 @@
 
     if in_planes:
         block_out, gw_first, dz, dy, gz, gain_sum = second_part(
-            inner, x_in, cross, yo, yo_t, grad_gathered, w_out, dyo, g, mixed, zx, coef, prm, gathered
+            inner, x_in, cross, branch, yo_t, grad_gathered, dyo, g, mixed, zx, coef, prm, gathered
         )
         gw_z, grad_xs, grad_bcdt, gl, small = third_part(
             own_cols, heads, zx, bcdt, pos, prm, head_prm, expand, mixed, states, dy, pre, gathered, gz
@@ -1663,7 +1671,7 @@
             block_out, grad_x, gw_z, gw_x, gw_b, gw_c, gw_dt, gw_out, g_conv_w, g_conv_b, g_gate, g_norm, g_dt_bias,
             g_a_log, g_skip
         ) = results_part(
-            own_cols, heads, block_out, grad_x, gw_first, gw_z, gw_x, sums
+            own_cols, heads, width, block_out, grad_x, gw_first, gw_z, gw_x, sums
         )
         return (
             block_out, grad_x, g_norm[0], gw_z, gw_x, gw_b.T, gw_c.T, gw_dt.T, g_conv_w.T, g_conv_b[0], g_dt_bias[0],

time: 240 us -> 235 us (0.979)
  Pallas kernels: 234 us -> 230 us
    pallas_call x1, Pallas kernels: 45.8 us -> 41.3 us  [second_part(): pl.pallas_call(functools.partial(second_kernel, inner), out_shape=(jax.Sh...]
where the time goes in v4:
time: 235 us; the launch traced here: 233 us
  Pallas kernels  230 us (98%)
    pallas_call x1, Pallas kernels, first_part(): pl.pallas_call(functools.partial(first_kernel, inner, heads, own_cols), o...  84.5 us
    pallas_call x1, Pallas kernels, fourth_part(): pl.pallas_call(functools.partial(fourth_kernel, heads), out_shape=(jax.Sh...  49.5 us
    pallas_call x1, Pallas kernels, third_part(): pl.pallas_call(functools.partial(third_kernel, own_cols, heads), out_shap...  48.1 us
    pallas_call x1, Pallas kernels, second_part(): pl.pallas_call(functools.partial(second_kernel, inner), out_shape=(jax.Sh...  41.3 us
    pallas_call x1, Pallas kernels, results_part(): pl.pallas_call(functools.partial(results_kernel, own_cols, heads), out_sh...  6.48 us

profile of v4, /device:TPU:0, one launch (start us, length us, event | category | flops | bytes accessed | tf_op | source)
XLA Modules:
  0.0 233.5 jit_solution(13652141582947076865)
XLA Ops:
  0.7 0.8 concatenate.3
  1.5 0.6 broadcast_in_dim.12.flat_ref
  2.1 84.5 %shard_map.271 = (bf16[1024,2048]{1,0:T(8,128)(2,1)}, bf16[1024,2048]{1,0:T(8,128)(2,1)}, bf16[1024,384]{1,0:T(8,128)(2,1)}, bf16[384,2048]{1,0:T(8,128)(2,1)}, ...) custom-call(bf16[256,2048]{1,0:T(8,128)(2,1)} %x_ref.5, ...), custom_call_target="tpu_custom_call" | custom-call | tf_op jit(solution)/shard_map/pallas_call | solution.py:673
  86.6 41.3 %shard_map.272 = (bf16[256,2048]{1,0:T(8,128)(2,1)}, bf16[896,256]{1,0:T(8,128)(2,1)}, bf16[1024,1024]{1,0:T(8,128)(2,1)}, bf16[1024,1024]{1,0:T(8,128)(2,1)}, b...) custom-call(bf16[256,2048]{1,0:T(8,128)(2,1)} %x_ref.5, f32[8,1024]{1,0:T(8,128)} %get-tuple-element.62.cross_ref, ...), custom_call_target="tpu_custom_call" | custom-call | tf_op jit(solution)/shard_map/pallas_call | solution.py:1069
  128.0 48.1 %shard_map.273 = (bf16[1152,256]{1,0:T(8,128)(2,1)}, bf16[1024,1024]{1,0:T(8,128)(2,1)}, bf16[1024,384]{1,0:T(8,128)(2,1)}, bf16[4,1120,256]{2,1,0:T(8,128)(2,1)}, f32[8,1280]{1,0:T(8,128)}) custom-call(bf16[1024,2048]{1,0:T(8,128)(2,1)} %get-tuple-element.69.zx_ref, bf16[1024,384]{1,0:T(8,128)(2,1)} %get-tuple-element.74.bcdt_ref, ...), custom_call_target="tpu_custom_call" | custom-call | tf_op jit(solution)/shard_map/pallas_call | solution.py:1240
  176.1 49.5 %shard_map.274 = (bf16[1120,256]{1,0:T(8,128)(2,1)}, f32[256,2048]{1,0:T(8,128)}, f32[4,8,1792]{2,1,0:T(8,128)}) custom-call(bf16[256,2048]{1,0:T(8,128)(2,1)} %x_ref.5, bf16[256,2048]{1,0:T(8,128)(2,1)} %d_own_ref.3, f32[1,2048]{1,0:T(1,128)} %bitcast.19, f32[8,1280]{1,0:T(8,128)} %get-tuple-element.82.small_ref, f32[8,1024]{1,0:T(8,128)} %get-tuple-element.83.gain_sum_ref, ...), custom_call_target="tpu_custom_call" | custom-call | tf_op jit(solution)/shard_map/pallas_call | solution.py:1427
  225.6 6.5 %shard_map.275 = (bf16[256,2048]{1,0:T(8,128)(2,1)}, f32[256,2048]{1,0:T(8,128)}, f32[256,1024]{1,0:T(8,128)}, f32[256,1024]{1,0:T(8,128)}, f32[32,256]{1,0:T(8,...) custom-call(bf16[256,2048]{1,0:T(8,128)(2,1)} %get-tuple-element.73., ...), custom_call_target="tpu_custom_call" | custom-call | tf_op jit(solution)/shard_map/pallas_call | solution.py:1549
  232.1 1.4 reduce
  (1 shorter events, 0.0 us)

commit v5 on v4

--- a/solution.py
+++ b/solution.py
@@ -1462,32 +1462,42 @@
 
 def results_kernel(
     own_cols, heads, block_ref, grad_x_ref, first_ref, z_ref, x_ref, sums_ref,
-    block_out, grad_x, gw_z, gw_x, gw_b, gw_c, gw_dt, gw_out, conv_w, conv_b, gate, norm, dt_bias, a_log, skip,
-    held_block, held_grad_x, first, z, x, held_z, held_x, held_out, load_sems, sems,
+    block_out, grad_x_out, gw_z_out, gw_x_out, gw_b_out, gw_c_out, gw_dt_out, gw_out_out, conv_w_out, conv_b_out, gate_out,
+    norm_out, dt_bias_out, a_log_out, skip_out,
+    block, grad_x, first, z, x, sums, gw_z, gw_x, gw_b, gw_c, gw_dt, gw_out, conv_w, conv_b, gate, norm, dt_bias, a_log,
+    skip, load_sems, sems,
 ):
     loads, copies = Copies(load_sems), Copies(sems)
-    for source, target in ((first_ref, first), (z_ref, z), (x_ref, x), (grad_x_ref, held_grad_x), (block_ref, held_block)):
+    for source, target in (
+        (sums_ref, sums), (first_ref, first), (z_ref, z), (x_ref, x), (grad_x_ref, grad_x), (block_ref, block)
+    ):
         loads.start(source, target)
-    load_first, load_z, load_x, load_grad_x, load_block = loads.started
+    load_sums, load_first, load_z, load_x, load_grad_x, load_block = loads.started
     taken = first.shape[0]
     width = gw_z.shape[1]
-    count = sums_ref.shape[0]
+    count = sums.shape[0]
     inner = gate.shape[1]
     wide = width + 2 * LANES
 
     def over_tp(rows, columns):
-        total = sums_ref[0, rows, columns]
+        total = sums[0, rows, columns]
         for n in range(1, count):
-            total = total + sums_ref[n, rows, columns]
+            total = total + sums[n, rows, columns]
         return total
 
+    load_sums.wait()
+    tiles = width // LANES
     for n in range(count):
         own = slice(n * width, (n + 1) * width)
-        conv_w[:, own] = sums_ref[n, 0:4, :width]
-        conv_b[:, own] = sums_ref[n, 4:5, :width]
-        gate[:, own] = sums_ref[n, 5:6, :width]
+        conv_w[:, own] = sums[n, 0:4, :width]
+        gate[:, own] = sums[n, 5:6, :width]
+        for tile in range(tiles):
+            row = n * tiles + tile
+            conv_b[row : row + 1, :] = sums[n, 4:5, tile * LANES : (tile + 1) * LANES]
     conv_w[:, inner:] = over_tp(slice(0, 4), slice(width, wide))
-    conv_b[:, inner:] = over_tp(slice(4, 5), slice(width, wide))
+    for tile in range(2):
+        row = count * tiles + tile
+        conv_b[row : row + 1, :] = over_tp(slice(4, 5), slice(width + tile * LANES, width + (tile + 1) * LANES))
     quarter = norm.shape[1] // 4
     for n in range(4):
         norm[:, n * quarter : (n + 1) * quarter] = over_tp(slice(n, n + 1), slice(wide, None))
@@ -1495,10 +1505,11 @@
     dt_bias[...] = over_tp(slice(7, 8), slice(0, LANES))[:, :total_heads]
     a_log[...] = over_tp(slice(7, 8), slice(LANES, 2 * LANES))[:, :total_heads]
     skip[...] = over_tp(slice(6, 7), slice(width, width + LANES))[:, :total_heads]
-    load_grad_x.wait()
-    copies.start(held_grad_x, grad_x)
-    load_block.wait()
-    copies.start(held_block, block_out)
+    for source, target in (
+        (conv_w, conv_w_out), (conv_b, conv_b_out), (gate, gate_out), (norm, norm_out), (dt_bias, dt_bias_out),
+        (a_log, a_log_out), (skip, skip_out),
+    ):
+        copies.start(source, target)
 
     def turn(source, held, target):
         def one(i, carry):
@@ -1511,15 +1522,21 @@
 
     load_first.wait()
     load_z.wait()
-    held_out[:taken, :] = first[...].astype(F32)
-    held_out[taken:, :] = z[width:, :].astype(F32)
-    copies.start(held_out, gw_out)
-    turn(z, held_z, gw_z)
+    gw_out[:taken, :] = first[...].astype(F32)
+    gw_out[taken:, :] = z[width:, :].astype(F32)
+    copies.start(gw_out, gw_out_out)
+    load_grad_x.wait()
+    copies.start(grad_x, grad_x_out)
+    load_block.wait()
+    copies.start(block, block_out)
+    turn(z, gw_z, gw_z_out)
     load_x.wait()
-    turn(x, held_x, gw_x)
     gw_b[...] = x[width : width + own_cols, :].astype(F32)
     gw_c[...] = x[width + own_cols : width + 2 * own_cols, :].astype(F32)
     gw_dt[...] = x[width + 2 * own_cols : width + 2 * own_cols + heads, :].astype(F32)
+    for source, target in ((gw_b, gw_b_out), (gw_c, gw_c_out), (gw_dt, gw_dt_out)):
+        copies.start(source, target)
+    turn(x, gw_x, gw_x_out)
     for copy in copies.started:
         copy.wait()
 
@@ -1529,7 +1546,6 @@
     count = sums.shape[0]
     inner = width * count
     model = grad_x.shape[1]
-    vmem = pl.BlockSpec(memory_space=pltpu.VMEM)
     anywhere = pl.BlockSpec(memory_space=pl.ANY)
     shapes = [
         (cut, width),
@@ -1539,27 +1555,25 @@
         (heads, cut),
         (width, cut),
         (4, inner + 2 * LANES),
-        (1, inner + 2 * LANES),
+        (inner // LANES + 2, LANES),
         (1, inner),
         (1, model),
         (1, heads * count),
         (1, heads * count),
         (1, heads * count),
     ]
+    sources = (block_out, grad_x, first, gw_z, gw_x, sums)
     return pl.pallas_call(
         functools.partial(results_kernel, own_cols, heads),
-        out_shape=[
-            jax.ShapeDtypeStruct(block_out.shape, BF16),
-            jax.ShapeDtypeStruct(grad_x.shape, F32),
-        ]
+        out_shape=[jax.ShapeDtypeStruct(large.shape, large.dtype) for large in sources[:2]]
         + [jax.ShapeDtypeStruct(shape, F32) for shape in shapes],
-        in_specs=[anywhere] * 5 + [vmem],
-        out_specs=[anywhere] * 4 + [vmem] * 3 + [anywhere] + [vmem] * 7,
-        scratch_shapes=[pltpu.VMEM(large.shape, large.dtype) for large in (block_out, grad_x, first, gw_z, gw_x)]
-        + [pltpu.VMEM((cut, width), F32), pltpu.VMEM((cut, width), F32), pltpu.VMEM((width, cut), F32)]
-        + [pltpu.SemaphoreType.DMA((5,)), pltpu.SemaphoreType.DMA((5,))],
+        in_specs=[anywhere] * len(sources),
+        out_specs=[anywhere] * (2 + len(shapes)),
+        scratch_shapes=[pltpu.VMEM(large.shape, large.dtype) for large in sources]
+        + [pltpu.VMEM(shape, F32) for shape in shapes]
+        + [pltpu.SemaphoreType.DMA((len(sources),)), pltpu.SemaphoreType.DMA((2 + len(shapes),))],
         compiler_params=pltpu.CompilerParams(vmem_limit_bytes=60 * 1024 * 1024),
-    )(block_out, grad_x, first, gw_z, gw_x, sums)
+    )(*sources)
 
 
 def in_norm_scale(values):
@@ -1674,7 +1688,7 @@
             own_cols, heads, width, block_out, grad_x, gw_first, gw_z, gw_x, sums
         )
         return (
-            block_out, grad_x, g_norm[0], gw_z, gw_x, gw_b.T, gw_c.T, gw_dt.T, g_conv_w.T, g_conv_b[0], g_dt_bias[0],
+            block_out, grad_x, g_norm[0], gw_z, gw_x, gw_b.T, gw_c.T, gw_dt.T, g_conv_w.T, g_conv_b.reshape(-1), g_dt_bias[0],
             g_a_log[0], g_skip[0], g_gate[0], gw_out
         )
     else:

time: 235 us -> 232 us (0.987)
  no operation moved by 1% of the time
where the time goes in v5:
time: 232 us; the launch traced here: 231 us
  Pallas kernels  229 us (99%)
    pallas_call x1, Pallas kernels, first_part(): pl.pallas_call(functools.partial(first_kernel, inner, heads, own_cols), o...  84.5 us
    pallas_call x1, Pallas kernels, fourth_part(): pl.pallas_call(functools.partial(fourth_kernel, heads), out_shape=(jax.Sh...  49.5 us
    pallas_call x1, Pallas kernels, third_part(): pl.pallas_call(functools.partial(third_kernel, own_cols, heads), out_shap...  48.2 us
    pallas_call x1, Pallas kernels, second_part(): pl.pallas_call(functools.partial(second_kernel, inner), out_shape=(jax.Sh...  41.4 us
    pallas_call x1, Pallas kernels, results_part(): pl.pallas_call(functools.partial(results_kernel, own_cols, heads), out_sh...  5.24 us

profile of v5, /device:TPU:0, one launch (start us, length us, event | category | flops | bytes accessed | tf_op | source)
XLA Modules:
  0.0 231.0 jit_solution(11867087071466699507)
XLA Ops:
  0.7 0.8 concatenate.3
  1.5 0.6 broadcast_in_dim.12.flat_ref
  2.1 84.5 %shard_map.271 = (bf16[1024,2048]{1,0:T(8,128)(2,1)}, bf16[1024,2048]{1,0:T(8,128)(2,1)}, bf16[1024,384]{1,0:T(8,128)(2,1)}, bf16[384,2048]{1,0:T(8,128)(2,1)}, ...) custom-call(bf16[256,2048]{1,0:T(8,128)(2,1)} %x_ref.5, ...), custom_call_target="tpu_custom_call" | custom-call | tf_op jit(solution)/shard_map/pallas_call | solution.py:673
  86.6 41.4 %shard_map.272 = (bf16[256,2048]{1,0:T(8,128)(2,1)}, bf16[896,256]{1,0:T(8,128)(2,1)}, bf16[1024,1024]{1,0:T(8,128)(2,1)}, bf16[1024,1024]{1,0:T(8,128)(2,1)}, b...) custom-call(bf16[256,2048]{1,0:T(8,128)(2,1)} %x_ref.5, f32[8,1024]{1,0:T(8,128)} %get-tuple-element.62.cross_ref, ...), custom_call_target="tpu_custom_call" | custom-call | tf_op jit(solution)/shard_map/pallas_call | solution.py:1069
  127.9 48.2 %shard_map.273 = (bf16[1152,256]{1,0:T(8,128)(2,1)}, bf16[1024,1024]{1,0:T(8,128)(2,1)}, bf16[1024,384]{1,0:T(8,128)(2,1)}, bf16[4,1120,256]{2,1,0:T(8,128)(2,1)}, f32[8,1280]{1,0:T(8,128)}) custom-call(bf16[1024,2048]{1,0:T(8,128)(2,1)} %get-tuple-element.69.zx_ref, bf16[1024,384]{1,0:T(8,128)(2,1)} %get-tuple-element.74.bcdt_ref, ...), custom_call_target="tpu_custom_call" | custom-call | tf_op jit(solution)/shard_map/pallas_call | solution.py:1240
  176.1 49.5 %shard_map.274 = (bf16[1120,256]{1,0:T(8,128)(2,1)}, f32[256,2048]{1,0:T(8,128)}, f32[4,8,1792]{2,1,0:T(8,128)}) custom-call(bf16[256,2048]{1,0:T(8,128)(2,1)} %x_ref.5, bf16[256,2048]{1,0:T(8,128)(2,1)} %d_own_ref.3, f32[1,2048]{1,0:T(1,128)} %bitcast.20, f32[8,1280]{1,0:T(8,128)} %get-tuple-element.82.small_ref, f32[8,1024]{1,0:T(8,128)} %get-tuple-element.83.gain_sum_ref, ...), custom_call_target="tpu_custom_call" | custom-call | tf_op jit(solution)/shard_map/pallas_call | solution.py:1427
  225.6 5.2 %shard_map.275 = (bf16[256,2048]{1,0:T(8,128)(2,1)}, f32[256,2048]{1,0:T(8,128)}, f32[256,1024]{1,0:T(8,128)}, f32[256,1024]{1,0:T(8,128)}, f32[32,256]{1,0:T(8,...) custom-call(bf16[256,2048]{1,0:T(8,128)(2,1)} %get-tuple-element.73., ...), custom_call_target="tpu_custom_call" | custom-call | tf_op jit(solution)/shard_map/pallas_call | solution.py:1566
  (1 shorter events, 0.0 us)
